TPU v7x, 768 devices: a whole 4x8x12 slice. The times are simulated.
768 devices in a mesh: ctx: 32 (over y_hi, x, core), tp: 24 (over y_lo, z).
Axes of the slice: x: 4, y: 8 (y_hi: 4, y_lo: 2; y = y_hi * 2 + y_lo), z: 12, core: 2. Of those that a mesh axis runs over, the one named last changes fastest.
Arguments:
- tokens: bfloat16 [18432, 4096], P(('ctx', 'tp')), may hold values from -6 to 6
- proj_weight: bfloat16 [4096, 3, 3072], P(None, None, 'tp'), may hold values from -0.09375 to 0.09375
- feat_taps: float32 [3, 3, 3072], P(None, None, 'tp'), may hold values from -2.5 to 2.5
- inner_taps: float32 [7, 3072], P(None, 'tp'), may hold values from -2.5 to 2.5
- grad_out: bfloat16 [18432, 3072], P('ctx', 'tp'), may hold values from -6 to 6
Outputs:
- gated: bfloat16 [18432, 3072], P('ctx', 'tp')
- grad_tokens: bfloat16 [18432, 4096], P(('ctx', 'tp'))
All inputs are finite; a program needn't handle non-finite values.
Results may differ from a plain program's by a relative error of at most 0.025.
Values may be sent and summed in bfloat16 or wider, within the bound.
No kernel may reach another device: no remote copies, remote signals or barrier semaphores. Data moves between devices by JAX's collectives and lax.ppermute only.
A program may use at most 32 MiB of HBM per device.

v0:
```python
import jax
import jax.numpy as jnp
from jax import lax
from jax.sharding import PartitionSpec as P


def from_behind(value, axis, steps):
    count = lax.axis_size(axis)
    first, last = (max(0, -steps), min(count, count - steps))
    return lax.ppermute(value, axis, [(source, source + steps) for source in range(first, last)])


def causal_taps(series, kernel):
    taps = kernel.shape[0]
    length = series.shape[0] - (taps - 1)
    summed = kernel[0] * series[taps - 1 : taps - 1 + length]
    for offset in range(1, taps):
        summed = summed + kernel[offset] * series[taps - 1 - offset : taps - 1 - offset + length]
    return summed


def anti_taps(series, kernel):
    taps = kernel.shape[0]
    length = series.shape[0] - (taps - 1)
    summed = kernel[0] * series[0:length]
    for offset in range(1, taps):
        summed = summed + kernel[offset] * series[offset : offset + length]
    return summed


def featurize(window, feat_taps, inner_taps):
    query_feat = causal_taps(window[6:, 0], feat_taps[0])
    key_feat = causal_taps(window[:, 1], feat_taps[1])
    value_feat = causal_taps(window[:, 2], feat_taps[2])
    inner_conv = causal_taps(key_feat * value_feat, inner_taps)
    return (query_feat, key_feat, value_feat, inner_conv)


def adjoint_rows(series, feat_taps):
    stacked = jnp.stack(
        [
            anti_taps(series[:, 0], feat_taps[0]),
            anti_taps(series[:, 1], feat_taps[1]),
            anti_taps(series[:, 2], feat_taps[2]),
        ],
        axis=1,
    ).astype(jnp.bfloat16)
    return stacked.reshape(stacked.shape[0], 3 * stacked.shape[2])


def local(tokens, proj_weight, feat_taps, inner_taps, grad_out):
    channels = proj_weight.shape[2]
    flat_weight = proj_weight.reshape(proj_weight.shape[0], 3 * channels)
    projected = jnp.dot(
        lax.all_gather(tokens, "tp", axis=0, tiled=True),
        flat_weight,
        preferred_element_type=jnp.float32,
    ).astype(jnp.bfloat16)
    row_count = projected.shape[0]
    projected = projected.reshape(row_count, 3, channels)
    earlier = from_behind(projected[row_count - 8 :], "ctx", 1)
    window = jnp.concatenate([earlier, projected], axis=0).astype(jnp.float32)
    query_feat, key_feat, value_feat, inner_conv = featurize(window, feat_taps, inner_taps)
    gated = (query_feat * inner_conv).astype(jnp.bfloat16)
    grad_f = grad_out.astype(jnp.float32)
    grad_query = grad_f * inner_conv
    grad_inner = grad_f * query_feat
    leading_mix = anti_taps(grad_inner[:8], inner_taps)
    leading = jnp.stack(
        [grad_query[:2], leading_mix * value_feat[6:8], leading_mix * key_feat[6:8]], axis=1
    )
    received, received_inner = from_behind((leading, grad_inner[:6]), "ctx", -1)
    grad_mix = anti_taps(jnp.concatenate([grad_inner, received_inner], axis=0), inner_taps)
    grad_key = jnp.concatenate([grad_mix * value_feat[6:], received[:, 1]], axis=0)
    grad_value = jnp.concatenate([grad_mix * key_feat[6:], received[:, 2]], axis=0)
    grad_query = jnp.concatenate([grad_query, received[:, 0]], axis=0)
    grad_series = jnp.stack([grad_query, grad_key, grad_value], axis=1)
    grad_proj = adjoint_rows(grad_series, feat_taps)
    grad_tokens = lax.psum_scatter(
        lax.dot_general(
            grad_proj, flat_weight, (((1,), (1,)), ((), ())), preferred_element_type=jnp.float32
        ).astype(jnp.bfloat16),
        "tp",
        scatter_dimension=0,
        tiled=True,
    )
    return (gated, grad_tokens)


def solution(mesh):
    in_specs = (
        P(("ctx", "tp"), None),
        P(None, None, "tp"),
        P(None, None, "tp"),
        P(None, "tp"),
        P("ctx", "tp"),
    )
    out_specs = (P("ctx", "tp"), P(("ctx", "tp"), None))
    return jax.shard_map(local, mesh=mesh, in_specs=in_specs, out_specs=out_specs, check_vma=False)
```

profile of v0, /device:TPU:2, one launch (start us, length us, event | category | flops | bytes accessed | tf_op | source)
XLA Modules:
  0.0 276.9 jit_solution(7563267710511175016)
XLA Ops:
  7.2 0.0 all-gather.2.cloned.1.call-start
  7.2 0.7 all-gather.2.cloned.1.call-update
  7.9 0.0 reduce-scatter.2.cloned.1.call-start
  8.0 3.2 %copy.8 = bf16[4096,3,128]{0,2,1:T(8,128)(2,1)S(1)} copy(bf16[4096,3,128]{2,0,1:T(8,128)(2,1)} %param.6) | data formatting | bytes 6291456 | tf_op args[1]
  11.2 120.4 %all-gather.2.cloned.1.call-done = bf16[576,4096]{1,0:T(8,128)(2,1)} async-done(((bf16[24,4096]{1,0:T(8,128)(2,1)}), bf16[576,4096]{1,0:T(8,128)(2,1)}) %all-gather.2.cloned.1.call-update) | async-done | bytes 4718608 | tf_op jit(solution)/shard_map/all_gather | solution.py:55
  131.5 5.0 %convolution_convert_fusion = bf16[576,384]{1,0:T(8,128)(2,1)S(1)} fusion(bf16[576,4096]{1,0:T(8,128)(2,1)} %all-gather.2.cloned.1.call-done, bf16[4096,384]{0,1:T(8,128)(2,1)S(1)} %bitcast.128), kind=kOutput, calls=%fused_computation.1 | convolution fusion | flops 1812160512 | bytes 8306688 | tf_op jit(solution)/shard_map/dot_general | solution.py:54
  136.5 2.1 collective-permute-start
  138.6 1.3 copy.9
  139.9 0.3 copy.10
  140.2 1.5 collective-permute-done
  141.6 0.1 maximum_convert_fusion
  141.7 0.1 convert_multiply_fusion
  141.8 0.2 fusion.77
  142.0 0.3 convert_multiply_fusion.1
  142.3 2.3 collective-permute-start.2
  144.7 1.9 collective-permute-start.1
  146.6 0.3 slice_multiply_fusion.1
  147.0 1.0 collective-permute-done.1
  147.9 0.1 fusion.63
  148.0 0.2 fusion.61
  148.3 4.4 %bitcast_convert_fusion = bf16[576,4096]{1,0:T(8,128)(2,1)} fusion(bf16[4096,3,128]{2,0,1:T(8,128)(2,1)S(1)} %copy-done, bf16[576,1,128]{2,0,1:T(8,128)(2,1)S(1)} %fusion.63, bf16[576,1,128]{2,0,1:T(8,128)(2,1)S(1)} %get-tuple-element.33, bf16[576,1,128]{2,0,1:T(8,128)(2,1)S(1)} %get-tuple-element.32), kind=kOutput, calls=%fused_computation | convolution fusion | flops 1814740992 | bytes 8306688 | tf_op jit(solution)/shard_map/dot_general | solution.py:80
  152.6 0.0 reduce-scatter.2.cloned.1.call-update
  152.7 0.7 multiply_convert_fusion
  153.3 116.7 %reduce-scatter.2.cloned.1.call-done = bf16[24,4096]{1,0:T(8,128)(2,1)} async-done(((bf16[576,4096]{1,0:T(8,128)(2,1)}), bf16[24,4096]{1,0:T(8,128)(2,1)}) %reduce-scatter.2.cloned.1.call-update) | async-done | bytes 196624 | tf_op jit(solution)/shard_map/reduce_scatter | solution.py:79
  (21 shorter events, 0.1 us)
Async XLA Ops:
  7.2 124.4 %all-gather.2.cloned.1.call-start = ((), (), s32[]{:S(2)}) async-start(), calls=%async_computation.1 | async-start | bytes 4915200 | tf_op jit(solution)/shard_map/all_gather | solution.py:55
  7.9 3.3 %copy-start.4 = (f32[7,128]{1,0:T(8,128)S(1)}, f32[7,128]{1,0:T(8,128)}, u32[]{:S(2)}) copy-start(f32[7,128]{1,0:T(8,128)} %param.8) | copy-start | bytes 10756
  7.9 262.2 %reduce-scatter.2.cloned.1.call-start = ((), (), s32[]{:S(2)}) async-start(), calls=%async_computation.2 | async-start | bytes 4915200 | tf_op jit(solution)/shard_map/reduce_scatter | solution.py:79
  131.5 7.1 %copy-start.3 = (f32[3,3,128]{2,1,0:T(4,128)S(1)}, f32[3,3,128]{2,1,0:T(4,128)}, u32[]{:S(2)}) copy-start(f32[3,3,128]{2,1,0:T(4,128)} %param.7) | copy-start | bytes 13828
  136.5 2.1 copy-start.2
  136.5 5.2 %copy-start.1 = (bf16[576,128]{1,0:T(8,128)(2,1)S(1)}, bf16[576,128]{1,0:T(8,128)(2,1)}, u32[]{:S(2)}) copy-start(bf16[576,128]{1,0:T(8,128)(2,1)} %param.9) | copy-start | bytes 442372
  136.5 5.1 %collective-permute-start = (bf16[8,3,128]{2,0,1:T(8,128)(2,1)S(1)}, bf16[8,3,128]{2,0,1:T(8,128)(2,1)S(1)}, u32[]{:S(2)}, u32[]{:S(2)}) collective-permute-start(bf16[8,3,128]{2,0,1:T(8,128)(2,1)S(1)} %slice_bitcast_fusion.9), channel_id=1, source_target_pairs={{0,24},{24,48},{48,72},{72,96},{96,120},{120,144},{144,168},{168,1... | collective-permute-start | bytes 18440 | tf_op jit(solution)/shard_map/ppermute | solution.py:10
  142.0 6.2 %copy-start = (bf16[4096,3,128]{2,0,1:T(8,128)(2,1)S(1)}, bf16[4096,3,128]{2,0,1:T(8,128)(2,1)}, u32[]{:S(2)}) copy-start(bf16[4096,3,128]{2,0,1:T(8,128)(2,1)} %param.6) | copy-start | bytes 9437188
  142.3 4.3 %collective-permute-start.2 = (f32[6,128]{1,0:T(8,128)S(1)}, f32[6,128]{1,0:T(8,128)S(1)}, u32[]{:S(2)}, u32[]{:S(2)}) collective-permute-start(f32[6,128]{1,0:T(8,128)S(1)} %slice.381), channel_id=1, source_target_pairs={{24,0},{48,24},{72,48},{96,72},{120,96},{144,120},{168,144},{192,1... | collective-permute-start | bytes 9224 | tf_op jit(solution)/shard_map/ppermute | solution.py:10
  144.7 3.2 %collective-permute-start.1 = (f32[2,3,128]{2,0,1:T(2,128)S(1)}, f32[2,3,128]{2,0,1:T(2,128)S(1)}, u32[]{:S(2)}, u32[]{:S(2)}) collective-permute-start(f32[2,3,128]{2,0,1:T(2,128)S(1)} %pad_maximum_fusion.4), channel_id=1, source_target_pairs={{24,0},{48,24},{72,48},{96,72},{120,96},{144,120},{168,144},{192,1... | collective-permute-start | bytes 9224 | tf_op jit(solution)/shard_map/ppermute | solution.py:10
Sparse Core Ops, SparseCore 0:
  10.4 121.1 all-gather.1
  152.8 117.2 reduce-scatter.1
where the time goes:
time: 277 us
  waiting for transfers between devices  240 us (87%)
  between operations  14.2 us (5%)
  matrix products  9.34 us (3%)
  starting transfers between devices  6.38 us (2%)
  local copies, waits for them, and re-layouts  4.77 us (2%)
    all_gather x1, waiting for transfers between devices, local(): lax.all_gather(tokens, 'tp', axis=0, tiled=True)  120 us
    reduce_scatter x1, waiting for transfers between devices, local(): lax.psum_scatter(lax.dot_general(grad_proj, flat_weight, (((1,), (1,)), (...  117 us
    ppermute x3, starting transfers between devices, from_behind(): lax.ppermute(value, axis, [(source, source + steps) for source in range(f...  6.3 us
  transfers between devices with their start and end apart: 5, of which 4 were waited for; matrix products, arithmetic and copies ran while one was open for 2% of the time, Pallas kernels for 0%

commit v1 on v0

--- a/solution.py
+++ b/solution.py
@@ -1,7 +1,11 @@
 import jax
 import jax.numpy as jnp
 from jax import lax
+from jax.sharding import Mesh
 from jax.sharding import PartitionSpec as P
+
+CTX = ("yh", "x", "c")
+TP = ("yl", "z")
 
 
 def from_behind(value, axis, steps):
@@ -50,15 +54,29 @@
 
 def local(tokens, proj_weight, feat_taps, inner_taps, grad_out):
     channels = proj_weight.shape[2]
-    flat_weight = proj_weight.reshape(proj_weight.shape[0], 3 * channels)
+    width = proj_weight.shape[0]
+    flat_weight = proj_weight.reshape(width, 3 * channels)
+    shard = tokens.shape[0]
+    depth = lax.axis_size("z")
+    upper = lax.axis_index("yl")
+    other = lax.ppermute(tokens, "yl", [(0, 1), (1, 0)])
+    pair = jnp.where(
+        upper == 0,
+        jnp.concatenate([tokens, other], axis=0),
+        jnp.concatenate([other, tokens], axis=0),
+    )
     projected = jnp.dot(
-        lax.all_gather(tokens, "tp", axis=0, tiled=True),
+        lax.all_gather(pair, "z", axis=0, tiled=True),
         flat_weight,
         preferred_element_type=jnp.float32,
     ).astype(jnp.bfloat16)
     row_count = projected.shape[0]
-    projected = projected.reshape(row_count, 3, channels)
-    earlier = from_behind(projected[row_count - 8 :], "ctx", 1)
+    projected = (
+        projected.reshape(depth, 2, shard, 3 * channels)
+        .transpose(1, 0, 2, 3)
+        .reshape(row_count, 3, channels)
+    )
+    earlier = from_behind(projected[row_count - 8 :], CTX, 1)
     window = jnp.concatenate([earlier, projected], axis=0).astype(jnp.float32)
     query_feat, key_feat, value_feat, inner_conv = featurize(window, feat_taps, inner_taps)
     gated = (query_feat * inner_conv).astype(jnp.bfloat16)
@@ -69,31 +87,41 @@
     leading = jnp.stack(
         [grad_query[:2], leading_mix * value_feat[6:8], leading_mix * key_feat[6:8]], axis=1
     )
-    received, received_inner = from_behind((leading, grad_inner[:6]), "ctx", -1)
+    received, received_inner = from_behind((leading, grad_inner[:6]), CTX, -1)
     grad_mix = anti_taps(jnp.concatenate([grad_inner, received_inner], axis=0), inner_taps)
     grad_key = jnp.concatenate([grad_mix * value_feat[6:], received[:, 1]], axis=0)
     grad_value = jnp.concatenate([grad_mix * key_feat[6:], received[:, 2]], axis=0)
     grad_query = jnp.concatenate([grad_query, received[:, 0]], axis=0)
     grad_series = jnp.stack([grad_query, grad_key, grad_value], axis=1)
     grad_proj = adjoint_rows(grad_series, feat_taps)
-    grad_tokens = lax.psum_scatter(
+    grad_proj = (
+        grad_proj.reshape(2, depth, shard, 3 * channels)
+        .transpose(1, 0, 2, 3)
+        .reshape(row_count, 3 * channels)
+    )
+    summed = lax.psum_scatter(
         lax.dot_general(
             grad_proj, flat_weight, (((1,), (1,)), ((), ())), preferred_element_type=jnp.float32
         ).astype(jnp.bfloat16),
-        "tp",
+        "z",
         scatter_dimension=0,
         tiled=True,
     )
+    low, high = summed[:shard], summed[shard:]
+    mine = jnp.where(upper == 0, low, high)
+    theirs = lax.ppermute(jnp.where(upper == 0, high, low), "yl", [(0, 1), (1, 0)])
+    grad_tokens = (mine.astype(jnp.float32) + theirs.astype(jnp.float32)).astype(jnp.bfloat16)
     return (gated, grad_tokens)
 
 
 def solution(mesh):
+    grid = Mesh(mesh.devices.reshape(4, 4, 2, 2, 12), CTX + TP)
     in_specs = (
-        P(("ctx", "tp"), None),
-        P(None, None, "tp"),
-        P(None, None, "tp"),
-        P(None, "tp"),
-        P("ctx", "tp"),
+        P(CTX + TP, None),
+        P(None, None, TP),
+        P(None, None, TP),
+        P(None, TP),
+        P(CTX, TP),
     )
-    out_specs = (P("ctx", "tp"), P(("ctx", "tp"), None))
-    return jax.shard_map(local, mesh=mesh, in_specs=in_specs, out_specs=out_specs, check_vma=False)
+    out_specs = (P(CTX, TP), P(CTX + TP, None))
+    return jax.shard_map(local, mesh=grid, in_specs=in_specs, out_specs=out_specs, check_vma=False)

time: 277 us -> 215 us (0.78)
  waiting for transfers between devices: 240 us -> 159 us
  local copies, waits for them, and re-layouts: 4.77 us -> 11.7 us
  starting transfers between devices: 6.38 us -> 12.7 us
  other arithmetic: 1.98 us -> 7.45 us
    all_gather x1, waiting for transfers between devices: 120 us -> 73.1 us  [local(): lax.all_gather(pair, 'z', axis=0, tiled=True)]
    reduce_scatter x1, waiting for transfers between devices: 117 us -> 73.7 us  [local(): lax.psum_scatter(lax.dot_general(grad_proj, flat_weight, (((1,), (1,)), (...]
    ppermute x0 -> x2, waiting for transfers between devices: none -> 8.73 us  [the longest x1 5.25 us: local(): other = lax.ppermute(tokens, 'yl', [(0, 1), (1, 0)])]
    ppermute x0 -> x2, starting transfers between devices: none -> 6.85 us  [the longest x1 3.48 us: local(): other = lax.ppermute(tokens, 'yl', [(0, 1), (1, 0)])]
    reshape x1 -> x3, local copies, waits for them, and re-layouts: 0.26 us -> 4.07 us  [the longest x2 3.27 us: local(): projected = projected.reshape(depth, 2, shard, 3 * channels).transpose(1,...]
    select_n x0 -> x2, other arithmetic: none -> 2.9 us  [the longest x1 1.85 us: local(): jnp.where(upper == 0, jnp.concatenate([tokens, other], axis=0), jnp.conca...]
  transfers between devices with their start and end apart: 5 -> 7, of which waited for: 4 -> 6; matrix products, arithmetic and copies ran while one was open for 2% -> 2% of each run, Pallas kernels for 0% -> 0%
where the time goes in v1:
time: 215 us
  waiting for transfers between devices  159 us (74%)
  between operations  14.3 us (7%)
  starting transfers between devices  12.7 us (6%)
  local copies, waits for them, and re-layouts  11.7 us (5%)
  matrix products  9.26 us (4%)
  other arithmetic  7.45 us (3%)
    reduce_scatter x1, waiting for transfers between devices, local(): lax.psum_scatter(lax.dot_general(grad_proj, flat_weight, (((1,), (1,)), (...  73.7 us
    all_gather x1, waiting for transfers between devices, local(): lax.all_gather(pair, 'z', axis=0, tiled=True)  73.1 us
    ppermute x3, starting transfers between devices, from_behind(): lax.ppermute(value, axis, [(source, source + steps) for source in range(f...  5.75 us
    ppermute x1, waiting for transfers between devices, local(): other = lax.ppermute(tokens, 'yl', [(0, 1), (1, 0)])  5.25 us
    dot_general x1, matrix products, local(): jnp.dot(lax.all_gather(pair, 'z', axis=0, tiled=True), flat_weight, prefe...  4.96 us
  transfers between devices with their start and end apart: 7, of which 6 were waited for; matrix products, arithmetic and copies ran while one was open for 2% of the time, Pallas kernels for 0%

profile of v1, /device:TPU:2, one launch (start us, length us, event | category | flops | bytes accessed | tf_op | source)
XLA Modules:
  0.0 214.8 jit_solution(3282579368917402086)
XLA Ops:
  7.2 3.5 %collective-permute-start = (bf16[24,4096]{1,0:T(8,128)(2,1)}, bf16[24,4096]{1,0:T(8,128)(2,1)S(1)}, u32[]{:S(2)}, u32[]{:S(2)}) collective-permute-start(bf16[24,4096]{1,0:T(8,128)(2,1)} %param.5), channel_id=1, source_target_pairs={{0,12},{12,0},{1,13},{13,1},{2,14},{14,2},{3,15},{15,3},{4,16},{16... | collective-permute-start | bytes 589832 | tf_op jit(solution)/shard_map/ppermute | solution.py:62
  10.7 5.2 %collective-permute-done = bf16[24,4096]{1,0:T(8,128)(2,1)S(1)} collective-permute-done((bf16[24,4096]{1,0:T(8,128)(2,1)}, bf16[24,4096]{1,0:T(8,128)(2,1)S(1)}, u32[]{:S(2)}, u32[]{:S(2)}) %collective-permute-start) | collective-permute-done | bytes 196640 | tf_op jit(solution)/shard_map/ppermute | solution.py:62
  16.0 1.9 maximum_select_fusion
  17.9 3.2 %copy.19 = bf16[4096,3,128]{0,2,1:T(8,128)(2,1)S(1)} copy(bf16[4096,3,128]{2,0,1:T(8,128)(2,1)} %param.6) | data formatting | bytes 6291456 | tf_op args[1]
  21.1 73.1 %all-gather.2.cloned.1.call-done = bf16[576,4096]{1,0:T(8,128)(2,1)} async-done(((bf16[48,4096]{1,0:T(8,128)(2,1)}), bf16[576,4096]{1,0:T(8,128)(2,1)}) %all-gather.2.cloned.1.call-update) | async-done | bytes 4718608 | tf_op jit(solution)/shard_map/all_gather | solution.py:69
  94.3 5.0 %convolution_convert_fusion.1 = bf16[576,384]{1,0:T(8,128)(2,1)S(1)} fusion(bf16[576,4096]{1,0:T(8,128)(2,1)} %all-gather.2.cloned.1.call-done, bf16[4096,384]{0,1:T(8,128)(2,1)S(1)} %bitcast.132), kind=kOutput, calls=%fused_computation.1 | convolution fusion | flops 1812160512 | bytes 8306688 | tf_op jit(solution)/shard_map/dot_general | solution.py:68
  99.3 0.8 copy.26
  100.1 2.1 reshape.47
  102.2 1.2 copy.21
  103.3 1.9 collective-permute-start.1
  105.3 3.0 %collective-permute-done.1 = bf16[8,3,128]{2,0,1:T(8,128)(2,1)S(1)} collective-permute-done((bf16[8,3,128]{2,0,1:T(8,128)(2,1)S(1)}, bf16[8,3,128]{2,0,1:T(8,128)(2,1)S(1)}, u32[]{:S(2)}, u32[]{:S(2)}) %collective-permute-start.1) | collective-permute-done | bytes 6176 | tf_op jit(solution)/shard_map/ppermute | solution.py:14
  108.4 0.8 convert_multiply_fusion
  109.2 1.9 collective-permute-start.3
  111.7 1.9 collective-permute-start.2
  114.0 0.9 collective-permute-done.2
  115.3 1.2 copy.23
  116.5 2.1 convert_element_type.33
  118.6 1.1 copy.24
  119.6 4.3 %convolution_convert_fusion = bf16[576,4096]{1,0:T(8,128)(2,1)} fusion(bf16[576,384]{1,0:T(8,128)(2,1)S(1)} %bitcast.136, bf16[4096,384]{0,1:T(8,128)(2,1)S(1)} %bitcast.133), kind=kOutput, calls=%fused_computation | convolution fusion | flops 1814298624 | bytes 8306688 | tf_op jit(solution)/shard_map/dot_general | solution.py:103
  123.9 73.7 %reduce-scatter.2.cloned.1.call-done = bf16[48,4096]{1,0:T(8,128)(2,1)} async-done(((bf16[576,4096]{1,0:T(8,128)(2,1)}), bf16[48,4096]{1,0:T(8,128)(2,1)}) %reduce-scatter.2.cloned.1.call-update) | async-done | bytes 393232 | tf_op jit(solution)/shard_map/reduce_scatter | solution.py:102
  197.6 1.0 broadcast_select_fusion
  198.6 3.4 %collective-permute-start.4 = (bf16[24,4096]{1,0:T(8,128)(2,1)S(1)}, bf16[24,4096]{1,0:T(8,128)(2,1)S(1)}, u32[]{:S(2)}, u32[]{:S(2)}) collective-permute-start(bf16[24,4096]{1,0:T(8,128)(2,1)S(1)} %broadcast_select_fusion), channel_id=1, source_target_pairs={{0,12},{12,0},{1,13},{13,1},{2,14},{14,2},{3,15},{15,3},{4,16},{16... | collective-permute-start | bytes 589832 | tf_op jit(solution)/shard_map/ppermute | solution.py:112
  202.7 3.5 %collective-permute-done.4 = bf16[24,4096]{1,0:T(8,128)(2,1)S(1)} collective-permute-done((bf16[24,4096]{1,0:T(8,128)(2,1)S(1)}, bf16[24,4096]{1,0:T(8,128)(2,1)S(1)}, u32[]{:S(2)}, u32[]{:S(2)}) %collective-permute-start.4) | collective-permute-done | bytes 196640 | tf_op jit(solution)/shard_map/ppermute | solution.py:112
  206.2 1.8 add_convert_fusion
  (33 shorter events, 2.1 us)
Async XLA Ops:
  7.2 87.1 %all-gather.2.cloned.1.call-start = ((), (), s32[]{:S(2)}) async-start(), calls=%async_computation.1 | async-start | bytes 5111808 | tf_op jit(solution)/shard_map/all_gather | solution.py:69
  7.2 8.7 %collective-permute-start = (bf16[24,4096]{1,0:T(8,128)(2,1)}, bf16[24,4096]{1,0:T(8,128)(2,1)S(1)}, u32[]{:S(2)}, u32[]{:S(2)}) collective-permute-start(bf16[24,4096]{1,0:T(8,128)(2,1)} %param.5), channel_id=1, source_target_pairs={{0,12},{12,0},{1,13},{13,1},{2,14},{14,2},{3,15},{15,3},{4,16},{16... | collective-permute-start | bytes 589832 | tf_op jit(solution)/shard_map/ppermute | solution.py:62
  17.8 3.3 %copy-start.4 = (f32[7,128]{1,0:T(8,128)S(1)}, f32[7,128]{1,0:T(8,128)}, u32[]{:S(2)}) copy-start(f32[7,128]{1,0:T(8,128)} %param.8) | copy-start | bytes 10756
  17.8 179.7 %reduce-scatter.2.cloned.1.call-start = ((), (), s32[]{:S(2)}) async-start(), calls=%async_computation.2 | async-start | bytes 5111808 | tf_op jit(solution)/shard_map/reduce_scatter | solution.py:102
  94.3 11.0 %copy-start.3 = (f32[3,3,128]{2,1,0:T(4,128)S(1)}, f32[3,3,128]{2,1,0:T(4,128)}, u32[]{:S(2)}) copy-start(f32[3,3,128]{2,1,0:T(4,128)} %param.7) | copy-start | bytes 13828
  99.2 9.1 %copy-start.1 = (bf16[576,128]{1,0:T(8,128)(2,1)S(1)}, bf16[576,128]{1,0:T(8,128)(2,1)}, u32[]{:S(2)}) copy-start(bf16[576,128]{1,0:T(8,128)(2,1)} %param.9) | copy-start | bytes 442372
  102.2 9.2 %copy-start.2 = (bf16[576,128]{1,0:T(8,128)(2,1)S(1)}, bf16[576,128]{1,0:T(8,128)(2,1)}, u32[]{:S(2)}) copy-start(bf16[576,128]{1,0:T(8,128)(2,1)} %param.9) | copy-start | bytes 442372
  103.3 4.9 %collective-permute-start.1 = (bf16[8,3,128]{2,0,1:T(8,128)(2,1)S(1)}, bf16[8,3,128]{2,0,1:T(8,128)(2,1)S(1)}, u32[]{:S(2)}, u32[]{:S(2)}) collective-permute-start(bf16[8,3,128]{2,0,1:T(8,128)(2,1)S(1)} %slice.355), channel_id=1, source_target_pairs={{0,24},{24,48},{48,72},{72,96},{96,120},{120,144},{144,168},{168,1... | collective-permute-start | bytes 18440 | tf_op jit(solution)/shard_map/ppermute | solution.py:14
  109.2 4.4 %collective-permute-start.3 = (f32[6,128]{1,0:T(8,128)S(1)}, f32[6,128]{1,0:T(8,128)S(1)}, u32[]{:S(2)}, u32[]{:S(2)}) collective-permute-start(f32[6,128]{1,0:T(8,128)S(1)} %slice.385), channel_id=1, source_target_pairs={{24,0},{48,24},{72,48},{96,72},{120,96},{144,120},{168,144},{192,1... | collective-permute-start | bytes 9224 | tf_op jit(solution)/shard_map/ppermute | solution.py:14
  111.7 3.2 %collective-permute-start.2 = (f32[2,3,128]{2,0,1:T(2,128)S(1)}, f32[2,3,128]{2,0,1:T(2,128)S(1)}, u32[]{:S(2)}, u32[]{:S(2)}) collective-permute-start(f32[2,3,128]{2,0,1:T(2,128)S(1)} %pad_maximum_fusion.5), channel_id=1, source_target_pairs={{24,0},{48,24},{72,48},{96,72},{120,96},{144,120},{168,144},{192,1... | collective-permute-start | bytes 9224 | tf_op jit(solution)/shard_map/ppermute | solution.py:14
  123.9 78.1 %copy-start = (f32[576,128]{1,0:T(8,128)S(1)}, f32[576,128]{1,0:T(8,128)}, u32[]{:S(2)}) copy-start(f32[576,128]{1,0:T(8,128)} %get-tuple-element.9) | copy-start | bytes 884740
  198.6 7.6 %collective-permute-start.4 = (bf16[24,4096]{1,0:T(8,128)(2,1)S(1)}, bf16[24,4096]{1,0:T(8,128)(2,1)S(1)}, u32[]{:S(2)}, u32[]{:S(2)}) collective-permute-start(bf16[24,4096]{1,0:T(8,128)(2,1)S(1)} %broadcast_select_fusion), channel_id=1, source_target_pairs={{0,12},{12,0},{1,13},{13,1},{2,14},{14,2},{3,15},{15,3},{4,16},{16... | collective-permute-start | bytes 589832 | tf_op jit(solution)/shard_map/ppermute | solution.py:112
Sparse Core Ops, SparseCore 0:
  18.0 76.2 all-gather.1
  124.1 73.4 reduce-scatter.1

commit v2 on v0

v2 whole, which is shorter than its diff:
```python
import jax
import jax.numpy as jnp
from jax import lax
from jax.experimental import pallas as pl
from jax.experimental.pallas import tpu as pltpu
from jax.sharding import Mesh
from jax.sharding import PartitionSpec as P

CTX = ("yh", "x", "c")
TP = ("yl", "z")
HALO = 8


def exchange(value, axes, sizes, route):
    total = 1
    for size in sizes:
        total *= size
    pairs = []
    for source in range(total):
        coords, rest = [], source
        for size in reversed(sizes):
            coords.append(rest % size)
            rest //= size
        target = route(*reversed(coords))
        if target is None:
            continue
        flat = 0
        for place, size in zip(target, sizes):
            flat = flat * size + place
        pairs.append((source, flat))
    return lax.ppermute(value, axes, pairs)


def swap_homes(value):
    return exchange(value, ("c", "yl"), (2, 2), lambda c, yl: (yl, c))


def project_kernel(x_ref, w_ref, o_ref):
    o_ref[0] = jnp.dot(x_ref[...], w_ref[0], preferred_element_type=jnp.float32).astype(o_ref.dtype)


def project(rows, weight):
    count, depth = rows.shape
    parts, _, channels = weight.shape
    return pl.pallas_call(
        project_kernel,
        grid=(parts,),
        in_specs=[
            pl.BlockSpec((count, depth), lambda j: (0, 0)),
            pl.BlockSpec((1, depth, channels), lambda j: (j, 0, 0)),
        ],
        out_specs=pl.BlockSpec((1, count, channels), lambda j: (j, 0, 0)),
        out_shape=jax.ShapeDtypeStruct((parts, count, channels), jnp.bfloat16),
        compiler_params=pltpu.CompilerParams(vmem_limit_bytes=40 * 1024 * 1024),
        name="project",
    )(rows, weight)


def spread_kernel(g_ref, w_ref, o_ref):
    contract = (((1,), (1,)), ((), ()))
    total = lax.dot_general(g_ref[0], w_ref[0], contract, preferred_element_type=jnp.float32)
    for part in range(1, g_ref.shape[0]):
        total = total + lax.dot_general(
            g_ref[part], w_ref[part], contract, preferred_element_type=jnp.float32
        )
    o_ref[...] = total.astype(o_ref.dtype)


def spread(grads, weight):
    parts, count, channels = grads.shape
    depth = weight.shape[1]
    block = min(depth, 1024)
    return pl.pallas_call(
        spread_kernel,
        grid=(depth // block,),
        in_specs=[
            pl.BlockSpec((parts, count, channels), lambda i: (0, 0, 0)),
            pl.BlockSpec((parts, block, channels), lambda i: (0, i, 0)),
        ],
        out_specs=pl.BlockSpec((count, block), lambda i: (0, i)),
        out_shape=jax.ShapeDtypeStruct((count, depth), jnp.bfloat16),
        compiler_params=pltpu.CompilerParams(vmem_limit_bytes=40 * 1024 * 1024),
        name="spread",
    )(grads, weight)


def causal(series, taps):
    total = taps[0:1] * series
    for offset in range(1, taps.shape[0]):
        total = total + taps[offset : offset + 1] * pltpu.roll(series, offset, 0)
    return total


def adjoint(series, taps):
    total = taps[0:1] * series
    for offset in range(1, taps.shape[0]):
        total = total + taps[offset : offset + 1] * pltpu.roll(series, series.shape[0] - offset, 0)
    return total


def mix_kernel(proj_ref, prev_ref, next_ref, feat_ref, inner_ref, grad_ref, grad_next_ref, gated_ref, dproj_ref):
    count = proj_ref.shape[1]
    last = HALO + count

    def window(part):
        return jnp.concatenate([prev_ref[part], proj_ref[part], next_ref[part]], axis=0).astype(jnp.float32)

    inner_taps = inner_ref[...]
    query = causal(window(0), feat_ref[0])
    key = causal(window(1), feat_ref[1])
    value = causal(window(2), feat_ref[2])
    inner = causal(key * value, inner_taps)
    gated_ref[...] = (query * inner)[HALO:last].astype(gated_ref.dtype)
    grad_next = grad_next_ref[...]
    grad = jnp.concatenate([jnp.zeros_like(grad_next), grad_ref[...], grad_next], axis=0).astype(jnp.float32)
    mixed = adjoint(grad * query, inner_taps)
    dproj_ref[0] = adjoint(grad * inner, feat_ref[0])[HALO:last].astype(dproj_ref.dtype)
    dproj_ref[1] = adjoint(mixed * value, feat_ref[1])[HALO:last].astype(dproj_ref.dtype)
    dproj_ref[2] = adjoint(mixed * key, feat_ref[2])[HALO:last].astype(dproj_ref.dtype)


def mix(proj, prev, following, feat, inner, grad, grad_next):
    parts, count, channels = proj.shape
    lanes = min(channels, 128)

    def whole(shape):
        lead = len(shape) - 1
        return pl.BlockSpec(shape[:-1] + (lanes,), lambda i: (0,) * lead + (i,))

    operands = (proj, prev, following, feat, inner, grad, grad_next)
    return pl.pallas_call(
        mix_kernel,
        grid=(channels // lanes,),
        in_specs=[whole(operand.shape) for operand in operands],
        out_specs=[whole((count, channels)), whole(proj.shape)],
        out_shape=[
            jax.ShapeDtypeStruct((count, channels), jnp.bfloat16),
            jax.ShapeDtypeStruct(proj.shape, jnp.bfloat16),
        ],
        compiler_params=pltpu.CompilerParams(vmem_limit_bytes=40 * 1024 * 1024),
        name="mix",
    )(*operands)


def build(sizes):
    ring = sizes[0] * 2

    strips = sizes[0] * sizes[1] * 4

    def along(value, step):
        def route(yh, x, c, yl):
            strip = ((yh * sizes[1] + x) * 2 + yl) * 2 + c + step
            if not 0 <= strip < strips:
                return None
            return (strip // 4 // sizes[1], strip // 4 % sizes[1], strip % 2, strip // 2 % 2)

        return exchange(value, ("yh", "x", "c", "yl"), (sizes[0], sizes[1], 2, 2), route)

    def local(tokens, proj_weight, feat_taps, inner_taps, grad_out):
        upper = lax.axis_index("yl")
        core = lax.axis_index("c")
        depth = proj_weight.shape[0]

        gathered = lax.all_gather(swap_homes(tokens), "z", axis=0, tiled=True)

        planes = proj_weight.transpose(1, 0, 2)
        half = depth // 2
        sent = lax.dynamic_slice_in_dim(planes, core * half, half, 1)

        def beside(yh, c, yl):
            place = (yh * 2 + yl + (1 if c else ring - 1)) % ring
            return (place // 2, c, place % 2)

        came = exchange(sent, ("yh", "c", "yl"), (sizes[0], 2, 2), beside)
        rest = lax.ppermute(came, "c", [(0, 1), (1, 0)])
        other_planes = jnp.where(
            core == 0,
            jnp.concatenate([came, rest], axis=1),
            jnp.concatenate([rest, came], axis=1),
        )

        def both(mine, theirs, axis):
            return jnp.where(
                upper == 0,
                jnp.concatenate([mine, theirs], axis=axis),
                jnp.concatenate([theirs, mine], axis=axis),
            )

        def other(value):
            return lax.ppermute(value, "yl", [(0, 1), (1, 0)])

        weight = both(planes, other_planes, 2)
        feat = both(feat_taps, other(feat_taps), 2)
        inner = both(inner_taps, other(inner_taps), 1)

        count = grad_out.shape[0] // 2
        near = lax.dynamic_slice_in_dim(grad_out, upper * count, count, 0)
        far = lax.dynamic_slice_in_dim(grad_out, (1 - upper) * count, count, 0)
        near = swap_homes(near)
        far = exchange(far, ("c", "yl"), (2, 2), lambda c, yl: (1 - yl, c))
        grad = jnp.where(
            core == 0,
            jnp.concatenate([near, far], axis=1),
            jnp.concatenate([far, near], axis=1),
        )
        grad_next = along(grad[:HALO], -1)

        proj = project(gathered, weight)
        prev = along(proj[:, count - HALO :], 1)
        following = along(proj[:, :HALO], -1)
        gated, dproj = mix(proj, prev, following, feat, inner, grad, grad_next)

        grad_tokens = lax.psum_scatter(spread(dproj, weight), "z", scatter_dimension=0, tiled=True)

        channels = inner_taps.shape[1]
        first, second = gated[:, :channels], gated[:, channels:]
        near = swap_homes(jnp.where(core == 0, first, second))
        far = exchange(
            jnp.where(core == 0, second, first), ("c", "yl"), (2, 2), lambda c, yl: (yl, 1 - c)
        )
        gated = jnp.where(
            upper == 0,
            jnp.concatenate([near, far], axis=0),
            jnp.concatenate([far, near], axis=0),
        )
        return (gated, swap_homes(grad_tokens))

    return local


def solution(mesh):
    sizes = (4, 4, 2, 2, 12)
    grid = Mesh(mesh.devices.reshape(sizes), CTX + TP)
    in_specs = (
        P(CTX + TP, None),
        P(None, None, TP),
        P(None, None, TP),
        P(None, TP),
        P(CTX, TP),
    )
    out_specs = (P(CTX, TP), P(CTX + TP, None))
    return jax.shard_map(build(sizes), mesh=grid, in_specs=in_specs, out_specs=out_specs, check_vma=False)
```

time: 277 us -> 187 us (0.68)
  the two profiles are of different devices: /device:TPU:2 before, /device:TPU:1 now
where the time goes in v2:
time: 187 us
  waiting for transfers between devices  95 us (51%)
  starting transfers between devices  51.7 us (28%)
  between operations  14.4 us (8%)
  other arithmetic  10.2 us (5%)
  Pallas kernels  7.97 us (4%)
  local copies, waits for them, and re-layouts  7.4 us (4%)
    reduce_scatter x1, waiting for transfers between devices, local(): lax.psum_scatter(spread(dproj, weight), 'z', scatter_dimension=0, tiled=T...  54.2 us
    ppermute x10, starting transfers between devices, exchange(): return lax.ppermute(value, axes, pairs)  41.8 us
    ppermute x10, waiting for transfers between devices, exchange(): return lax.ppermute(value, axes, pairs)  30.2 us
    all_gather x1, waiting for transfers between devices, local(): gathered = lax.all_gather(swap_homes(tokens), 'z', axis=0, tiled=True)  10.5 us
    unnamed x17, local copies, waits for them, and re-layouts  5.83 us
    ppermute x1, starting transfers between devices, local(): rest = lax.ppermute(came, 'c', [(0, 1), (1, 0)])  5.79 us
    select_n x3, other arithmetic, both(): jnp.where(upper == 0, jnp.concatenate([mine, theirs], axis=axis), jnp.con...  4.57 us
    ppermute x2, starting transfers between devices, other(): return lax.ppermute(value, 'yl', [(0, 1), (1, 0)])  4.05 us
  transfers between devices with their start and end apart: 15, of which 7 were waited for; matrix products, arithmetic and copies ran while one was open for 6% of the time, Pallas kernels for 1%

profile of v2, /device:TPU:1, one launch (start us, length us, event | category | flops | bytes accessed | tf_op | source)
XLA Modules:
  0.0 186.7 jit_solution(13130427612943388194)
XLA Ops:
  7.2 4.6 %collective-permute-start = (bf16[24,4096]{1,0:T(8,128)(2,1)}, bf16[24,4096]{1,0:T(8,128)(2,1)S(1)}, u32[]{:S(2)}, u32[]{:S(2)}) collective-permute-start(bf16[24,4096]{1,0:T(8,128)(2,1)} %param.5), channel_id=1, source_target_pairs={{0,0},{12,24},{24,12},{36,36},{1,1},{13,25},{25,13},{37,37},{2,2},... | collective-permute-start | bytes 589832 | tf_op jit(solution)/shard_map/ppermute | solution.py:31
  11.8 3.5 %collective-permute-done = bf16[24,4096]{1,0:T(8,128)(2,1)S(1)} collective-permute-done((bf16[24,4096]{1,0:T(8,128)(2,1)}, bf16[24,4096]{1,0:T(8,128)(2,1)S(1)}, u32[]{:S(2)}, u32[]{:S(2)}) %collective-permute-start) | collective-permute-done | bytes 196640 | tf_op jit(solution)/shard_map/ppermute | solution.py:31
  17.7 1.9 %collective-permute-start.1 = (bf16[3,2048,128]{2,1,0:T(8,128)(2,1)S(1)}, bf16[3,2048,128]{2,1,0:T(8,128)(2,1)S(1)}, u32[]{:S(2)}, u32[]{:S(2)}) collective-permute-start(bf16[3,2048,128]{2,1,0:T(8,128)(2,1)S(1)} %dynamic-slice_bitcast_fusion), channel_id=1, source_target_pairs={{0,588},{12,0},{24,36},{36,216},{192,12},{204,192},{216,228},{228,... | collective-permute-start | bytes 4718600 | tf_op jit(solution)/shard_map/ppermute | solution.py:31
  19.6 20.4 %collective-permute-done.1 = bf16[3,2048,128]{2,1,0:T(8,128)(2,1)S(1)} collective-permute-done((bf16[3,2048,128]{2,1,0:T(8,128)(2,1)S(1)}, bf16[3,2048,128]{2,1,0:T(8,128)(2,1)S(1)}, u32[]{:S(2)}, u32[]{:S(2)}) %collective-permute-start.1) | collective-permute-done | bytes 1572896 | tf_op jit(solution)/shard_map/ppermute | solution.py:31
  40.1 5.8 %collective-permute-start.2 = (bf16[3,2048,128]{2,1,0:T(8,128)(2,1)S(1)}, bf16[3,2048,128]{2,1,0:T(8,128)(2,1)S(1)}, u32[]{:S(2)}, u32[]{:S(2)}) collective-permute-start(bf16[3,2048,128]{2,1,0:T(8,128)(2,1)S(1)} %collective-permute-done.1), channel_id=1, source_target_pairs={{0,24},{24,0},{1,25},{25,1},{2,26},{26,2},{3,27},{27,3},{4,28},{28... | collective-permute-start | bytes 4718600 | tf_op jit(solution)/shard_map/ppermute | solution.py:175
  45.9 1.9 %collective-permute-start.6 = (f32[7,128]{1,0:T(8,128)S(1)}, f32[7,128]{1,0:T(8,128)S(1)}, u32[]{:S(2)}, u32[]{:S(2)}) collective-permute-start(f32[7,128]{1,0:T(8,128)S(1)} %copy-done.7), channel_id=1, source_target_pairs={{0,12},{12,0},{1,13},{13,1},{2,14},{14,2},{3,15},{15,3},{4,16},{16... | collective-permute-start | bytes 10760 | tf_op jit(solution)/shard_map/ppermute | solution.py:190
  47.8 3.5 %collective-permute-start.7 = (bf16[288,128]{1,0:T(8,128)(2,1)S(1)}, bf16[288,128]{1,0:T(8,128)(2,1)S(1)}, u32[]{:S(2)}, u32[]{:S(2)}) collective-permute-start(bf16[288,128]{1,0:T(8,128)(2,1)S(1)} %get-tuple-element.10), channel_id=1, source_target_pairs={{0,0},{12,24},{24,12},{36,36},{1,1},{13,25},{25,13},{37,37},{2,2},... | collective-permute-start | bytes 221192 | tf_op jit(solution)/shard_map/ppermute | solution.py:31
  51.4 1.9 %collective-permute-start.8 = (bf16[288,128]{1,0:T(8,128)(2,1)S(1)}, bf16[288,128]{1,0:T(8,128)(2,1)}, u32[]{:S(2)}, u32[]{:S(2)}) collective-permute-start(bf16[288,128]{1,0:T(8,128)(2,1)S(1)} %get-tuple-element.11), channel_id=1, source_target_pairs={{0,24},{12,0},{24,36},{36,12},{1,25},{13,1},{25,37},{37,13},{2,26}... | collective-permute-start | bytes 221192 | tf_op jit(solution)/shard_map/ppermute | solution.py:31
  53.3 2.1 %collective-permute-start.5 = (f32[3,3,128]{2,1,0:T(4,128)S(1)}, f32[3,3,128]{2,1,0:T(4,128)S(1)}, u32[]{:S(2)}, u32[]{:S(2)}) collective-permute-start(f32[3,3,128]{2,1,0:T(4,128)S(1)} %copy-done.6), channel_id=1, source_target_pairs={{0,12},{12,0},{1,13},{13,1},{2,14},{14,2},{3,15},{15,3},{4,16},{16... | collective-permute-start | bytes 13832 | tf_op jit(solution)/shard_map/ppermute | solution.py:190
  56.5 2.9 %collective-permute-start.9 = (bf16[8,256]{1,0:T(8,128)(2,1)S(1)}, bf16[8,256]{1,0:T(8,128)(2,1)S(1)}, u32[]{:S(2)}, u32[]{:S(2)}) collective-permute-start(bf16[8,256]{1,0:T(8,128)(2,1)S(1)} %slice.22), channel_id=1, source_target_pairs={{12,24},{24,0},{36,12},{48,36},{60,72},{72,48},{84,60},{96,84},{10... | collective-permute-start | bytes 12296 | tf_op jit(solution)/shard_map/ppermute | solution.py:31
  59.5 3.9 %maximum_select_fusion.1 = bf16[3,4096,128]{2,1,0:T(8,128)(2,1)S(1)} fusion(bf16[3,2048,128]{2,1,0:T(8,128)(2,1)S(1)} %collective-permute-done.2, bf16[3,2048,128]{2,1,0:T(8,128)(2,1)S(1)} %collective-permute-done.1, pred[]{:T(512)S(6)} %eq.5), kind=kLoop, calls=%fused_computation.1 | loop fusion | flops 14155776 | bytes 6291457 | tf_op jit(solution)/shard_map/jit(_where)/select_n | solution.py:176
  63.4 4.6 %maximum_select_fusion.w_ref = bf16[3,4096,256]{2,1,0:T(8,128)(2,1)} fusion(bf16[3,4096,128]{2,1,0:T(8,128)(2,1)S(1)} %maximum_select_fusion.1, bf16[3,4096,128]{2,1,0:T(8,128)(2,1)S(1)} %bitcast.3, pred[]{:T(512)S(6)} %eq.4), kind=kLoop, calls=%fused_computation | loop fusion | flops 28311552 | bytes 12582913 | tf_op jit(solution)/shard_map/jit(_where)/select_n | solution.py:183
  68.0 10.5 %all-gather.2.cloned.1.call-done.x_ref = bf16[288,4096]{1,0:T(8,128)(2,1)} async-done(((bf16[24,4096]{1,0:T(8,128)(2,1)}), bf16[288,4096]{1,0:T(8,128)(2,1)}) %all-gather.2.cloned.1.call-update) | async-done | bytes 2359312 | tf_op jit(solution)/shard_map/all_gather | solution.py:164
  78.5 2.8 %copy-done = bf16[3,4096,256]{2,1,0:T(8,128)(2,1)S(1)} copy-done((bf16[3,4096,256]{2,1,0:T(8,128)(2,1)S(1)}, bf16[3,4096,256]{2,1,0:T(8,128)(2,1)}, u32[]{:S(2)}) %copy-start) | copy-done | bytes 6291480
  82.9 2.4 %project.1.proj_ref = bf16[3,288,256]{2,1,0:T(8,128)(2,1)S(1)} custom-call(bf16[288,4096]{1,0:T(8,128)(2,1)S(1)} %copy-done.2, bf16[3,4096,256]{2,1,0:T(8,128)(2,1)S(1)} %copy-done), custom_call_target="tpu_custom_call" | custom-call | tf_op jit(solution)/shard_map/project/pallas_call | solution.py:45
  85.4 10.5 %collective-permute-start.3 = (bf16[3,8,256]{2,1,0:T(8,128)(2,1)S(1)}, bf16[3,8,256]{2,1,0:T(8,128)(2,1)S(1)}, u32[]{:S(2)}, u32[]{:S(2)}) collective-permute-start(bf16[3,8,256]{2,1,0:T(8,128)(2,1)S(1)} %get-tuple-element.7), channel_id=1, source_target_pairs={{0,24},{12,36},{24,12},{36,48},{48,72},{60,84},{72,60},{84,96},{96... | collective-permute-start | bytes 36872 | tf_op jit(solution)/shard_map/ppermute | solution.py:31
  95.9 1.9 %collective-permute-start.4 = (bf16[3,8,256]{2,1,0:T(8,128)(2,1)S(1)}, bf16[3,8,256]{2,1,0:T(8,128)(2,1)S(1)}, u32[]{:S(2)}, u32[]{:S(2)}) collective-permute-start(bf16[3,8,256]{2,1,0:T(8,128)(2,1)S(1)} %get-tuple-element.6), channel_id=1, source_target_pairs={{12,24},{24,0},{36,12},{48,36},{60,72},{72,48},{84,60},{96,84},{10... | collective-permute-start | bytes 36872 | tf_op jit(solution)/shard_map/ppermute | solution.py:31
  97.8 3.0 %collective-permute-done.4.next_ref = bf16[3,8,256]{2,1,0:T(8,128)(2,1)S(1)} collective-permute-done((bf16[3,8,256]{2,1,0:T(8,128)(2,1)S(1)}, bf16[3,8,256]{2,1,0:T(8,128)(2,1)S(1)}, u32[]{:S(2)}, u32[]{:S(2)}) %collective-permute-start.4) | collective-permute-done | bytes 12320 | tf_op jit(solution)/shard_map/ppermute | solution.py:31
  102.4 4.0 %spread.1 = bf16[288,4096]{1,0:T(8,128)(2,1)} custom-call(bf16[3,288,256]{2,1,0:T(8,128)(2,1)S(1)} %get-tuple-element.5.g_ref, bf16[3,4096,256]{2,1,0:T(8,128)(2,1)S(1)} %copy-done.1), custom_call_target="tpu_custom_call" | custom-call | tf_op jit(solution)/shard_map/spread/pallas_call | solution.py:73
  106.5 54.2 %reduce-scatter.2.cloned.1.call-done = bf16[24,4096]{1,0:T(8,128)(2,1)} async-done(((bf16[288,4096]{1,0:T(8,128)(2,1)}), bf16[24,4096]{1,0:T(8,128)(2,1)}) %reduce-scatter.2.cloned.1.call-update) | async-done | bytes 196624 | tf_op jit(solution)/shard_map/reduce_scatter | solution.py:213
  160.7 10.7 %collective-permute-start.12 = (bf16[24,4096]{1,0:T(8,128)(2,1)}, bf16[24,4096]{1,0:T(8,128)(2,1)S(1)}, u32[]{:S(2)}, u32[]{:S(2)}) collective-permute-start(bf16[24,4096]{1,0:T(8,128)(2,1)} %reduce-scatter.2.cloned.1.call-done), channel_id=1, source_target_pairs={{0,0},{12,24},{24,12},{36,36},{1,1},{13,25},{25,13},{37,37},{2,2},... | collective-permute-start | bytes 589832 | tf_op jit(solution)/shard_map/ppermute | solution.py:31
  171.4 1.9 %collective-permute-start.10 = (bf16[288,128]{1,0:T(8,128)(2,1)S(1)}, bf16[288,128]{1,0:T(8,128)(2,1)S(1)}, u32[]{:S(2)}, u32[]{:S(2)}) collective-permute-start(bf16[288,128]{1,0:T(8,128)(2,1)S(1)} %get-tuple-element.8), channel_id=1, source_target_pairs={{0,0},{12,24},{24,12},{36,36},{1,1},{13,25},{25,13},{37,37},{2,2},... | collective-permute-start | bytes 221192 | tf_op jit(solution)/shard_map/ppermute | solution.py:31
  173.3 1.9 %collective-permute-start.11 = (bf16[288,128]{1,0:T(8,128)(2,1)S(1)}, bf16[288,128]{1,0:T(8,128)(2,1)S(1)}, u32[]{:S(2)}, u32[]{:S(2)}) collective-permute-start(bf16[288,128]{1,0:T(8,128)(2,1)S(1)} %get-tuple-element.9), channel_id=1, source_target_pairs={{0,12},{12,36},{24,0},{36,24},{1,13},{13,37},{25,1},{37,25},{2,14}... | collective-permute-start | bytes 221192 | tf_op jit(solution)/shard_map/ppermute | solution.py:31
  175.3 1.8 collective-permute-done.10
  (39 shorter events, 9.4 us)
Async XLA Ops:
  7.2 38.7 %copy-start.7 = (f32[7,128]{1,0:T(8,128)S(1)}, f32[7,128]{1,0:T(8,128)}, u32[]{:S(2)}) copy-start(f32[7,128]{1,0:T(8,128)} %param.8) | copy-start | bytes 10756
  7.2 46.1 %copy-start.6 = (f32[3,3,128]{2,1,0:T(4,128)S(1)}, f32[3,3,128]{2,1,0:T(4,128)}, u32[]{:S(2)}) copy-start(f32[3,3,128]{2,1,0:T(4,128)} %param.7) | copy-start | bytes 13828
  7.2 71.3 %all-gather.2.cloned.1.call-start = ((), (), s32[]{:S(2)}) async-start(), calls=%async_computation.1 | async-start | bytes 2555904 | tf_op jit(solution)/shard_map/all_gather | solution.py:164
  7.2 8.2 %collective-permute-start = (bf16[24,4096]{1,0:T(8,128)(2,1)}, bf16[24,4096]{1,0:T(8,128)(2,1)S(1)}, u32[]{:S(2)}, u32[]{:S(2)}) collective-permute-start(bf16[24,4096]{1,0:T(8,128)(2,1)} %param.5), channel_id=1, source_target_pairs={{0,0},{12,24},{24,12},{36,36},{1,1},{13,25},{25,13},{37,37},{2,2},... | collective-permute-start | bytes 589832 | tf_op jit(solution)/shard_map/ppermute | solution.py:31
  15.4 0.7 copy-start.4
  16.1 31.7 %copy-start.5 = (bf16[576,128]{1,0:T(8,128)(2,1)S(1)}, bf16[576,128]{1,0:T(8,128)(2,1)}, u32[]{:S(2)}) copy-start(bf16[576,128]{1,0:T(8,128)(2,1)} %param.9) | copy-start | bytes 442372
  16.1 144.6 %reduce-scatter.2.cloned.1.call-start = ((), (), s32[]{:S(2)}) async-start(), calls=%async_computation.2 | async-start | bytes 2555904 | tf_op jit(solution)/shard_map/reduce_scatter | solution.py:213
  17.7 22.4 %collective-permute-start.1 = (bf16[3,2048,128]{2,1,0:T(8,128)(2,1)S(1)}, bf16[3,2048,128]{2,1,0:T(8,128)(2,1)S(1)}, u32[]{:S(2)}, u32[]{:S(2)}) collective-permute-start(bf16[3,2048,128]{2,1,0:T(8,128)(2,1)S(1)} %dynamic-slice_bitcast_fusion), channel_id=1, source_target_pairs={{0,588},{12,0},{24,36},{36,216},{192,12},{204,192},{216,228},{228,... | collective-permute-start | bytes 4718600 | tf_op jit(solution)/shard_map/ppermute | solution.py:31
  40.1 19.4 %collective-permute-start.2 = (bf16[3,2048,128]{2,1,0:T(8,128)(2,1)S(1)}, bf16[3,2048,128]{2,1,0:T(8,128)(2,1)S(1)}, u32[]{:S(2)}, u32[]{:S(2)}) collective-permute-start(bf16[3,2048,128]{2,1,0:T(8,128)(2,1)S(1)} %collective-permute-done.1), channel_id=1, source_target_pairs={{0,24},{24,0},{1,25},{25,1},{2,26},{26,2},{3,27},{27,3},{4,28},{28... | collective-permute-start | bytes 4718600 | tf_op jit(solution)/shard_map/ppermute | solution.py:175
  45.9 9.6 %collective-permute-start.6 = (f32[7,128]{1,0:T(8,128)S(1)}, f32[7,128]{1,0:T(8,128)S(1)}, u32[]{:S(2)}, u32[]{:S(2)}) collective-permute-start(f32[7,128]{1,0:T(8,128)S(1)} %copy-done.7), channel_id=1, source_target_pairs={{0,12},{12,0},{1,13},{13,1},{2,14},{14,2},{3,15},{15,3},{4,16},{16... | collective-permute-start | bytes 10760 | tf_op jit(solution)/shard_map/ppermute | solution.py:190
  47.8 7.7 %collective-permute-start.7 = (bf16[288,128]{1,0:T(8,128)(2,1)S(1)}, bf16[288,128]{1,0:T(8,128)(2,1)S(1)}, u32[]{:S(2)}, u32[]{:S(2)}) collective-permute-start(bf16[288,128]{1,0:T(8,128)(2,1)S(1)} %get-tuple-element.10), channel_id=1, source_target_pairs={{0,0},{12,24},{24,12},{36,36},{1,1},{13,25},{25,13},{37,37},{2,2},... | collective-permute-start | bytes 221192 | tf_op jit(solution)/shard_map/ppermute | solution.py:31
  51.4 4.1 %collective-permute-start.8 = (bf16[288,128]{1,0:T(8,128)(2,1)S(1)}, bf16[288,128]{1,0:T(8,128)(2,1)}, u32[]{:S(2)}, u32[]{:S(2)}) collective-permute-start(bf16[288,128]{1,0:T(8,128)(2,1)S(1)} %get-tuple-element.11), channel_id=1, source_target_pairs={{0,24},{12,0},{24,36},{36,12},{1,25},{13,1},{25,37},{37,13},{2,26}... | collective-permute-start | bytes 221192 | tf_op jit(solution)/shard_map/ppermute | solution.py:31
  53.3 44.5 %collective-permute-start.5 = (f32[3,3,128]{2,1,0:T(4,128)S(1)}, f32[3,3,128]{2,1,0:T(4,128)S(1)}, u32[]{:S(2)}, u32[]{:S(2)}) collective-permute-start(f32[3,3,128]{2,1,0:T(4,128)S(1)} %copy-done.6), channel_id=1, source_target_pairs={{0,12},{12,0},{1,13},{13,1},{2,14},{14,2},{3,15},{15,3},{4,16},{16... | collective-permute-start | bytes 13832 | tf_op jit(solution)/shard_map/ppermute | solution.py:190
  56.5 6.9 %copy-start.3 = (bf16[4096,3,128]{2,0,1:T(8,128)(2,1)S(1)}, bf16[4096,3,128]{2,0,1:T(8,128)(2,1)}, u32[]{:S(2)}) copy-start(bf16[4096,3,128]{2,0,1:T(8,128)(2,1)} %param.6) | copy-start | bytes 9437188
  56.5 41.3 %collective-permute-start.9 = (bf16[8,256]{1,0:T(8,128)(2,1)S(1)}, bf16[8,256]{1,0:T(8,128)(2,1)S(1)}, u32[]{:S(2)}, u32[]{:S(2)}) collective-permute-start(bf16[8,256]{1,0:T(8,128)(2,1)S(1)} %slice.22), channel_id=1, source_target_pairs={{12,24},{24,0},{36,12},{48,36},{60,72},{72,48},{84,60},{96,84},{10... | collective-permute-start | bytes 12296 | tf_op jit(solution)/shard_map/ppermute | solution.py:31
  78.5 2.8 %copy-start = (bf16[3,4096,256]{2,1,0:T(8,128)(2,1)S(1)}, bf16[3,4096,256]{2,1,0:T(8,128)(2,1)}, u32[]{:S(2)}) copy-start(bf16[3,4096,256]{2,1,0:T(8,128)(2,1)} %maximum_select_fusion.w_ref) | copy-start | bytes 18874372
  81.2 1.7 copy-start.2
  82.9 19.5 %copy-start.1 = (bf16[3,4096,256]{2,1,0:T(8,128)(2,1)S(1)}, bf16[3,4096,256]{2,1,0:T(8,128)(2,1)}, u32[]{:S(2)}) copy-start(bf16[3,4096,256]{2,1,0:T(8,128)(2,1)} %maximum_select_fusion.w_ref) | copy-start | bytes 18874372
  85.4 12.5 %collective-permute-start.3 = (bf16[3,8,256]{2,1,0:T(8,128)(2,1)S(1)}, bf16[3,8,256]{2,1,0:T(8,128)(2,1)S(1)}, u32[]{:S(2)}, u32[]{:S(2)}) collective-permute-start(bf16[3,8,256]{2,1,0:T(8,128)(2,1)S(1)} %get-tuple-element.7), channel_id=1, source_target_pairs={{0,24},{12,36},{24,12},{36,48},{48,72},{60,84},{72,60},{84,96},{96... | collective-permute-start | bytes 36872 | tf_op jit(solution)/shard_map/ppermute | solution.py:31
  95.9 5.0 %collective-permute-start.4 = (bf16[3,8,256]{2,1,0:T(8,128)(2,1)S(1)}, bf16[3,8,256]{2,1,0:T(8,128)(2,1)S(1)}, u32[]{:S(2)}, u32[]{:S(2)}) collective-permute-start(bf16[3,8,256]{2,1,0:T(8,128)(2,1)S(1)} %get-tuple-element.6), channel_id=1, source_target_pairs={{12,24},{24,0},{36,12},{48,36},{60,72},{72,48},{84,60},{96,84},{10... | collective-permute-start | bytes 36872 | tf_op jit(solution)/shard_map/ppermute | solution.py:31
  160.7 18.4 %collective-permute-start.12 = (bf16[24,4096]{1,0:T(8,128)(2,1)}, bf16[24,4096]{1,0:T(8,128)(2,1)S(1)}, u32[]{:S(2)}, u32[]{:S(2)}) collective-permute-start(bf16[24,4096]{1,0:T(8,128)(2,1)} %reduce-scatter.2.cloned.1.call-done), channel_id=1, source_target_pairs={{0,0},{12,24},{24,12},{36,36},{1,1},{13,25},{25,13},{37,37},{2,2},... | collective-permute-start | bytes 589832 | tf_op jit(solution)/shard_map/ppermute | solution.py:31
  171.4 5.7 %collective-permute-start.10 = (bf16[288,128]{1,0:T(8,128)(2,1)S(1)}, bf16[288,128]{1,0:T(8,128)(2,1)S(1)}, u32[]{:S(2)}, u32[]{:S(2)}) collective-permute-start(bf16[288,128]{1,0:T(8,128)(2,1)S(1)} %get-tuple-element.8), channel_id=1, source_target_pairs={{0,0},{12,24},{24,12},{36,36},{1,1},{13,25},{25,13},{37,37},{2,2},... | collective-permute-start | bytes 221192 | tf_op jit(solution)/shard_map/ppermute | solution.py:31
  173.3 5.1 %collective-permute-start.11 = (bf16[288,128]{1,0:T(8,128)(2,1)S(1)}, bf16[288,128]{1,0:T(8,128)(2,1)S(1)}, u32[]{:S(2)}, u32[]{:S(2)}) collective-permute-start(bf16[288,128]{1,0:T(8,128)(2,1)S(1)} %get-tuple-element.9), channel_id=1, source_target_pairs={{0,12},{12,36},{24,0},{36,24},{1,13},{13,37},{25,1},{37,25},{2,14}... | collective-permute-start | bytes 221192 | tf_op jit(solution)/shard_map/ppermute | solution.py:31
Sparse Core Ops, SparseCore 0:
  16.2 62.2 all-gather.1
  106.6 54.0 reduce-scatter.1

commit v3 on v2

v3 whole, which is shorter than its diff:
```python
import jax
import jax.numpy as jnp
from jax import lax
from jax.experimental import pallas as pl
from jax.experimental.pallas import tpu as pltpu
from jax.sharding import Mesh
from jax.sharding import PartitionSpec as P

CTX = ("yh", "x", "c")
TP = ("yl", "zh", "zl")
RING = ("zh", "zl")
HALO = 8
SHARD = 24


def exchange(value, axes, sizes, route):
    total = 1
    for size in sizes:
        total *= size
    pairs = []
    for source in range(total):
        coords, rest = [], source
        for size in reversed(sizes):
            coords.append(rest % size)
            rest //= size
        target = route(*reversed(coords))
        if target is None:
            continue
        flat = 0
        for place, size in zip(target, sizes):
            flat = flat * size + place
        pairs.append((source, flat))
    return lax.ppermute(value, axes, pairs)


def swap_homes(value):
    return exchange(value, ("c", "yl"), (2, 2), lambda c, yl: (yl, c))


def fetch(source, target, sems):
    copies = [
        pltpu.make_async_copy(source(i), target(i), sems.at[i]) for i in range(sems.shape[0])
    ]
    for copy in copies:
        copy.start()
    return copies


def project_own_kernel(x_ref, w_ref, o_ref, w_buf, sems):
    copies = fetch(lambda j: w_ref.at[j], lambda j: w_buf.at[j], sems)
    for part, copy in enumerate(copies):
        copy.wait()
        total = jnp.dot(x_ref[...], w_buf[part], preferred_element_type=jnp.float32)
        o_ref[part] = total.astype(o_ref.dtype)


def project_rest_kernel(lane_ref, plus_ref, minus_ref, own_ref, w_ref, o_ref, head_ref, tail_ref, w_buf, sems):
    copies = fetch(lambda j: w_ref.at[j], lambda j: w_buf.at[j], sems)
    rows = jnp.concatenate([plus_ref[...], minus_ref[...]], axis=0)
    count = plus_ref.shape[0]
    lane = lane_ref[0]
    for part, copy in enumerate(copies):
        copy.wait()
        total = jnp.dot(rows, w_buf[part], preferred_element_type=jnp.float32)
        own = own_ref[part].astype(jnp.float32)
        plus, minus = total[:count], total[count:]
        o_ref[part] = total.astype(o_ref.dtype)

        def pick(chosen, start):
            third = [block[start : start + HALO] for block in (own, plus, minus)]
            ahead = lax.rem(lane + 1, 3)
            value = jnp.where(ahead == chosen, third[1], third[2])
            return jnp.where(lane == chosen, third[0], value)

        head_ref[part] = pick(0, 0).astype(head_ref.dtype)
        tail_ref[part] = pick(2, count - HALO).astype(tail_ref.dtype)


def vmem():
    return pl.BlockSpec(memory_space=pltpu.MemorySpace.VMEM)


def smem():
    return pl.BlockSpec(memory_space=pltpu.MemorySpace.SMEM)


def hbm():
    return pl.BlockSpec(memory_space=pltpu.MemorySpace.HBM)


PARAMS = pltpu.CompilerParams(vmem_limit_bytes=48 * 1024 * 1024)


def project_own(rows, weight):
    parts, _, channels = weight.shape
    return pl.pallas_call(
        project_own_kernel,
        in_specs=[vmem(), hbm()],
        out_specs=vmem(),
        out_shape=jax.ShapeDtypeStruct((parts, rows.shape[0], channels), jnp.bfloat16),
        scratch_shapes=[pltpu.VMEM(weight.shape, weight.dtype), pltpu.SemaphoreType.DMA((parts,))],
        compiler_params=PARAMS,
        name="project_own",
    )(rows, weight)


def project_rest(lane, plus, minus, own, weight):
    parts, _, channels = weight.shape
    edge = jax.ShapeDtypeStruct((parts, HALO, channels), jnp.bfloat16)
    return pl.pallas_call(
        project_rest_kernel,
        in_specs=[smem(), vmem(), vmem(), vmem(), hbm()],
        out_specs=[vmem(), vmem(), vmem()],
        out_shape=[
            jax.ShapeDtypeStruct((parts, 2 * plus.shape[0], channels), jnp.bfloat16),
            edge,
            edge,
        ],
        scratch_shapes=[pltpu.VMEM(weight.shape, weight.dtype), pltpu.SemaphoreType.DMA((parts,))],
        compiler_params=PARAMS,
        name="project_rest",
    )(lane, plus, minus, own, weight)


def join_kernel(place_ref, mine_ref, came_ref, rest_ref, o_ref):
    lanes = mine_ref.shape[2]
    half = pl.program_id(1)
    theirs = jnp.where(half == place_ref[1], came_ref[0], rest_ref[0])
    mine = mine_ref[0]
    first = place_ref[0] == 0
    o_ref[0, :, :lanes] = jnp.where(first, mine, theirs)
    o_ref[0, :, lanes:] = jnp.where(first, theirs, mine)


def join(place, mine, came, rest):
    parts, depth, lanes = mine.shape
    half = depth // 2
    return pl.pallas_call(
        join_kernel,
        grid=(parts, 2),
        in_specs=[
            smem(),
            pl.BlockSpec((1, half, lanes), lambda j, k: (j, k, 0)),
            pl.BlockSpec((1, half, lanes), lambda j, k: (j, 0, 0)),
            pl.BlockSpec((1, half, lanes), lambda j, k: (j, 0, 0)),
        ],
        out_specs=pl.BlockSpec((1, half, 2 * lanes), lambda j, k: (j, k, 0)),
        out_shape=jax.ShapeDtypeStruct((parts, depth, 2 * lanes), mine.dtype),
        compiler_params=PARAMS,
        name="join",
    )(place, mine, came, rest)


def causal(series, taps):
    total = taps[0:1] * series
    for offset in range(1, taps.shape[0]):
        total = total + taps[offset : offset + 1] * pltpu.roll(series, offset, 0)
    return total


def adjoint(series, taps):
    total = taps[0:1] * series
    for offset in range(1, taps.shape[0]):
        total = total + taps[offset : offset + 1] * pltpu.roll(series, series.shape[0] - offset, 0)
    return total


def mix_kernel(
    lane_ref, own_ref, rest_ref, prev_ref, next_ref, feat_ref, inner_ref, grad_ref, grad_next_ref, w_ref,
    gated_ref, keep_ref, plus_ref, minus_ref,
    window, back, w_buf, sems,
):
    parts, count, channels = own_ref.shape
    total_rows = grad_ref.shape[0]
    last = HALO + total_rows
    block = w_buf.shape[1] // sems.shape[0]
    copies = fetch(
        lambda i: w_ref.at[:, pl.ds(i * block, block), :],
        lambda i: w_buf.at[:, pl.ds(i * block, block), :],
        sems,
    )
    lane = lane_ref[0]
    groups = [lane, lax.rem(lane + 1, 3), lax.rem(lane + 2, 3)]
    shard = SHARD
    members = count // shard

    def start(group, member):
        return pl.multiple_of((3 * member + groups[group]) * shard, 8)

    for part in range(parts):
        window[part, :HALO] = prev_ref[part].astype(jnp.float32)
        window[part, last:] = next_ref[part].astype(jnp.float32)
        blocks = (own_ref[part], rest_ref[part, :count], rest_ref[part, count:])
        for group, rows in enumerate(blocks):
            rows = rows.astype(jnp.float32)
            for member in range(members):
                window[part, pl.ds(start(group, member) + HALO, shard)] = rows[
                    member * shard : (member + 1) * shard
                ]
    lanes = min(channels, 128)
    for side in range(channels // lanes):
        cut = slice(side * lanes, (side + 1) * lanes)
        inner_taps = inner_ref[:, cut]
        feat = [feat_ref[part][:, cut] for part in range(parts)]
        query = causal(window[0, :, cut], feat[0])
        key = causal(window[1, :, cut], feat[1])
        value = causal(window[2, :, cut], feat[2])
        inner = causal(key * value, inner_taps)
        gated_ref[:, cut] = (query * inner)[HALO:last].astype(gated_ref.dtype)
        grad_next = grad_next_ref[:, cut]
        grad = jnp.concatenate([jnp.zeros_like(grad_next), grad_ref[:, cut], grad_next], axis=0)
        grad = grad.astype(jnp.float32)
        mixed = adjoint(grad * query, inner_taps)
        back[0, :, cut] = adjoint(grad * inner, feat[0])[HALO:last]
        back[1, :, cut] = adjoint(mixed * value, feat[1])[HALO:last]
        back[2, :, cut] = adjoint(mixed * key, feat[2])[HALO:last]
    left = [
        jnp.concatenate(
            [
                back[part, pl.ds(start(group, member), shard)]
                for group in range(3)
                for member in range(members)
            ],
            axis=0,
        ).astype(jnp.bfloat16)
        for part in range(parts)
    ]
    contract = (((1,), (1,)), ((), ()))
    for i, copy in enumerate(copies):
        copy.wait()
        cut = slice(i * block, (i + 1) * block)
        total = lax.dot_general(left[0], w_buf[0, cut], contract, preferred_element_type=jnp.float32)
        for part in range(1, parts):
            total = total + lax.dot_general(
                left[part], w_buf[part, cut], contract, preferred_element_type=jnp.float32
            )
        keep_ref[:, cut] = total[:count]
        plus_ref[:, cut] = total[count : 2 * count].astype(plus_ref.dtype)
        minus_ref[:, cut] = total[2 * count :].astype(minus_ref.dtype)


def mix(lane, own, rest, prev, following, feat, inner, grad, grad_next, weight):
    parts, count, channels = own.shape
    depth = weight.shape[1]
    rows = grad.shape[0]
    steps = max(1, depth // 512)
    return pl.pallas_call(
        mix_kernel,
        in_specs=[smem()] + [vmem()] * 8 + [hbm()],
        out_specs=[vmem()] * 4,
        out_shape=[
            jax.ShapeDtypeStruct((rows, channels), jnp.bfloat16),
            jax.ShapeDtypeStruct((count, depth), jnp.float32),
            jax.ShapeDtypeStruct((count, depth), jnp.bfloat16),
            jax.ShapeDtypeStruct((count, depth), jnp.bfloat16),
        ],
        scratch_shapes=[
            pltpu.VMEM((parts, rows + 2 * HALO, channels), jnp.float32),
            pltpu.VMEM((parts, rows, channels), jnp.float32),
            pltpu.VMEM(weight.shape, weight.dtype),
            pltpu.SemaphoreType.DMA((steps,)),
        ],
        compiler_params=PARAMS,
        name="mix",
    )(lane, own, rest, prev, following, feat, inner, grad, grad_next, weight)


def build(sizes):
    ring = sizes[0] * 2

    strips = sizes[0] * sizes[1] * 4

    def along(value, step):
        def route(yh, x, c, yl):
            strip = ((yh * sizes[1] + x) * 2 + yl) * 2 + c + step
            if not 0 <= strip < strips:
                return None
            return (strip // 4 // sizes[1], strip // 4 % sizes[1], strip % 2, strip // 2 % 2)

        return exchange(value, ("yh", "x", "c", "yl"), (sizes[0], sizes[1], 2, 2), route)

    spots = sizes[4] * sizes[5]

    def turn(value, step):
        return lax.ppermute(value, RING, [(z, (z + step) % spots) for z in range(spots)])

    def local(tokens, proj_weight, feat_taps, inner_taps, grad_out):
        upper = lax.axis_index("yl")
        core = lax.axis_index("c")
        lane = lax.axis_index("zl").astype(jnp.int32).reshape(1)
        width = proj_weight.shape[0]
        channels = inner_taps.shape[1]

        rehomed = swap_homes(tokens)
        padded = jnp.concatenate([rehomed, rehomed[:8]], axis=0)
        own = lax.all_gather(padded, "zh", axis=0, tiled=False)
        own = own[:, :SHARD].reshape(sizes[4] * SHARD, width)

        planes = proj_weight.transpose(1, 0, 2)
        half = width // 2
        sent = lax.dynamic_slice_in_dim(planes, core * half, half, 1)

        def beside(yh, c, yl):
            place = (yh * 2 + yl + (1 if c else ring - 1)) % ring
            return (place // 2, c, place % 2)

        came = exchange(sent, ("yh", "c", "yl"), (sizes[0], 2, 2), beside)

        def both(mine, theirs, axis):
            return jnp.where(
                upper == 0,
                jnp.concatenate([mine, theirs], axis=axis),
                jnp.concatenate([theirs, mine], axis=axis),
            )

        taps = jnp.concatenate([feat_taps.reshape(9, channels), inner_taps], axis=0)
        taps = both(taps, lax.ppermute(taps, "yl", [(0, 1), (1, 0)]), 1)
        feat = taps[:9].reshape(3, 3, 2 * channels)
        inner = taps[9:]

        count = grad_out.shape[0] // 2
        near = lax.dynamic_slice_in_dim(grad_out, upper * count, count, 0)
        far = lax.dynamic_slice_in_dim(grad_out, (1 - upper) * count, count, 0)
        near = swap_homes(near)
        far = exchange(far, ("c", "yl"), (2, 2), lambda c, yl: (1 - yl, c))
        grad = jnp.where(
            core == 0,
            jnp.concatenate([near, far], axis=1),
            jnp.concatenate([far, near], axis=1),
        )
        grad_next = along(grad[:HALO], -1)

        came, grad, grad_next, feat, inner = lax.optimization_barrier((came, grad, grad_next, feat, inner))
        rest = lax.ppermute(came, "c", [(0, 1), (1, 0)])
        weight = join(jnp.stack([upper, core]).astype(jnp.int32), planes, came, rest)

        plus, minus = turn(own, -1), turn(own, 1)
        proj_own = project_own(own, weight)
        proj_rest, head, tail = project_rest(lane, plus, minus, proj_own, weight)
        prev = along(tail, 1)
        following = along(head, -1)
        gated, keep, to_plus, to_minus = mix(
            lane, proj_own, proj_rest, prev, following, feat, inner, grad, grad_next, weight
        )
        summed = keep + turn(to_plus, 1).astype(jnp.float32) + turn(to_minus, -1).astype(jnp.float32)
        grad_tokens = lax.psum_scatter(
            summed.astype(jnp.bfloat16), "zh", scatter_dimension=0, tiled=True
        )

        first, second = gated[:, :channels], gated[:, channels:]
        near = swap_homes(jnp.where(core == 0, first, second))
        far = exchange(
            jnp.where(core == 0, second, first), ("c", "yl"), (2, 2), lambda c, yl: (yl, 1 - c)
        )
        gated = jnp.where(
            upper == 0,
            jnp.concatenate([near, far], axis=0),
            jnp.concatenate([far, near], axis=0),
        )
        grad_tokens, gated = lax.optimization_barrier((grad_tokens, gated))
        return (gated, swap_homes(grad_tokens))

    return local


def solution(mesh):
    sizes = (4, 4, 2, 2, 4, 3)
    grid = Mesh(mesh.devices.reshape(sizes), CTX + TP)
    in_specs = (
        P(CTX + TP, None),
        P(None, None, TP),
        P(None, None, TP),
        P(None, TP),
        P(CTX, TP),
    )
    out_specs = (P(CTX, TP), P(CTX + TP, None))
    return jax.shard_map(build(sizes), mesh=grid, in_specs=in_specs, out_specs=out_specs, check_vma=False)
```

time: 187 us -> 220 us (1.18)
  waiting for transfers between devices: 95 us -> 119 us
  Pallas kernels: 7.97 us -> 21.4 us
  other arithmetic: 10.2 us -> 2.71 us
  starting transfers between devices: 51.7 us -> 56.8 us
  local copies, waits for them, and re-layouts: 7.4 us -> 4.69 us
    ppermute x2 -> x5, waiting for transfers between devices: 0.01 us -> 24.3 us  [the longest x4 24.3 us: turn(): lax.ppermute(value, RING, [(z, (z + step) % spots) for z in range(spots)])]
    all_gather x1, waiting for transfers between devices: 10.5 us -> 34.2 us  [local(): own = lax.all_gather(padded, 'zh', axis=0, tiled=False)]
    reduce_scatter x1, waiting for transfers between devices: 54.2 us -> 32 us  [local(): lax.psum_scatter(summed.astype(jnp.bfloat16), 'zh', scatter_dimension=0,...]
    pallas_call x3 -> x4, Pallas kernels: 7.97 us -> 21.4 us  [the longest x1 7.4 us: join(): pl.pallas_call(join_kernel, grid=(parts, 2), in_specs=[smem(), pl.BlockSp...]
    ppermute x2 -> x5, starting transfers between devices: 4.05 us -> 15.5 us  [the longest x4 11.8 us: turn(): lax.ppermute(value, RING, [(z, (z + step) % spots) for z in range(spots)])]
    unnamed x17 -> x9, local copies, waits for them, and re-layouts: 5.83 us -> 0.69 us
    select_n x3 -> x1, other arithmetic: 4.57 us -> 0.01 us  [both(): jnp.where(upper == 0, jnp.concatenate([mine, theirs], axis=axis), jnp.con...]
    select_n x1 -> x0, other arithmetic: 3.93 us -> none  [local(): jnp.where(core == 0, jnp.concatenate([came, rest], axis=1), jnp.concatena...]
  transfers between devices with their start and end apart: 15 -> 18, of which waited for: 7 -> 12; matrix products, arithmetic and copies ran while one was open for 6% -> 1% of each run, Pallas kernels for 1% -> 5%
where the time goes in v3:
time: 220 us; the launch traced here: 219 us
  waiting for transfers between devices  119 us (54%)
  starting transfers between devices  56.8 us (26%)
  Pallas kernels  21.4 us (10%)
  between operations  14.4 us (7%)
  local copies, waits for them, and re-layouts  4.69 us (2%)
  other arithmetic  2.71 us (1%)
    ppermute x10, starting transfers between devices, exchange(): return lax.ppermute(value, axes, pairs)  39.3 us
    all_gather x1, waiting for transfers between devices, local(): own = lax.all_gather(padded, 'zh', axis=0, tiled=False)  34.2 us
    reduce_scatter x1, waiting for transfers between devices, local(): lax.psum_scatter(summed.astype(jnp.bfloat16), 'zh', scatter_dimension=0,...  32 us
    ppermute x10, waiting for transfers between devices, exchange(): return lax.ppermute(value, axes, pairs)  28.3 us
    ppermute x4, waiting for transfers between devices, turn(): lax.ppermute(value, RING, [(z, (z + step) % spots) for z in range(spots)])  24.3 us
    ppermute x4, starting transfers between devices, turn(): lax.ppermute(value, RING, [(z, (z + step) % spots) for z in range(spots)])  11.8 us
    pallas_call x1, Pallas kernels, join(): pl.pallas_call(join_kernel, grid=(parts, 2), in_specs=[smem(), pl.BlockSp...  7.4 us
    pallas_call x1, Pallas kernels, project_rest(): pl.pallas_call(project_rest_kernel, in_specs=[smem(), vmem(), vmem(), vme...  5.3 us
  transfers between devices with their start and end apart: 18, of which 12 were waited for; matrix products, arithmetic and copies ran while one was open for 1% of the time, Pallas kernels for 5%

profile of v3, /device:TPU:1, one launch (start us, length us, event | category | flops | bytes accessed | tf_op | source)
XLA Modules:
  0.0 218.9 jit_solution(7218606298868997862)
XLA Ops:
  7.3 2.8 %dynamic-slice_bitcast_fusion = bf16[3,2048,128]{2,1,0:T(8,128)(2,1)} fusion(bf16[4096,3,128]{2,0,1:T(8,128)(2,1)} %param.6, s32[]{:T(128)S(6)} %select_n.45), kind=kLoop, calls=%fused_computation.1 | loop fusion | bytes 3145732 | tf_op jit(solution)/shard_map/dynamic_slice | solution.py:301
  10.0 4.0 %collective-permute-start.1 = (bf16[3,2048,128]{2,1,0:T(8,128)(2,1)}, bf16[3,2048,128]{2,1,0:T(8,128)(2,1)S(1)}, u32[]{:S(2)}, u32[]{:S(2)}) collective-permute-start(bf16[3,2048,128]{2,1,0:T(8,128)(2,1)} %dynamic-slice_bitcast_fusion), channel_id=1, source_target_pairs={{0,588},{12,0},{24,36},{36,216},{192,12},{204,192},{216,228},{228,... | collective-permute-start | bytes 4718600 | tf_op jit(solution)/shard_map/ppermute | solution.py:33
  14.1 11.9 %collective-permute-start = (bf16[24,4096]{1,0:T(8,128)(2,1)S(1)}, bf16[24,4096]{1,0:T(8,128)(2,1)S(1)}, u32[]{:S(2)}, u32[]{:S(2)}) collective-permute-start(bf16[24,4096]{1,0:T(8,128)(2,1)S(1)} %copy-done.3), channel_id=1, source_target_pairs={{0,0},{12,24},{24,12},{36,36},{1,1},{13,25},{25,13},{37,37},{2,2},... | collective-permute-start | bytes 589832 | tf_op jit(solution)/shard_map/ppermute | solution.py:33
  26.0 18.5 %collective-permute-done = bf16[24,4096]{1,0:T(8,128)(2,1)S(1)} collective-permute-done((bf16[24,4096]{1,0:T(8,128)(2,1)S(1)}, bf16[24,4096]{1,0:T(8,128)(2,1)S(1)}, u32[]{:S(2)}, u32[]{:S(2)}) %collective-permute-start) | collective-permute-done | bytes 196640 | tf_op jit(solution)/shard_map/ppermute | solution.py:33
  49.2 3.7 %collective-permute-start.5 = (f32[16,128]{1,0:T(8,128)S(1)}, f32[16,128]{1,0:T(8,128)S(1)}, u32[]{:S(2)}, u32[]{:S(2)}) collective-permute-start(f32[16,128]{1,0:T(8,128)S(1)} %pad_maximum_fusion.1), channel_id=1, source_target_pairs={{0,12},{12,0},{1,13},{13,1},{2,14},{14,2},{3,15},{15,3},{4,16},{16... | collective-permute-start | bytes 24584 | tf_op jit(solution)/shard_map/ppermute | solution.py:317
  53.1 2.5 %collective-permute-start.4 = (bf16[8,256]{1,0:T(8,128)(2,1)S(1)}, bf16[8,256]{1,0:T(8,128)(2,1)S(1)}, u32[]{:S(2)}, u32[]{:S(2)}) collective-permute-start(bf16[8,256]{1,0:T(8,128)(2,1)S(1)} %slice.30), channel_id=1, source_target_pairs={{12,24},{24,0},{36,12},{48,36},{60,72},{72,48},{84,60},{96,84},{10... | collective-permute-start | bytes 12296 | tf_op jit(solution)/shard_map/ppermute | solution.py:33
  55.6 2.4 %collective-permute-done.4.grad_next_ref = bf16[8,256]{1,0:T(8,128)(2,1)S(1)} collective-permute-done((bf16[8,256]{1,0:T(8,128)(2,1)S(1)}, bf16[8,256]{1,0:T(8,128)(2,1)S(1)}, u32[]{:S(2)}, u32[]{:S(2)}) %collective-permute-start.4) | collective-permute-done | bytes 4128 | tf_op jit(solution)/shard_map/ppermute | solution.py:33
  59.9 34.2 %all-gather.3.cloned.1.call-done = bf16[128,4096]{1,0:T(8,128)(2,1)} async-done(((bf16[32,4096]{1,0:T(8,128)(2,1)}), bf16[128,4096]{1,0:T(8,128)(2,1)}) %all-gather.3.cloned.1.call-update) | async-done | bytes 1048592 | tf_op jit(solution)/shard_map/all_gather | solution.py:296
  97.2 3.4 %collective-permute-start.8 = (bf16[96,4096]{1,0:T(8,128)(2,1)S(1)}, bf16[96,4096]{1,0:T(8,128)(2,1)}, u32[]{:S(2)}, u32[]{:S(2)}) collective-permute-start(bf16[96,4096]{1,0:T(8,128)(2,1)S(1)} %bitcast.10), channel_id=1, source_target_pairs={{0,1},{1,2},{2,3},{3,4},{4,5},{5,6},{6,7},{7,8},{8,9},{9,10},{10,1... | collective-permute-start | bytes 2359304 | tf_op jit(solution)/shard_map/ppermute | solution.py:285
  100.7 7.4 %join.1.w_ref = bf16[3,4096,256]{2,1,0:T(8,128)(2,1)} custom-call(s32[2]{0:T(128)S(1)} %pad_add_fusion.place_ref, bf16[3,4096,128]{2,1,0:T(8,128)(2,1)} %bitcast.12, bf16[3,2048,128]{2,1,0:T(8,128)(2,1)S(1)} %collective-permute-done.1.came_ref, bf16[3,2048,128]{2,1,0:T(8,128)(2,1)} %collective-permute-done.6.rest_ref), custom_call_target="tpu_custom_call" | custom-call | tf_op jit(solution)/shard_map/join/pallas_call | solution.py:138
  108.1 3.6 %project_own.1.own_ref = bf16[3,96,256]{2,1,0:T(8,128)(2,1)S(1)} custom-call(bf16[96,4096]{1,0:T(8,128)(2,1)S(1)} %bitcast.11, bf16[3,4096,256]{2,1,0:T(8,128)(2,1)} %join.1.w_ref), custom_call_target="tpu_custom_call" | custom-call | tf_op jit(solution)/shard_map/project_own/pallas_call | solution.py:96
  111.7 3.8 %collective-permute-done.7.plus_ref = bf16[96,4096]{1,0:T(8,128)(2,1)S(1)} collective-permute-done((bf16[96,4096]{1,0:T(8,128)(2,1)S(1)}, bf16[96,4096]{1,0:T(8,128)(2,1)S(1)}, u32[]{:S(2)}, u32[]{:S(2)}) %collective-permute-start.7) | collective-permute-done | bytes 786464 | tf_op jit(solution)/shard_map/ppermute | solution.py:285
  115.5 3.1 %collective-permute-done.8.minus_ref = bf16[96,4096]{1,0:T(8,128)(2,1)} collective-permute-done((bf16[96,4096]{1,0:T(8,128)(2,1)S(1)}, bf16[96,4096]{1,0:T(8,128)(2,1)}, u32[]{:S(2)}, u32[]{:S(2)}) %collective-permute-start.8) | collective-permute-done | bytes 786464 | tf_op jit(solution)/shard_map/ppermute | solution.py:285
  118.7 5.3 %project_rest.1 = (bf16[3,192,256]{2,1,0:T(8,128)(2,1)S(1)}, bf16[3,8,256]{2,1,0:T(8,128)(2,1)S(1)}, bf16[3,8,256]{2,1,0:T(8,128)(2,1)S(1)}) custom-call(s32[1]{0:T(128)} %bitcast.lane_ref, bf16[96,4096]{1,0:T(8,128)(2,1)S(1)} %collective-permute-done.7.plus_ref, bf16[96,4096]{1,0:T(8,128)(2,1)} %collective-permute-done.8.minus_ref, ...), custom_call_target="tpu_custom_call" | custom-call | tf_op jit(solution)/shard_map/project_rest/pallas_call | solution.py:110
  124.0 3.6 %collective-permute-start.10 = (bf16[3,8,256]{2,1,0:T(8,128)(2,1)S(1)}, bf16[3,8,256]{2,1,0:T(8,128)(2,1)S(1)}, u32[]{:S(2)}, u32[]{:S(2)}) collective-permute-start(bf16[3,8,256]{2,1,0:T(8,128)(2,1)S(1)} %get-tuple-element.19), channel_id=1, source_target_pairs={{12,24},{24,0},{36,12},{48,36},{60,72},{72,48},{84,60},{96,84},{10... | collective-permute-start | bytes 36872 | tf_op jit(solution)/shard_map/ppermute | solution.py:33
  127.6 3.1 %collective-permute-start.9 = (bf16[3,8,256]{2,1,0:T(8,128)(2,1)S(1)}, bf16[3,8,256]{2,1,0:T(8,128)(2,1)S(1)}, u32[]{:S(2)}, u32[]{:S(2)}) collective-permute-start(bf16[3,8,256]{2,1,0:T(8,128)(2,1)S(1)} %get-tuple-element.18), channel_id=1, source_target_pairs={{0,24},{12,36},{24,12},{36,48},{48,72},{60,84},{72,60},{84,96},{96... | collective-permute-start | bytes 36872 | tf_op jit(solution)/shard_map/ppermute | solution.py:33
  131.5 5.1 %mix.1 = (bf16[288,256]{1,0:T(8,128)(2,1)S(1)}, f32[96,4096]{1,0:T(8,128)S(1)}, bf16[96,4096]{1,0:T(8,128)(2,1)S(1)}, bf16[96,4096]{1,0:T(8,128)(2,1)S(1)}) custom-call(s32[1]{0:T(128)} %bitcast.lane_ref, bf16[3,96,256]{2,1,0:T(8,128)(2,1)S(1)} %project_own.1.own_ref, bf16[3,192,256]{2,1,0:T(8,128)(2,1)S(1)} %get-tuple-element.17.rest_ref, ...), custom_call_target="tpu_custom_call" | custom-call | tf_op jit(solution)/shard_map/mix/pallas_call | solution.py:247
  138.8 4.3 %collective-permute-start.12 = (bf16[96,4096]{1,0:T(8,128)(2,1)S(1)}, bf16[96,4096]{1,0:T(8,128)(2,1)S(1)}, u32[]{:S(2)}, u32[]{:S(2)}) collective-permute-start(bf16[96,4096]{1,0:T(8,128)(2,1)S(1)} %get-tuple-element.26), channel_id=1, source_target_pairs={{0,11},{1,0},{2,1},{3,2},{4,3},{5,4},{6,5},{7,6},{8,7},{9,8},{10,9... | collective-permute-start | bytes 2359304 | tf_op jit(solution)/shard_map/ppermute | solution.py:285
  143.2 15.7 %collective-permute-done.11 = bf16[96,4096]{1,0:T(8,128)(2,1)S(1)} collective-permute-done((bf16[96,4096]{1,0:T(8,128)(2,1)S(1)}, bf16[96,4096]{1,0:T(8,128)(2,1)S(1)}, u32[]{:S(2)}, u32[]{:S(2)}) %collective-permute-start.11) | collective-permute-done | bytes 786464 | tf_op jit(solution)/shard_map/ppermute | solution.py:285
  161.6 3.7 %collective-permute-start.13 = (bf16[288,128]{1,0:T(8,128)(2,1)S(1)}, bf16[288,128]{1,0:T(8,128)(2,1)S(1)}, u32[]{:S(2)}, u32[]{:S(2)}) collective-permute-start(bf16[288,128]{1,0:T(8,128)(2,1)S(1)} %get-tuple-element.30), channel_id=1, source_target_pairs={{0,0},{12,24},{24,12},{36,36},{1,1},{13,25},{25,13},{37,37},{2,2},... | collective-permute-start | bytes 221192 | tf_op jit(solution)/shard_map/ppermute | solution.py:33
  167.3 3.1 %collective-permute-done.14 = bf16[288,128]{1,0:T(8,128)(2,1)S(1)} collective-permute-done((bf16[288,128]{1,0:T(8,128)(2,1)S(1)}, bf16[288,128]{1,0:T(8,128)(2,1)S(1)}, u32[]{:S(2)}, u32[]{:S(2)}) %collective-permute-start.14) | collective-permute-done | bytes 73760 | tf_op jit(solution)/shard_map/ppermute | solution.py:33
  171.1 32.0 %reduce-scatter.2.cloned.1.call-done = bf16[24,4096]{1,0:T(8,128)(2,1)} async-done(((bf16[96,4096]{1,0:T(8,128)(2,1)}), bf16[24,4096]{1,0:T(8,128)(2,1)}) %reduce-scatter.2.cloned.1.call-update) | async-done | bytes 196624 | tf_op jit(solution)/shard_map/reduce_scatter | solution.py:346
  203.1 4.7 %collective-permute-start.15 = (bf16[24,4096]{1,0:T(8,128)(2,1)}, bf16[24,4096]{1,0:T(8,128)(2,1)S(1)}, u32[]{:S(2)}, u32[]{:S(2)}) collective-permute-start(bf16[24,4096]{1,0:T(8,128)(2,1)} %reduce-scatter.2.cloned.1.call-done), channel_id=1, source_target_pairs={{0,0},{12,24},{24,12},{36,36},{1,1},{13,25},{25,13},{37,37},{2,2},... | collective-permute-start | bytes 589832 | tf_op jit(solution)/shard_map/ppermute | solution.py:33
  207.8 3.5 %collective-permute-done.15 = bf16[24,4096]{1,0:T(8,128)(2,1)S(1)} collective-permute-done((bf16[24,4096]{1,0:T(8,128)(2,1)}, bf16[24,4096]{1,0:T(8,128)(2,1)S(1)}, u32[]{:S(2)}, u32[]{:S(2)}) %collective-permute-start.15) | collective-permute-done | bytes 196640 | tf_op jit(solution)/shard_map/ppermute | solution.py:33
  (43 shorter events, 19.0 us)
Async XLA Ops:
  7.2 86.9 %all-gather.3.cloned.1.call-start = ((), (), s32[]{:S(2)}) async-start(), calls=%async_computation.2 | async-start | bytes 1310720 | tf_op jit(solution)/shard_map/all_gather | solution.py:296
  7.2 6.8 %copy-start.3 = (bf16[24,4096]{1,0:T(8,128)(2,1)S(1)}, bf16[24,4096]{1,0:T(8,128)(2,1)}, u32[]{:S(2)}) copy-start(bf16[24,4096]{1,0:T(8,128)(2,1)} %param.5) | copy-start | bytes 589828
  7.2 38.1 %copy-start = (bf16[576,128]{1,0:T(8,128)(2,1)S(1)}, bf16[576,128]{1,0:T(8,128)(2,1)}, u32[]{:S(2)}) copy-start(bf16[576,128]{1,0:T(8,128)(2,1)} %param.9) | copy-start | bytes 442372
  7.2 41.9 %copy-start.2 = (f32[3,3,128]{2,1,0:T(4,128)S(1)}, f32[3,3,128]{2,1,0:T(4,128)}, u32[]{:S(2)}) copy-start(f32[3,3,128]{2,1,0:T(4,128)} %param.7) | copy-start | bytes 13828
  7.2 42.0 %copy-start.1 = (f32[7,128]{1,0:T(8,128)S(1)}, f32[7,128]{1,0:T(8,128)}, u32[]{:S(2)}) copy-start(f32[7,128]{1,0:T(8,128)} %param.8) | copy-start | bytes 10756
  10.0 48.0 %collective-permute-start.1 = (bf16[3,2048,128]{2,1,0:T(8,128)(2,1)}, bf16[3,2048,128]{2,1,0:T(8,128)(2,1)S(1)}, u32[]{:S(2)}, u32[]{:S(2)}) collective-permute-start(bf16[3,2048,128]{2,1,0:T(8,128)(2,1)} %dynamic-slice_bitcast_fusion), channel_id=1, source_target_pairs={{0,588},{12,0},{24,36},{36,216},{192,12},{204,192},{216,228},{228,... | collective-permute-start | bytes 4718600 | tf_op jit(solution)/shard_map/ppermute | solution.py:33
  14.1 30.4 %collective-permute-start = (bf16[24,4096]{1,0:T(8,128)(2,1)S(1)}, bf16[24,4096]{1,0:T(8,128)(2,1)S(1)}, u32[]{:S(2)}, u32[]{:S(2)}) collective-permute-start(bf16[24,4096]{1,0:T(8,128)(2,1)S(1)} %copy-done.3), channel_id=1, source_target_pairs={{0,0},{12,24},{24,12},{36,36},{1,1},{13,25},{25,13},{37,37},{2,2},... | collective-permute-start | bytes 589832 | tf_op jit(solution)/shard_map/ppermute | solution.py:33
  45.2 157.9 %reduce-scatter.2.cloned.1.call-start = ((), (), s32[]{:S(2)}) async-start(), calls=%async_computation.1 | async-start | bytes 983040 | tf_op jit(solution)/shard_map/reduce_scatter | solution.py:346
  45.3 7.7 %collective-permute-start.2 = (bf16[288,128]{1,0:T(8,128)(2,1)S(1)}, bf16[288,128]{1,0:T(8,128)(2,1)S(1)}, u32[]{:S(2)}, u32[]{:S(2)}) collective-permute-start(bf16[288,128]{1,0:T(8,128)(2,1)S(1)} %get-tuple-element.32), channel_id=1, source_target_pairs={{0,0},{12,24},{24,12},{36,36},{1,1},{13,25},{25,13},{37,37},{2,2},... | collective-permute-start | bytes 221192 | tf_op jit(solution)/shard_map/ppermute | solution.py:33
  47.2 5.8 %collective-permute-start.3 = (bf16[288,128]{1,0:T(8,128)(2,1)S(1)}, bf16[288,128]{1,0:T(8,128)(2,1)S(1)}, u32[]{:S(2)}, u32[]{:S(2)}) collective-permute-start(bf16[288,128]{1,0:T(8,128)(2,1)S(1)} %get-tuple-element.33), channel_id=1, source_target_pairs={{0,24},{12,0},{24,36},{36,12},{1,25},{13,1},{25,37},{37,13},{2,26}... | collective-permute-start | bytes 221192 | tf_op jit(solution)/shard_map/ppermute | solution.py:33
  49.2 6.4 %collective-permute-start.5 = (f32[16,128]{1,0:T(8,128)S(1)}, f32[16,128]{1,0:T(8,128)S(1)}, u32[]{:S(2)}, u32[]{:S(2)}) collective-permute-start(f32[16,128]{1,0:T(8,128)S(1)} %pad_maximum_fusion.1), channel_id=1, source_target_pairs={{0,12},{12,0},{1,13},{13,1},{2,14},{14,2},{3,15},{15,3},{4,16},{16... | collective-permute-start | bytes 24584 | tf_op jit(solution)/shard_map/ppermute | solution.py:317
  53.1 4.9 %collective-permute-start.4 = (bf16[8,256]{1,0:T(8,128)(2,1)S(1)}, bf16[8,256]{1,0:T(8,128)(2,1)S(1)}, u32[]{:S(2)}, u32[]{:S(2)}) collective-permute-start(bf16[8,256]{1,0:T(8,128)(2,1)S(1)} %slice.30), channel_id=1, source_target_pairs={{12,24},{24,0},{36,12},{48,36},{60,72},{72,48},{84,60},{96,84},{10... | collective-permute-start | bytes 12296 | tf_op jit(solution)/shard_map/ppermute | solution.py:33
  58.0 42.7 %collective-permute-start.6 = (bf16[3,2048,128]{2,1,0:T(8,128)(2,1)S(1)}, bf16[3,2048,128]{2,1,0:T(8,128)(2,1)}, u32[]{:S(2)}, u32[]{:S(2)}) collective-permute-start(bf16[3,2048,128]{2,1,0:T(8,128)(2,1)S(1)} %collective-permute-done.1.came_ref), channel_id=1, source_target_pairs={{0,24},{24,0},{1,25},{25,1},{2,26},{26,2},{3,27},{27,3},{4,28},{28... | collective-permute-start | bytes 4718600 | tf_op jit(solution)/shard_map/ppermute | solution.py:334
  95.3 20.3 %collective-permute-start.7 = (bf16[96,4096]{1,0:T(8,128)(2,1)S(1)}, bf16[96,4096]{1,0:T(8,128)(2,1)S(1)}, u32[]{:S(2)}, u32[]{:S(2)}) collective-permute-start(bf16[96,4096]{1,0:T(8,128)(2,1)S(1)} %bitcast.9), channel_id=1, source_target_pairs={{0,11},{1,0},{2,1},{3,2},{4,3},{5,4},{6,5},{7,6},{8,7},{9,8},{10,9... | collective-permute-start | bytes 2359304 | tf_op jit(solution)/shard_map/ppermute | solution.py:285
  97.2 21.5 %collective-permute-start.8 = (bf16[96,4096]{1,0:T(8,128)(2,1)S(1)}, bf16[96,4096]{1,0:T(8,128)(2,1)}, u32[]{:S(2)}, u32[]{:S(2)}) collective-permute-start(bf16[96,4096]{1,0:T(8,128)(2,1)S(1)} %bitcast.10), channel_id=1, source_target_pairs={{0,1},{1,2},{2,3},{3,4},{4,5},{5,6},{6,7},{7,8},{8,9},{9,10},{10,1... | collective-permute-start | bytes 2359304 | tf_op jit(solution)/shard_map/ppermute | solution.py:285
  124.0 6.7 %collective-permute-start.10 = (bf16[3,8,256]{2,1,0:T(8,128)(2,1)S(1)}, bf16[3,8,256]{2,1,0:T(8,128)(2,1)S(1)}, u32[]{:S(2)}, u32[]{:S(2)}) collective-permute-start(bf16[3,8,256]{2,1,0:T(8,128)(2,1)S(1)} %get-tuple-element.19), channel_id=1, source_target_pairs={{12,24},{24,0},{36,12},{48,36},{60,72},{72,48},{84,60},{96,84},{10... | collective-permute-start | bytes 36872 | tf_op jit(solution)/shard_map/ppermute | solution.py:33
  127.6 3.9 %collective-permute-start.9 = (bf16[3,8,256]{2,1,0:T(8,128)(2,1)S(1)}, bf16[3,8,256]{2,1,0:T(8,128)(2,1)S(1)}, u32[]{:S(2)}, u32[]{:S(2)}) collective-permute-start(bf16[3,8,256]{2,1,0:T(8,128)(2,1)S(1)} %get-tuple-element.18), channel_id=1, source_target_pairs={{0,24},{12,36},{24,12},{36,48},{48,72},{60,84},{72,60},{84,96},{96... | collective-permute-start | bytes 36872 | tf_op jit(solution)/shard_map/ppermute | solution.py:33
  136.7 22.2 %collective-permute-start.11 = (bf16[96,4096]{1,0:T(8,128)(2,1)S(1)}, bf16[96,4096]{1,0:T(8,128)(2,1)S(1)}, u32[]{:S(2)}, u32[]{:S(2)}) collective-permute-start(bf16[96,4096]{1,0:T(8,128)(2,1)S(1)} %get-tuple-element.25), channel_id=1, source_target_pairs={{0,1},{1,2},{2,3},{3,4},{4,5},{5,6},{6,7},{7,8},{8,9},{9,10},{10,1... | collective-permute-start | bytes 2359304 | tf_op jit(solution)/shard_map/ppermute | solution.py:285
  138.8 21.6 %collective-permute-start.12 = (bf16[96,4096]{1,0:T(8,128)(2,1)S(1)}, bf16[96,4096]{1,0:T(8,128)(2,1)S(1)}, u32[]{:S(2)}, u32[]{:S(2)}) collective-permute-start(bf16[96,4096]{1,0:T(8,128)(2,1)S(1)} %get-tuple-element.26), channel_id=1, source_target_pairs={{0,11},{1,0},{2,1},{3,2},{4,3},{5,4},{6,5},{7,6},{8,7},{9,8},{10,9... | collective-permute-start | bytes 2359304 | tf_op jit(solution)/shard_map/ppermute | solution.py:285
  161.6 5.7 %collective-permute-start.13 = (bf16[288,128]{1,0:T(8,128)(2,1)S(1)}, bf16[288,128]{1,0:T(8,128)(2,1)S(1)}, u32[]{:S(2)}, u32[]{:S(2)}) collective-permute-start(bf16[288,128]{1,0:T(8,128)(2,1)S(1)} %get-tuple-element.30), channel_id=1, source_target_pairs={{0,0},{12,24},{24,12},{36,36},{1,1},{13,25},{25,13},{37,37},{2,2},... | collective-permute-start | bytes 221192 | tf_op jit(solution)/shard_map/ppermute | solution.py:33
  165.3 5.1 %collective-permute-start.14 = (bf16[288,128]{1,0:T(8,128)(2,1)S(1)}, bf16[288,128]{1,0:T(8,128)(2,1)S(1)}, u32[]{:S(2)}, u32[]{:S(2)}) collective-permute-start(bf16[288,128]{1,0:T(8,128)(2,1)S(1)} %get-tuple-element.31), channel_id=1, source_target_pairs={{0,12},{12,36},{24,0},{36,24},{1,13},{13,37},{25,1},{37,25},{2,14}... | collective-permute-start | bytes 221192 | tf_op jit(solution)/shard_map/ppermute | solution.py:33
  203.1 8.3 %collective-permute-start.15 = (bf16[24,4096]{1,0:T(8,128)(2,1)}, bf16[24,4096]{1,0:T(8,128)(2,1)S(1)}, u32[]{:S(2)}, u32[]{:S(2)}) collective-permute-start(bf16[24,4096]{1,0:T(8,128)(2,1)} %reduce-scatter.2.cloned.1.call-done), channel_id=1, source_target_pairs={{0,0},{12,24},{24,12},{36,36},{1,1},{13,25},{25,13},{37,37},{2,2},... | collective-permute-start | bytes 589832 | tf_op jit(solution)/shard_map/ppermute | solution.py:33
Sparse Core Ops, SparseCore 0:
  45.4 48.6 all-gather.2
  161.7 41.3 reduce-scatter.1

commit v4 on v2

v4 whole, which is shorter than its diff:
```python
import jax
import jax.numpy as jnp
from jax import lax
from jax.experimental import pallas as pl
from jax.experimental.pallas import tpu as pltpu
from jax.sharding import Mesh
from jax.sharding import PartitionSpec as P

CTX = ("yh", "x", "c")
TP = ("yl", "z")
HALO = 8
TOP = 13.0


def exchange(value, axes, sizes, route):
    total = 1
    for size in sizes:
        total *= size
    pairs = []
    for source in range(total):
        coords, rest = [], source
        for size in reversed(sizes):
            coords.append(rest % size)
            rest //= size
        target = route(*reversed(coords))
        if target is None:
            continue
        flat = 0
        for place, size in zip(target, sizes):
            flat = flat * size + place
        pairs.append((source, flat))
    return lax.ppermute(value, axes, pairs)


def swap_homes(value):
    return exchange(value, ("c", "yl"), (2, 2), lambda c, yl: (yl, c))


def vmem():
    return pl.BlockSpec(memory_space=pltpu.MemorySpace.VMEM)


def smem():
    return pl.BlockSpec(memory_space=pltpu.MemorySpace.SMEM)


def hbm():
    return pl.BlockSpec(memory_space=pltpu.MemorySpace.HBM)


PARAMS = pltpu.CompilerParams(vmem_limit_bytes=48 * 1024 * 1024)


def slots(upper_ref, lanes):
    upper = upper_ref[0]
    return pl.multiple_of(upper * lanes, lanes), pl.multiple_of((1 - upper) * lanes, lanes)


def project_kernel(upper_ref, x_ref, grad_ref, mine_ref, low_ref, high_ref, o_ref, head_ref, tail_ref, w_buf, sems):
    parts, depth, lanes = mine_ref.shape
    half = depth // 2
    own, other = slots(upper_ref, lanes)
    copies = []
    for j in range(parts):
        moves = (
            (mine_ref.at[j], w_buf.at[j, :, pl.ds(own, lanes)]),
            (low_ref.at[j], w_buf.at[j, pl.ds(0, half), pl.ds(other, lanes)]),
            (high_ref.at[j], w_buf.at[j, pl.ds(half, half), pl.ds(other, lanes)]),
        )
        copies.append(
            [pltpu.make_async_copy(src, dst, sems.at[j, k]) for k, (src, dst) in enumerate(moves)]
        )
        for copy in copies[-1]:
            copy.start()
    rows = x_ref[:, :depth]
    scale = jnp.exp2(x_ref[:, depth : depth + 1].astype(jnp.float32) - TOP)
    count = rows.shape[0]
    for j in range(parts):
        for copy in copies[j]:
            copy.wait()
        total = jnp.dot(rows, w_buf[j], preferred_element_type=jnp.float32) * scale
        o_ref[j] = total.astype(o_ref.dtype)
        head_ref[j] = total[:HALO].astype(head_ref.dtype)
        tail_ref[j] = total[count - HALO :].astype(tail_ref.dtype)
    head_ref[parts] = grad_ref[:HALO]


def project(upper, rows, grad, mine, low, high):
    parts, depth, lanes = mine.shape
    count = rows.shape[0]
    return pl.pallas_call(
        project_kernel,
        in_specs=[smem(), vmem(), vmem(), hbm(), hbm(), hbm()],
        out_specs=[vmem()] * 3,
        out_shape=[
            jax.ShapeDtypeStruct((parts, count, 2 * lanes), jnp.bfloat16),
            jax.ShapeDtypeStruct((parts + 1, HALO, 2 * lanes), jnp.bfloat16),
            jax.ShapeDtypeStruct((parts, HALO, 2 * lanes), jnp.bfloat16),
        ],
        scratch_shapes=[
            pltpu.VMEM((parts, depth, 2 * lanes), mine.dtype),
            pltpu.SemaphoreType.DMA((parts, 3)),
        ],
        compiler_params=PARAMS,
        name="project",
    )(upper, rows, grad, mine, low, high)


def causal(series, taps):
    total = taps[0:1] * series
    for offset in range(1, taps.shape[0]):
        total = total + taps[offset : offset + 1] * pltpu.roll(series, offset, 0)
    return total


def adjoint(series, taps):
    total = taps[0:1] * series
    for offset in range(1, taps.shape[0]):
        total = total + taps[offset : offset + 1] * pltpu.roll(series, series.shape[0] - offset, 0)
    return total


def mix_kernel(
    upper_ref, proj_ref, prev_ref, next_ref, feat_ref, inner_ref, grad_ref, mine_ref, low_ref, high_ref,
    gated_ref, o_ref, w_buf, back, sems,
):
    parts, depth, lanes = mine_ref.shape
    count = grad_ref.shape[0]
    last = HALO + count
    steps = sems.shape[0]
    block = depth // steps
    own, other = slots(upper_ref, lanes)
    copies = []
    for i in range(steps):
        begin = i * block
        source, shift = (low_ref, begin) if begin < depth // 2 else (high_ref, begin - depth // 2)
        copies.append(
            (
                pltpu.make_async_copy(
                    mine_ref.at[:, pl.ds(begin, block), :],
                    w_buf.at[:, pl.ds(begin, block), pl.ds(own, lanes)],
                    sems.at[i, 0],
                ),
                pltpu.make_async_copy(
                    source.at[:, pl.ds(shift, block), :],
                    w_buf.at[:, pl.ds(begin, block), pl.ds(other, lanes)],
                    sems.at[i, 1],
                ),
            )
        )
        for copy in copies[-1]:
            copy.start()
    for side in range(2):
        cut = slice(side * lanes, (side + 1) * lanes)

        def window(part):
            rows = [prev_ref[part, :, cut], proj_ref[part, :, cut], next_ref[part, :, cut]]
            return jnp.concatenate(rows, axis=0).astype(jnp.float32)

        inner_taps = inner_ref[:, cut]
        feat = [feat_ref[part][:, cut] for part in range(parts)]
        query = causal(window(0), feat[0])
        key = causal(window(1), feat[1])
        value = causal(window(2), feat[2])
        inner = causal(key * value, inner_taps)
        gated_ref[:, cut] = (query * inner)[HALO:last].astype(gated_ref.dtype)
        grad_next = next_ref[parts, :, cut]
        grad = jnp.concatenate([jnp.zeros_like(grad_next), grad_ref[:, cut], grad_next], axis=0)
        grad = grad.astype(jnp.float32)
        mixed = adjoint(grad * query, inner_taps)
        back[0, :, cut] = adjoint(grad * inner, feat[0])[HALO:last].astype(back.dtype)
        back[1, :, cut] = adjoint(mixed * value, feat[1])[HALO:last].astype(back.dtype)
        back[2, :, cut] = adjoint(mixed * key, feat[2])[HALO:last].astype(back.dtype)
    contract = (((1,), (1,)), ((), ()))
    for i in range(steps):
        for copy in copies[i]:
            copy.wait()
        cut = slice(i * block, (i + 1) * block)
        total = lax.dot_general(back[0], w_buf[0, cut], contract, preferred_element_type=jnp.float32)
        for part in range(1, parts):
            total = total + lax.dot_general(
                back[part], w_buf[part, cut], contract, preferred_element_type=jnp.float32
            )
        o_ref[:, cut] = total.astype(o_ref.dtype)


def mix(upper, proj, prev, following, feat, inner, grad, mine, low, high):
    parts, depth, lanes = mine.shape
    count = grad.shape[0]
    steps = 8
    return pl.pallas_call(
        mix_kernel,
        in_specs=[smem()] + [vmem()] * 6 + [hbm()] * 3,
        out_specs=[vmem(), vmem()],
        out_shape=[
            jax.ShapeDtypeStruct((count, 2 * lanes), jnp.bfloat16),
            jax.ShapeDtypeStruct((count, depth), jnp.bfloat16),
        ],
        scratch_shapes=[
            pltpu.VMEM((parts, depth, 2 * lanes), mine.dtype),
            pltpu.VMEM((parts, count, 2 * lanes), jnp.bfloat16),
            pltpu.SemaphoreType.DMA((steps, 2)),
        ],
        compiler_params=PARAMS,
        name="mix",
    )(upper, proj, prev, following, feat, inner, grad, mine, low, high)


def encode(tokens):
    wide = tokens.astype(jnp.float32)
    peak = jnp.max(jnp.abs(wide), axis=1, keepdims=True)
    power = jnp.clip(jnp.floor(jnp.log2(jnp.maximum(peak, 1e-37))), -110.0, 110.0)
    scaled = wide * jnp.exp2(TOP - power)
    return jnp.concatenate(
        [scaled, jnp.broadcast_to(power, (tokens.shape[0], 128))], axis=1
    ).astype(jnp.float16)


def build(sizes):
    ring = sizes[0] * 2

    strips = sizes[0] * sizes[1] * 4

    def along(value, step):
        def route(yh, x, c, yl):
            strip = ((yh * sizes[1] + x) * 2 + yl) * 2 + c + step
            if not 0 <= strip < strips:
                return None
            return (strip // 4 // sizes[1], strip // 4 % sizes[1], strip % 2, strip // 2 % 2)

        return exchange(value, ("yh", "x", "c", "yl"), (sizes[0], sizes[1], 2, 2), route)

    def local(tokens, proj_weight, feat_taps, inner_taps, grad_out):
        upper = lax.axis_index("yl")
        core = lax.axis_index("c")
        width = proj_weight.shape[0]
        channels = inner_taps.shape[1]
        flag = upper.astype(jnp.int32).reshape(1)

        planes = proj_weight.transpose(1, 0, 2)
        half = width // 2
        low, high = planes[:, :half], planes[:, half:]
        count = grad_out.shape[0] // 2
        near = lax.dynamic_slice_in_dim(grad_out, upper * count, count, 0)
        far = lax.dynamic_slice_in_dim(grad_out, (1 - upper) * count, count, 0)
        taps = jnp.concatenate([feat_taps.reshape(9, channels), inner_taps], axis=0)

        rehomed = swap_homes(encode(tokens))
        rehomed, low, high, near, far, sent_taps = lax.optimization_barrier(
            (rehomed, low, high, near, far, taps)
        )

        def beside(step):
            def route(yh, yl):
                place = (yh * 2 + yl + step) % ring
                return (place // 2, place % 2)

            return route

        low = exchange(low, ("yh", "yl"), (sizes[0], 2), beside(-1))
        high = exchange(high, ("yh", "yl"), (sizes[0], 2), beside(1))

        def both(mine, theirs, axis):
            return jnp.where(
                upper == 0,
                jnp.concatenate([mine, theirs], axis=axis),
                jnp.concatenate([theirs, mine], axis=axis),
            )

        near = swap_homes(near)
        far = exchange(far, ("c", "yl"), (2, 2), lambda c, yl: (1 - yl, c))
        came_taps = lax.ppermute(sent_taps, "yl", [(0, 1), (1, 0)])
        rehomed, near, far, came_taps = lax.optimization_barrier((rehomed, near, far, came_taps))
        gathered = lax.all_gather(rehomed, "z", axis=0, tiled=True).astype(jnp.bfloat16)
        taps = both(taps, came_taps, 1)
        feat = taps[:9].reshape(3, 3, 2 * channels)
        inner = taps[9:]
        grad = jnp.where(
            core == 0,
            jnp.concatenate([near, far], axis=1),
            jnp.concatenate([far, near], axis=1),
        )

        proj, head, tail = project(flag, gathered, grad, planes, low, high)
        prev = along(tail, 1)
        following = along(head, -1)
        gated, spread = mix(flag, proj, prev, following, feat, inner, grad, planes, low, high)
        grad_tokens = lax.psum_scatter(spread, "z", scatter_dimension=0, tiled=True)

        first, second = gated[:, :channels], gated[:, channels:]
        near = swap_homes(jnp.where(core == 0, first, second))
        far = exchange(
            jnp.where(core == 0, second, first), ("c", "yl"), (2, 2), lambda c, yl: (yl, 1 - c)
        )
        gated = jnp.where(
            upper == 0,
            jnp.concatenate([near, far], axis=0),
            jnp.concatenate([far, near], axis=0),
        )
        grad_tokens, gated = lax.optimization_barrier((grad_tokens, gated))
        return (gated, swap_homes(grad_tokens))

    return local


def solution(mesh):
    sizes = (4, 4, 2, 2, 12)
    grid = Mesh(mesh.devices.reshape(sizes), CTX + TP)
    in_specs = (
        P(CTX + TP, None),
        P(None, None, TP),
        P(None, None, TP),
        P(None, TP),
        P(CTX, TP),
    )
    out_specs = (P(CTX, TP), P(CTX + TP, None))
    return jax.shard_map(build(sizes), mesh=grid, in_specs=in_specs, out_specs=out_specs, check_vma=False)
```

time: 187 us -> 205 us (1.096)
  blocking collectives: 0 us -> 45.8 us
  waiting for transfers between devices: 95 us -> 69.5 us
  other arithmetic: 10.2 us -> 4.22 us
  Pallas kernels: 7.97 us -> 11.7 us
    all_gather x0 -> x1, blocking collectives: none -> 45.8 us  [local(): lax.all_gather(rehomed, 'z', axis=0, tiled=True).astype(jnp.bfloat16)]
    ppermute x10, waiting for transfers between devices: 30.2 us -> 11.3 us  [exchange(): return lax.ppermute(value, axes, pairs)]
    ppermute x3 -> x1, waiting for transfers between devices: 0.01 us -> 17.7 us  [local(): came_taps = lax.ppermute(sent_taps, 'yl', [(0, 1), (1, 0)])]
    reduce_scatter x1, waiting for transfers between devices: 54.2 us -> 40.5 us  [local(): grad_tokens = lax.psum_scatter(spread, 'z', scatter_dimension=0, tiled=True)]
    all_gather x1 -> x0, waiting for transfers between devices: 10.5 us -> none  [local(): gathered = lax.all_gather(swap_homes(tokens), 'z', axis=0, tiled=True)]
    ppermute x10, starting transfers between devices: 41.8 us -> 50.3 us  [exchange(): return lax.ppermute(value, axes, pairs)]
    ppermute x3 -> x1, starting transfers between devices: 9.84 us -> 2.02 us  [local(): came_taps = lax.ppermute(sent_taps, 'yl', [(0, 1), (1, 0)])]
    select_n x3 -> x1, other arithmetic: 4.57 us -> 0.01 us  [both(): jnp.where(upper == 0, jnp.concatenate([mine, theirs], axis=axis), jnp.con...]
  transfers between devices with their start and end apart: 15 -> 12, of which waited for: 7 -> 7; matrix products, arithmetic and copies ran while one was open for 6% -> 3% of each run, Pallas kernels for 1% -> 0%
where the time goes in v4:
time: 205 us; the launch traced here: 204 us
  waiting for transfers between devices  69.5 us (34%)
  starting transfers between devices  52.4 us (26%)
  blocking collectives  45.8 us (22%)
  between operations  14.3 us (7%)
  Pallas kernels  11.7 us (6%)
  local copies, waits for them, and re-layouts  6.36 us (3%)
  other arithmetic  4.22 us (2%)
    ppermute x10, starting transfers between devices, exchange(): return lax.ppermute(value, axes, pairs)  50.3 us
    all_gather x1, blocking collectives, local(): lax.all_gather(rehomed, 'z', axis=0, tiled=True).astype(jnp.bfloat16)  45.8 us
    reduce_scatter x1, waiting for transfers between devices, local(): grad_tokens = lax.psum_scatter(spread, 'z', scatter_dimension=0, tiled=True)  40.5 us
    ppermute x1, waiting for transfers between devices, local(): came_taps = lax.ppermute(sent_taps, 'yl', [(0, 1), (1, 0)])  17.7 us
    ppermute x10, waiting for transfers between devices, exchange(): return lax.ppermute(value, axes, pairs)  11.3 us
    pallas_call x1, Pallas kernels, mix(): pl.pallas_call(mix_kernel, in_specs=[smem()] + [vmem()] * 6 + [hbm()] * 3...  6.89 us
    pallas_call x1, Pallas kernels, project(): pl.pallas_call(project_kernel, in_specs=[smem(), vmem(), vmem(), hbm(), h...  4.83 us
  transfers between devices with their start and end apart: 12, of which 7 were waited for; matrix products, arithmetic and copies ran while one was open for 3% of the time, Pallas kernels for 0%

profile of v4, /device:TPU:1, one launch (start us, length us, event | category | flops | bytes accessed | tf_op | source)
XLA Modules:
  0.0 204.2 jit_solution(13409716145742198344)
XLA Ops:
  7.2 1.1 fusion
  8.3 1.1 fusion.1
  9.5 4.6 %collective-permute-start = (f16[24,4224]{1,0:T(8,128)(2,1)S(1)}, f16[24,4224]{1,0:T(8,128)(2,1)S(1)}, u32[]{:S(2)}, u32[]{:S(2)}) collective-permute-start(f16[24,4224]{1,0:T(8,128)(2,1)S(1)} %pad_maximum_fusion), channel_id=1, source_target_pairs={{0,0},{12,24},{24,12},{36,36},{1,1},{13,25},{25,13},{37,37},{2,2},... | collective-permute-start | bytes 608264 | tf_op jit(solution)/shard_map/ppermute | solution.py:32
  14.1 3.8 %fusion.3 = (bf16[3,2048,128]{2,1,0:T(8,128)(2,1)}, bf16[3,2048,128]{2,1,0:T(8,128)(2,1)}) fusion(bf16[3,4096,128]{2,1,0:T(8,128)(2,1)} %bitcast.3), kind=kLoop, calls=%fused_computation.16 | loop fusion | bytes 6291456 | tf_op jit(solution)/shard_map/slice | solution.py:242
  18.0 2.0 collective-permute-start.4
  20.0 3.3 %collective-permute-start.5 = (bf16[3,2048,128]{2,1,0:T(8,128)(2,1)}, bf16[3,2048,128]{2,1,0:T(8,128)(2,1)S(1)}, u32[]{:S(2)}, u32[]{:S(2)}) collective-permute-start(bf16[3,2048,128]{2,1,0:T(8,128)(2,1)} %get-tuple-element.27), channel_id=1, source_target_pairs={{0,12},{12,192},{192,204},{204,384},{384,396},{396,576},{576,588},... | collective-permute-start | bytes 4718600 | tf_op jit(solution)/shard_map/ppermute | solution.py:32
  23.3 8.7 %collective-permute-start.1 = (bf16[288,128]{1,0:T(8,128)(2,1)S(1)}, bf16[288,128]{1,0:T(8,128)(2,1)}, u32[]{:S(2)}, u32[]{:S(2)}) collective-permute-start(bf16[288,128]{1,0:T(8,128)(2,1)S(1)} %get-tuple-element.20), channel_id=1, source_target_pairs={{0,0},{12,24},{24,12},{36,36},{1,1},{13,25},{25,13},{37,37},{2,2},... | collective-permute-start | bytes 221192 | tf_op jit(solution)/shard_map/ppermute | solution.py:32
  32.0 1.9 collective-permute-start.2
  33.9 2.0 collective-permute-start.3
  35.9 17.7 %collective-permute-done.3 = f32[16,128]{1,0:T(8,128)S(1)} collective-permute-done((f32[16,128]{1,0:T(8,128)S(1)}, f32[16,128]{1,0:T(8,128)S(1)}, u32[]{:S(2)}, u32[]{:S(2)}) %collective-permute-start.3) | collective-permute-done | bytes 8224 | tf_op jit(solution)/shard_map/ppermute | solution.py:272
  53.6 3.8 %collective-permute-done.1 = bf16[288,128]{1,0:T(8,128)(2,1)} collective-permute-done((bf16[288,128]{1,0:T(8,128)(2,1)S(1)}, bf16[288,128]{1,0:T(8,128)(2,1)}, u32[]{:S(2)}, u32[]{:S(2)}) %collective-permute-start.1) | collective-permute-done | bytes 73760 | tf_op jit(solution)/shard_map/ppermute | solution.py:32
  57.4 45.8 %all-gather.1 = f16[288,4224]{1,0:T(8,128)(2,1)S(1)} all-gather(f16[24,4224]{1,0:T(8,128)(2,1)S(1)} %collective-permute-done), channel_id=1, replica_groups=mesh['yh'=4,'x'=4,'c'=2,'yl'=2,'z'=12] {'z'}, dimensions={0}, use_global_device_ids=true | all-gather | bytes 2635776 | tf_op jit(solution)/shard_map/all_gather | solution.py:274
  103.4 1.0 maximum_select_fusion.grad_ref
  104.5 4.8 %project.1 = (bf16[3,288,256]{2,1,0:T(8,128)(2,1)S(1)}, bf16[4,8,256]{2,1,0:T(8,128)(2,1)S(1)}, bf16[3,8,256]{2,1,0:T(8,128)(2,1)S(1)}) custom-call(s32[1]{0:T(128)} %bitcast.upper_ref, bf16[288,4224]{1,0:T(8,128)(2,1)S(1)} %convert_element_type.8.x_ref, bf16[288,256]{1,0:T(8,128)(2,1)S(1)} %maximum_select_fusion.grad_ref, bf16[3,4096,128]{2,1,0:T(8,128)(2,1)} %bitcast.4, ...), custom_call_target="tpu_custom_call" | custom-call | tf_op jit(solution)/shard_map/project/pallas_call | solution.py:91
  110.1 8.1 %collective-permute-start.7 = (bf16[4,8,256]{2,1,0:T(8,128)(2,1)S(1)}, bf16[4,8,256]{2,1,0:T(8,128)(2,1)S(1)}, u32[]{:S(2)}, u32[]{:S(2)}) collective-permute-start(bf16[4,8,256]{2,1,0:T(8,128)(2,1)S(1)} %get-tuple-element.30), channel_id=1, source_target_pairs={{12,24},{24,0},{36,12},{48,36},{60,72},{72,48},{84,60},{96,84},{10... | collective-permute-start | bytes 49160 | tf_op jit(solution)/shard_map/ppermute | solution.py:32
  118.2 4.9 %collective-permute-start.6 = (bf16[3,8,256]{2,1,0:T(8,128)(2,1)S(1)}, bf16[3,8,256]{2,1,0:T(8,128)(2,1)S(1)}, u32[]{:S(2)}, u32[]{:S(2)}) collective-permute-start(bf16[3,8,256]{2,1,0:T(8,128)(2,1)S(1)} %get-tuple-element.29), channel_id=1, source_target_pairs={{0,24},{12,36},{24,12},{36,48},{48,72},{60,84},{72,60},{84,96},{96... | collective-permute-start | bytes 36872 | tf_op jit(solution)/shard_map/ppermute | solution.py:32
  123.9 1.0 copy-done.1
  124.9 6.9 %mix.1 = (bf16[288,256]{1,0:T(8,128)(2,1)S(1)}, bf16[288,4096]{1,0:T(8,128)(2,1)}) custom-call(s32[1]{0:T(128)} %bitcast.upper_ref, bf16[3,288,256]{2,1,0:T(8,128)(2,1)S(1)} %copy-done.1, bf16[3,8,256]{2,1,0:T(8,128)(2,1)S(1)} %collective-permute-done.6.prev_ref, bf16[4,8,256]{2,1,0:T(8,128)(2,1)S(1)} %collective-permute-done.7.next_ref, ...), custom_call_target="tpu_custom_call" | custom-call | tf_op jit(solution)/shard_map/mix/pallas_call | solution.py:191
  131.9 4.2 %collective-permute-start.8 = (bf16[288,128]{1,0:T(8,128)(2,1)S(1)}, bf16[288,128]{1,0:T(8,128)(2,1)S(1)}, u32[]{:S(2)}, u32[]{:S(2)}) collective-permute-start(bf16[288,128]{1,0:T(8,128)(2,1)S(1)} %get-tuple-element.38), channel_id=1, source_target_pairs={{0,0},{12,24},{24,12},{36,36},{1,1},{13,25},{25,13},{37,37},{2,2},... | collective-permute-start | bytes 221192 | tf_op jit(solution)/shard_map/ppermute | solution.py:32
  136.1 1.9 collective-permute-start.9
  138.1 3.1 %collective-permute-done.9 = bf16[288,128]{1,0:T(8,128)(2,1)S(1)} collective-permute-done((bf16[288,128]{1,0:T(8,128)(2,1)S(1)}, bf16[288,128]{1,0:T(8,128)(2,1)S(1)}, u32[]{:S(2)}, u32[]{:S(2)}) %collective-permute-start.9) | collective-permute-done | bytes 73760 | tf_op jit(solution)/shard_map/ppermute | solution.py:32
  141.9 40.5 %reduce-scatter.2.cloned.1.call-done = bf16[24,4096]{1,0:T(8,128)(2,1)} async-done(((bf16[288,4096]{1,0:T(8,128)(2,1)}), bf16[24,4096]{1,0:T(8,128)(2,1)}) %reduce-scatter.2.cloned.1.call-update) | async-done | bytes 196624 | tf_op jit(solution)/shard_map/reduce_scatter | solution.py:288
  182.4 10.7 %collective-permute-start.10 = (bf16[24,4096]{1,0:T(8,128)(2,1)}, bf16[24,4096]{1,0:T(8,128)(2,1)S(1)}, u32[]{:S(2)}, u32[]{:S(2)}) collective-permute-start(bf16[24,4096]{1,0:T(8,128)(2,1)} %reduce-scatter.2.cloned.1.call-done), channel_id=1, source_target_pairs={{0,0},{12,24},{24,12},{36,36},{1,1},{13,25},{25,13},{37,37},{2,2},... | collective-permute-start | bytes 589832 | tf_op jit(solution)/shard_map/ppermute | solution.py:32
  193.1 3.5 %collective-permute-done.10 = bf16[24,4096]{1,0:T(8,128)(2,1)S(1)} collective-permute-done((bf16[24,4096]{1,0:T(8,128)(2,1)}, bf16[24,4096]{1,0:T(8,128)(2,1)S(1)}, u32[]{:S(2)}, u32[]{:S(2)}) %collective-permute-start.10) | collective-permute-done | bytes 196640 | tf_op jit(solution)/shard_map/ppermute | solution.py:32
  (31 shorter events, 3.6 us)
Async XLA Ops:
  7.2 175.2 %reduce-scatter.2.cloned.1.call-start = ((), (), s32[]{:S(2)}) async-start(), calls=%async_computation.1 | async-start | bytes 2555904 | tf_op jit(solution)/shard_map/reduce_scatter | solution.py:288
  9.5 8.5 %collective-permute-start = (f16[24,4224]{1,0:T(8,128)(2,1)S(1)}, f16[24,4224]{1,0:T(8,128)(2,1)S(1)}, u32[]{:S(2)}, u32[]{:S(2)}) collective-permute-start(f16[24,4224]{1,0:T(8,128)(2,1)S(1)} %pad_maximum_fusion), channel_id=1, source_target_pairs={{0,0},{12,24},{24,12},{36,36},{1,1},{13,25},{25,13},{37,37},{2,2},... | collective-permute-start | bytes 608264 | tf_op jit(solution)/shard_map/ppermute | solution.py:32
  14.1 3.8 %copy-start.4 = (f32[3,3,128]{2,1,0:T(4,128)S(1)}, f32[3,3,128]{2,1,0:T(4,128)}, u32[]{:S(2)}) copy-start(f32[3,3,128]{2,1,0:T(4,128)} %param.7) | copy-start | bytes 13828
  14.1 3.8 %copy-start.3 = (f32[7,128]{1,0:T(8,128)S(1)}, f32[7,128]{1,0:T(8,128)}, u32[]{:S(2)}) copy-start(f32[7,128]{1,0:T(8,128)} %param.8) | copy-start | bytes 10756
  14.1 3.8 %copy-start.2 = (bf16[576,128]{1,0:T(8,128)(2,1)S(1)}, bf16[576,128]{1,0:T(8,128)(2,1)}, u32[]{:S(2)}) copy-start(bf16[576,128]{1,0:T(8,128)(2,1)} %param.9) | copy-start | bytes 442372
  18.0 86.5 %collective-permute-start.4 = (bf16[3,2048,128]{2,1,0:T(8,128)(2,1)}, bf16[3,2048,128]{2,1,0:T(8,128)(2,1)S(1)}, u32[]{:S(2)}, u32[]{:S(2)}) collective-permute-start(bf16[3,2048,128]{2,1,0:T(8,128)(2,1)} %get-tuple-element.26), channel_id=1, source_target_pairs={{0,588},{12,0},{192,12},{204,192},{384,204},{396,384},{576,396},{5... | collective-permute-start | bytes 4718600 | tf_op jit(solution)/shard_map/ppermute | solution.py:32
  20.0 84.5 %collective-permute-start.5 = (bf16[3,2048,128]{2,1,0:T(8,128)(2,1)}, bf16[3,2048,128]{2,1,0:T(8,128)(2,1)S(1)}, u32[]{:S(2)}, u32[]{:S(2)}) collective-permute-start(bf16[3,2048,128]{2,1,0:T(8,128)(2,1)} %get-tuple-element.27), channel_id=1, source_target_pairs={{0,12},{12,192},{192,204},{204,384},{384,396},{396,576},{576,588},... | collective-permute-start | bytes 4718600 | tf_op jit(solution)/shard_map/ppermute | solution.py:32
  23.3 34.1 %collective-permute-start.1 = (bf16[288,128]{1,0:T(8,128)(2,1)S(1)}, bf16[288,128]{1,0:T(8,128)(2,1)}, u32[]{:S(2)}, u32[]{:S(2)}) collective-permute-start(bf16[288,128]{1,0:T(8,128)(2,1)S(1)} %get-tuple-element.20), channel_id=1, source_target_pairs={{0,0},{12,24},{24,12},{36,36},{1,1},{13,25},{25,13},{37,37},{2,2},... | collective-permute-start | bytes 221192 | tf_op jit(solution)/shard_map/ppermute | solution.py:32
  32.0 25.4 %collective-permute-start.2 = (bf16[288,128]{1,0:T(8,128)(2,1)S(1)}, bf16[288,128]{1,0:T(8,128)(2,1)}, u32[]{:S(2)}, u32[]{:S(2)}) collective-permute-start(bf16[288,128]{1,0:T(8,128)(2,1)S(1)} %get-tuple-element.21), channel_id=1, source_target_pairs={{0,24},{12,0},{24,36},{36,12},{1,25},{13,1},{25,37},{37,13},{2,26}... | collective-permute-start | bytes 221192 | tf_op jit(solution)/shard_map/ppermute | solution.py:32
  33.9 19.7 %collective-permute-start.3 = (f32[16,128]{1,0:T(8,128)S(1)}, f32[16,128]{1,0:T(8,128)S(1)}, u32[]{:S(2)}, u32[]{:S(2)}) collective-permute-start(f32[16,128]{1,0:T(8,128)S(1)} %pad_maximum_fusion.1), channel_id=1, source_target_pairs={{0,12},{12,0},{1,13},{13,1},{2,14},{14,2},{3,15},{15,3},{4,16},{16... | collective-permute-start | bytes 24584 | tf_op jit(solution)/shard_map/ppermute | solution.py:272
  109.3 0.8 copy-start
  110.1 13.8 %collective-permute-start.7 = (bf16[4,8,256]{2,1,0:T(8,128)(2,1)S(1)}, bf16[4,8,256]{2,1,0:T(8,128)(2,1)S(1)}, u32[]{:S(2)}, u32[]{:S(2)}) collective-permute-start(bf16[4,8,256]{2,1,0:T(8,128)(2,1)S(1)} %get-tuple-element.30), channel_id=1, source_target_pairs={{12,24},{24,0},{36,12},{48,36},{60,72},{72,48},{84,60},{96,84},{10... | collective-permute-start | bytes 49160 | tf_op jit(solution)/shard_map/ppermute | solution.py:32
  118.2 5.7 %collective-permute-start.6 = (bf16[3,8,256]{2,1,0:T(8,128)(2,1)S(1)}, bf16[3,8,256]{2,1,0:T(8,128)(2,1)S(1)}, u32[]{:S(2)}, u32[]{:S(2)}) collective-permute-start(bf16[3,8,256]{2,1,0:T(8,128)(2,1)S(1)} %get-tuple-element.29), channel_id=1, source_target_pairs={{0,24},{12,36},{24,12},{36,48},{48,72},{60,84},{72,60},{84,96},{96... | collective-permute-start | bytes 36872 | tf_op jit(solution)/shard_map/ppermute | solution.py:32
  123.9 1.0 copy-start.1
  131.9 6.2 %collective-permute-start.8 = (bf16[288,128]{1,0:T(8,128)(2,1)S(1)}, bf16[288,128]{1,0:T(8,128)(2,1)S(1)}, u32[]{:S(2)}, u32[]{:S(2)}) collective-permute-start(bf16[288,128]{1,0:T(8,128)(2,1)S(1)} %get-tuple-element.38), channel_id=1, source_target_pairs={{0,0},{12,24},{24,12},{36,36},{1,1},{13,25},{25,13},{37,37},{2,2},... | collective-permute-start | bytes 221192 | tf_op jit(solution)/shard_map/ppermute | solution.py:32
  136.1 5.1 %collective-permute-start.9 = (bf16[288,128]{1,0:T(8,128)(2,1)S(1)}, bf16[288,128]{1,0:T(8,128)(2,1)S(1)}, u32[]{:S(2)}, u32[]{:S(2)}) collective-permute-start(bf16[288,128]{1,0:T(8,128)(2,1)S(1)} %get-tuple-element.39), channel_id=1, source_target_pairs={{0,12},{12,36},{24,0},{36,24},{1,13},{13,37},{25,1},{37,25},{2,14}... | collective-permute-start | bytes 221192 | tf_op jit(solution)/shard_map/ppermute | solution.py:32
  182.4 14.3 %collective-permute-start.10 = (bf16[24,4096]{1,0:T(8,128)(2,1)}, bf16[24,4096]{1,0:T(8,128)(2,1)S(1)}, u32[]{:S(2)}, u32[]{:S(2)}) collective-permute-start(bf16[24,4096]{1,0:T(8,128)(2,1)} %reduce-scatter.2.cloned.1.call-done), channel_id=1, source_target_pairs={{0,0},{12,24},{24,12},{36,36},{1,1},{13,25},{25,13},{37,37},{2,2},... | collective-permute-start | bytes 589832 | tf_op jit(solution)/shard_map/ppermute | solution.py:32
Sparse Core Ops, SparseCore 0:
  131.9 50.3 reduce-scatter.1

commit v5 on v4

--- a/solution.py
+++ b/solution.py
@@ -48,7 +48,7 @@
     return pl.BlockSpec(memory_space=pltpu.MemorySpace.HBM)
 
 
-PARAMS = pltpu.CompilerParams(vmem_limit_bytes=48 * 1024 * 1024)
+PARAMS = pltpu.CompilerParams(vmem_limit_bytes=24 * 1024 * 1024)
 
 
 def slots(upper_ref, lanes):
@@ -56,16 +56,14 @@
     return pl.multiple_of(upper * lanes, lanes), pl.multiple_of((1 - upper) * lanes, lanes)
 
 
-def project_kernel(upper_ref, x_ref, grad_ref, mine_ref, low_ref, high_ref, o_ref, head_ref, tail_ref, w_buf, sems):
+def project_kernel(upper_ref, x_ref, packed_ref, mine_ref, theirs_ref, o_ref, head_ref, tail_ref, w_buf, sems):
     parts, depth, lanes = mine_ref.shape
-    half = depth // 2
     own, other = slots(upper_ref, lanes)
     copies = []
     for j in range(parts):
         moves = (
             (mine_ref.at[j], w_buf.at[j, :, pl.ds(own, lanes)]),
-            (low_ref.at[j], w_buf.at[j, pl.ds(0, half), pl.ds(other, lanes)]),
-            (high_ref.at[j], w_buf.at[j, pl.ds(half, half), pl.ds(other, lanes)]),
+            (theirs_ref.at[j], w_buf.at[j, :, pl.ds(other, lanes)]),
         )
         copies.append(
             [pltpu.make_async_copy(src, dst, sems.at[j, k]) for k, (src, dst) in enumerate(moves)]
@@ -82,15 +80,15 @@
         o_ref[j] = total.astype(o_ref.dtype)
         head_ref[j] = total[:HALO].astype(head_ref.dtype)
         tail_ref[j] = total[count - HALO :].astype(tail_ref.dtype)
-    head_ref[parts] = grad_ref[:HALO]
-
-
-def project(upper, rows, grad, mine, low, high):
+    head_ref[parts] = packed_ref[:HALO].astype(head_ref.dtype)
+
+
+def project(upper, rows, packed, mine, theirs):
     parts, depth, lanes = mine.shape
     count = rows.shape[0]
     return pl.pallas_call(
         project_kernel,
-        in_specs=[smem(), vmem(), vmem(), hbm(), hbm(), hbm()],
+        in_specs=[smem(), vmem(), vmem(), hbm(), hbm()],
         out_specs=[vmem()] * 3,
         out_shape=[
             jax.ShapeDtypeStruct((parts, count, 2 * lanes), jnp.bfloat16),
@@ -99,11 +97,11 @@
         ],
         scratch_shapes=[
             pltpu.VMEM((parts, depth, 2 * lanes), mine.dtype),
-            pltpu.SemaphoreType.DMA((parts, 3)),
+            pltpu.SemaphoreType.DMA((parts, 2)),
         ],
         compiler_params=PARAMS,
         name="project",
-    )(upper, rows, grad, mine, low, high)
+    )(upper, rows, packed, mine, theirs)
 
 
 def causal(series, taps):
@@ -121,11 +119,11 @@
 
 
 def mix_kernel(
-    upper_ref, proj_ref, prev_ref, next_ref, feat_ref, inner_ref, grad_ref, mine_ref, low_ref, high_ref,
-    gated_ref, o_ref, w_buf, back, sems,
+    upper_ref, proj_ref, prev_ref, next_ref, packed_ref, mine_ref, theirs_ref,
+    gated_ref, o_ref, w_buf, back, o_buf, sems,
 ):
     parts, depth, lanes = mine_ref.shape
-    count = grad_ref.shape[0]
+    count = proj_ref.shape[1]
     last = HALO + count
     steps = sems.shape[0]
     block = depth // steps
@@ -133,7 +131,6 @@
     copies = []
     for i in range(steps):
         begin = i * block
-        source, shift = (low_ref, begin) if begin < depth // 2 else (high_ref, begin - depth // 2)
         copies.append(
             (
                 pltpu.make_async_copy(
@@ -142,7 +139,7 @@
                     sems.at[i, 0],
                 ),
                 pltpu.make_async_copy(
-                    source.at[:, pl.ds(shift, block), :],
+                    theirs_ref.at[:, pl.ds(begin, block), :],
                     w_buf.at[:, pl.ds(begin, block), pl.ds(other, lanes)],
                     sems.at[i, 1],
                 ),
@@ -157,21 +154,22 @@
             rows = [prev_ref[part, :, cut], proj_ref[part, :, cut], next_ref[part, :, cut]]
             return jnp.concatenate(rows, axis=0).astype(jnp.float32)
 
-        inner_taps = inner_ref[:, cut]
-        feat = [feat_ref[part][:, cut] for part in range(parts)]
+        taps = packed_ref[count:, cut]
+        feat = [taps[3 * part : 3 * part + 3] for part in range(parts)]
+        inner_taps = taps[9:]
         query = causal(window(0), feat[0])
         key = causal(window(1), feat[1])
         value = causal(window(2), feat[2])
         inner = causal(key * value, inner_taps)
         gated_ref[:, cut] = (query * inner)[HALO:last].astype(gated_ref.dtype)
-        grad_next = next_ref[parts, :, cut]
-        grad = jnp.concatenate([jnp.zeros_like(grad_next), grad_ref[:, cut], grad_next], axis=0)
-        grad = grad.astype(jnp.float32)
+        grad_next = next_ref[parts, :, cut].astype(jnp.float32)
+        grad = jnp.concatenate([jnp.zeros_like(grad_next), packed_ref[:count, cut], grad_next], axis=0)
         mixed = adjoint(grad * query, inner_taps)
         back[0, :, cut] = adjoint(grad * inner, feat[0])[HALO:last].astype(back.dtype)
         back[1, :, cut] = adjoint(mixed * value, feat[1])[HALO:last].astype(back.dtype)
         back[2, :, cut] = adjoint(mixed * key, feat[2])[HALO:last].astype(back.dtype)
     contract = (((1,), (1,)), ((), ()))
+    leaving = []
     for i in range(steps):
         for copy in copies[i]:
             copy.wait()
@@ -181,17 +179,21 @@
             total = total + lax.dot_general(
                 back[part], w_buf[part, cut], contract, preferred_element_type=jnp.float32
             )
-        o_ref[:, cut] = total.astype(o_ref.dtype)
-
-
-def mix(upper, proj, prev, following, feat, inner, grad, mine, low, high):
+        o_buf[:, cut] = total.astype(o_buf.dtype)
+        leaving.append(pltpu.make_async_copy(o_buf.at[:, cut], o_ref.at[:, cut], sems.at[i, 2]))
+        leaving[-1].start()
+    for copy in leaving:
+        copy.wait()
+
+
+def mix(upper, proj, prev, following, packed, mine, theirs):
     parts, depth, lanes = mine.shape
-    count = grad.shape[0]
+    count = proj.shape[1]
     steps = 8
     return pl.pallas_call(
         mix_kernel,
-        in_specs=[smem()] + [vmem()] * 6 + [hbm()] * 3,
-        out_specs=[vmem(), vmem()],
+        in_specs=[smem()] + [vmem()] * 4 + [hbm()] * 2,
+        out_specs=[vmem(), hbm()],
         out_shape=[
             jax.ShapeDtypeStruct((count, 2 * lanes), jnp.bfloat16),
             jax.ShapeDtypeStruct((count, depth), jnp.bfloat16),
@@ -199,11 +201,12 @@
         scratch_shapes=[
             pltpu.VMEM((parts, depth, 2 * lanes), mine.dtype),
             pltpu.VMEM((parts, count, 2 * lanes), jnp.bfloat16),
-            pltpu.SemaphoreType.DMA((steps, 2)),
+            pltpu.VMEM((count, depth), jnp.bfloat16),
+            pltpu.SemaphoreType.DMA((steps, 3)),
         ],
         compiler_params=PARAMS,
         name="mix",
-    )(upper, proj, prev, following, feat, inner, grad, mine, low, high)
+    )(upper, proj, prev, following, packed, mine, theirs)
 
 
 def encode(tokens):
@@ -233,58 +236,38 @@
     def local(tokens, proj_weight, feat_taps, inner_taps, grad_out):
         upper = lax.axis_index("yl")
         core = lax.axis_index("c")
-        width = proj_weight.shape[0]
         channels = inner_taps.shape[1]
         flag = upper.astype(jnp.int32).reshape(1)
 
+        count = grad_out.shape[0] // 2
+        taps = jnp.concatenate([feat_taps.reshape(9, channels), inner_taps], axis=0)
+
+        def message(which):
+            rows = lax.dynamic_slice_in_dim(grad_out, which * count, count, 0)
+            return jnp.concatenate([rows.astype(jnp.float32), taps], axis=0)
+
+        near = swap_homes(message(upper))
+        far = exchange(message(1 - upper), ("c", "yl"), (2, 2), lambda c, yl: (1 - yl, c))
         planes = proj_weight.transpose(1, 0, 2)
-        half = width // 2
-        low, high = planes[:, :half], planes[:, half:]
-        count = grad_out.shape[0] // 2
-        near = lax.dynamic_slice_in_dim(grad_out, upper * count, count, 0)
-        far = lax.dynamic_slice_in_dim(grad_out, (1 - upper) * count, count, 0)
-        taps = jnp.concatenate([feat_taps.reshape(9, channels), inner_taps], axis=0)
-
         rehomed = swap_homes(encode(tokens))
-        rehomed, low, high, near, far, sent_taps = lax.optimization_barrier(
-            (rehomed, low, high, near, far, taps)
-        )
-
-        def beside(step):
-            def route(yh, yl):
-                place = (yh * 2 + yl + step) % ring
-                return (place // 2, place % 2)
-
-            return route
-
-        low = exchange(low, ("yh", "yl"), (sizes[0], 2), beside(-1))
-        high = exchange(high, ("yh", "yl"), (sizes[0], 2), beside(1))
-
-        def both(mine, theirs, axis):
-            return jnp.where(
-                upper == 0,
-                jnp.concatenate([mine, theirs], axis=axis),
-                jnp.concatenate([theirs, mine], axis=axis),
-            )
-
-        near = swap_homes(near)
-        far = exchange(far, ("c", "yl"), (2, 2), lambda c, yl: (1 - yl, c))
-        came_taps = lax.ppermute(sent_taps, "yl", [(0, 1), (1, 0)])
-        rehomed, near, far, came_taps = lax.optimization_barrier((rehomed, near, far, came_taps))
+        rehomed, near, far, sent = lax.optimization_barrier((rehomed, near, far, planes))
+
+        def beside(yh, c, yl):
+            place = (yh * 2 + yl + (1 if c else ring - 1)) % ring
+            return (place // 2, c, place % 2)
+
+        theirs = exchange(sent, ("yh", "c", "yl"), (sizes[0], 2, 2), beside)
         gathered = lax.all_gather(rehomed, "z", axis=0, tiled=True).astype(jnp.bfloat16)
-        taps = both(taps, came_taps, 1)
-        feat = taps[:9].reshape(3, 3, 2 * channels)
-        inner = taps[9:]
-        grad = jnp.where(
+        packed = jnp.where(
             core == 0,
             jnp.concatenate([near, far], axis=1),
             jnp.concatenate([far, near], axis=1),
         )
 
-        proj, head, tail = project(flag, gathered, grad, planes, low, high)
+        proj, head, tail = project(flag, gathered, packed, planes, theirs)
         prev = along(tail, 1)
         following = along(head, -1)
-        gated, spread = mix(flag, proj, prev, following, feat, inner, grad, planes, low, high)
+        gated, spread = mix(flag, proj, prev, following, packed, planes, theirs)
         grad_tokens = lax.psum_scatter(spread, "z", scatter_dimension=0, tiled=True)
 
         first, second = gated[:, :channels], gated[:, channels:]

time: 205 us -> 173 us (0.84)
  waiting for transfers between devices: 69.5 us -> 54.5 us
  starting transfers between devices: 52.4 us -> 39.4 us
  blocking collectives: 45.8 us -> 43.7 us
    ppermute x1 -> x0, waiting for transfers between devices: 17.7 us -> none  [local(): came_taps = lax.ppermute(sent_taps, 'yl', [(0, 1), (1, 0)])]
    ppermute x10 -> x9, starting transfers between devices: 50.3 us -> 39.4 us  [exchange(): return lax.ppermute(value, axes, pairs)]
    slice x2 -> x0, local copies, waits for them, and re-layouts: 3.77 us -> none  [the longest x1 3.77 us: local(): low, high = (planes[:, :half], planes[:, half:])]
    ppermute x10 -> x9, waiting for transfers between devices: 11.3 us -> 13.7 us  [exchange(): return lax.ppermute(value, axes, pairs)]
    all_gather x1, blocking collectives: 45.8 us -> 43.7 us  [local(): lax.all_gather(rehomed, 'z', axis=0, tiled=True).astype(jnp.bfloat16)]
    unnamed x11 -> x9, local copies, waits for them, and re-layouts: 2.47 us -> 4.44 us
  transfers between devices with their start and end apart: 12 -> 10, of which waited for: 7 -> 7; matrix products, arithmetic and copies ran while one was open for 3% -> 2% of each run, Pallas kernels for 0% -> 0%
where the time goes in v5:
time: 173 us
  waiting for transfers between devices  54.5 us (32%)
  blocking collectives  43.7 us (25%)
  starting transfers between devices  39.4 us (23%)
  between operations  14.2 us (8%)
  Pallas kernels  11.1 us (6%)
  local copies, waits for them, and re-layouts  5.22 us (3%)
  other arithmetic  4.84 us (3%)
    all_gather x1, blocking collectives, local(): lax.all_gather(rehomed, 'z', axis=0, tiled=True).astype(jnp.bfloat16)  43.7 us
    reduce_scatter x1, waiting for transfers between devices, local(): grad_tokens = lax.psum_scatter(spread, 'z', scatter_dimension=0, tiled=True)  40.7 us
    ppermute x9, starting transfers between devices, exchange(): return lax.ppermute(value, axes, pairs)  39.4 us
    ppermute x9, waiting for transfers between devices, exchange(): return lax.ppermute(value, axes, pairs)  13.7 us
    pallas_call x1, Pallas kernels, mix(): pl.pallas_call(mix_kernel, in_specs=[smem()] + [vmem()] * 4 + [hbm()] * 2...  6.23 us
    pallas_call x1, Pallas kernels, project(): pl.pallas_call(project_kernel, in_specs=[smem(), vmem(), vmem(), hbm(), h...  4.82 us
    unnamed x9, local copies, waits for them, and re-layouts  4.44 us
  transfers between devices with their start and end apart: 10, of which 7 were waited for; matrix products, arithmetic and copies ran while one was open for 2% of the time, Pallas kernels for 0%

profile of v5, /device:TPU:1, one launch (start us, length us, event | category | flops | bytes accessed | tf_op | source)
XLA Modules:
  0.0 172.9 jit_solution(17975927135390060334)
XLA Ops:
  7.2 1.1 fusion
  8.3 1.1 fusion.1
  9.5 4.6 %collective-permute-start = (f16[24,4224]{1,0:T(8,128)(2,1)S(1)}, f16[24,4224]{1,0:T(8,128)(2,1)S(1)}, u32[]{:S(2)}, u32[]{:S(2)}) collective-permute-start(f16[24,4224]{1,0:T(8,128)(2,1)S(1)} %pad_maximum_fusion.4), channel_id=1, source_target_pairs={{0,0},{12,24},{24,12},{36,36},{1,1},{13,25},{25,13},{37,37},{2,2},... | collective-permute-start | bytes 608264 | tf_op jit(solution)/shard_map/ppermute | solution.py:32
  14.8 0.9 dynamic-slice_convert_fusion
  15.7 0.7 pad_maximum_fusion
  16.4 1.9 %collective-permute-start.1 = (f32[304,128]{1,0:T(8,128)S(1)}, f32[304,128]{1,0:T(8,128)S(1)}, u32[]{:S(2)}, u32[]{:S(2)}) collective-permute-start(f32[304,128]{1,0:T(8,128)S(1)} %get-tuple-element.29), channel_id=1, source_target_pairs={{0,0},{12,24},{24,12},{36,36},{1,1},{13,25},{25,13},{37,37},{2,2},... | collective-permute-start | bytes 466952 | tf_op jit(solution)/shard_map/ppermute | solution.py:32
  18.4 1.9 %collective-permute-start.2 = (f32[304,128]{1,0:T(8,128)S(1)}, f32[304,128]{1,0:T(8,128)S(1)}, u32[]{:S(2)}, u32[]{:S(2)}) collective-permute-start(f32[304,128]{1,0:T(8,128)S(1)} %get-tuple-element.28), channel_id=1, source_target_pairs={{0,24},{12,0},{24,36},{36,12},{1,25},{13,1},{25,37},{37,13},{2,26}... | collective-permute-start | bytes 466952 | tf_op jit(solution)/shard_map/ppermute | solution.py:32
  20.3 2.7 %collective-permute-done.1 = f32[304,128]{1,0:T(8,128)S(1)} collective-permute-done((f32[304,128]{1,0:T(8,128)S(1)}, f32[304,128]{1,0:T(8,128)S(1)}, u32[]{:S(2)}, u32[]{:S(2)}) %collective-permute-start.1) | collective-permute-done | bytes 155680 | tf_op jit(solution)/shard_map/ppermute | solution.py:32
  23.0 3.5 %collective-permute-done.2 = f32[304,128]{1,0:T(8,128)S(1)} collective-permute-done((f32[304,128]{1,0:T(8,128)S(1)}, f32[304,128]{1,0:T(8,128)S(1)}, u32[]{:S(2)}, u32[]{:S(2)}) %collective-permute-start.2) | collective-permute-done | bytes 155680 | tf_op jit(solution)/shard_map/ppermute | solution.py:32
  27.2 1.9 %collective-permute-start.3 = (bf16[3,4096,128]{2,1,0:T(8,128)(2,1)}, bf16[3,4096,128]{2,1,0:T(8,128)(2,1)S(1)}, u32[]{:S(2)}, u32[]{:S(2)}) collective-permute-start(bf16[3,4096,128]{2,1,0:T(8,128)(2,1)} %bitcast.2), channel_id=1, source_target_pairs={{0,588},{12,0},{24,36},{36,216},{192,12},{204,192},{216,228},{228,... | collective-permute-start | bytes 9437192 | tf_op jit(solution)/shard_map/ppermute | solution.py:32
  29.1 43.7 %all-gather.1 = f16[288,4224]{1,0:T(8,128)(2,1)S(1)} all-gather(f16[24,4224]{1,0:T(8,128)(2,1)S(1)} %collective-permute-done), channel_id=1, replica_groups=mesh['yh'=4,'x'=4,'c'=2,'yl'=2,'z'=12] {'z'}, dimensions={0}, use_global_device_ids=true | all-gather | bytes 2635776 | tf_op jit(solution)/shard_map/all_gather | solution.py:260
  73.7 1.0 copy-done
  74.7 4.8 %project.1 = (bf16[3,288,256]{2,1,0:T(8,128)(2,1)S(1)}, bf16[4,8,256]{2,1,0:T(8,128)(2,1)S(1)}, bf16[3,8,256]{2,1,0:T(8,128)(2,1)S(1)}) custom-call(s32[1]{0:T(128)} %bitcast.upper_ref, bf16[288,4224]{1,0:T(8,128)(2,1)S(1)} %convert_element_type.16.x_ref, f32[304,256]{1,0:T(8,128)S(1)} %maximum_select_fusion.packed_ref, bf16[3,4096,128]{2,1,0:T(8,128)(2,1)S(1)} %bitcast.3, ...), custom_call_target="tpu_custom_call" | custom-call | tf_op jit(solution)/shard_map/project/pallas_call | solution.py:89
  79.6 9.6 %collective-permute-start.5 = (bf16[4,8,256]{2,1,0:T(8,128)(2,1)S(1)}, bf16[4,8,256]{2,1,0:T(8,128)(2,1)S(1)}, u32[]{:S(2)}, u32[]{:S(2)}) collective-permute-start(bf16[4,8,256]{2,1,0:T(8,128)(2,1)S(1)} %get-tuple-element.19), channel_id=1, source_target_pairs={{12,24},{24,0},{36,12},{48,36},{60,72},{72,48},{84,60},{96,84},{10... | collective-permute-start | bytes 49160 | tf_op jit(solution)/shard_map/ppermute | solution.py:32
  89.2 2.8 %collective-permute-start.4 = (bf16[3,8,256]{2,1,0:T(8,128)(2,1)S(1)}, bf16[3,8,256]{2,1,0:T(8,128)(2,1)S(1)}, u32[]{:S(2)}, u32[]{:S(2)}) collective-permute-start(bf16[3,8,256]{2,1,0:T(8,128)(2,1)S(1)} %get-tuple-element.18), channel_id=1, source_target_pairs={{0,24},{12,36},{24,12},{36,48},{48,72},{60,84},{72,60},{84,96},{96... | collective-permute-start | bytes 36872 | tf_op jit(solution)/shard_map/ppermute | solution.py:32
  92.0 0.8 collective-permute-done.4.prev_ref
  92.8 6.2 %mix.1 = (bf16[288,256]{1,0:T(8,128)(2,1)S(1)}, bf16[288,4096]{1,0:T(8,128)(2,1)S(1)}) custom-call(s32[1]{0:T(128)} %bitcast.upper_ref, bf16[3,288,256]{2,1,0:T(8,128)(2,1)S(1)} %get-tuple-element.17.proj_ref, bf16[3,8,256]{2,1,0:T(8,128)(2,1)S(1)} %collective-permute-done.4.prev_ref, bf16[4,8,256]{2,1,0:T(8,128)(2,1)S(1)} %collective-permute-done.5.next_ref, ...), custom_call_target="tpu_custom_call" | custom-call | tf_op jit(solution)/shard_map/mix/pallas_call | solution.py:193
  99.0 1.4 copy-done.1
  100.5 4.2 %collective-permute-start.6 = (bf16[288,128]{1,0:T(8,128)(2,1)S(1)}, bf16[288,128]{1,0:T(8,128)(2,1)S(1)}, u32[]{:S(2)}, u32[]{:S(2)}) collective-permute-start(bf16[288,128]{1,0:T(8,128)(2,1)S(1)} %get-tuple-element.24), channel_id=1, source_target_pairs={{0,0},{12,24},{24,12},{36,36},{1,1},{13,25},{25,13},{37,37},{2,2},... | collective-permute-start | bytes 221192 | tf_op jit(solution)/shard_map/ppermute | solution.py:32
  104.7 1.9 %collective-permute-start.7 = (bf16[288,128]{1,0:T(8,128)(2,1)S(1)}, bf16[288,128]{1,0:T(8,128)(2,1)S(1)}, u32[]{:S(2)}, u32[]{:S(2)}) collective-permute-start(bf16[288,128]{1,0:T(8,128)(2,1)S(1)} %get-tuple-element.25), channel_id=1, source_target_pairs={{0,12},{12,36},{24,0},{36,24},{1,13},{13,37},{25,1},{37,25},{2,14}... | collective-permute-start | bytes 221192 | tf_op jit(solution)/shard_map/ppermute | solution.py:32
  106.7 3.1 %collective-permute-done.7 = bf16[288,128]{1,0:T(8,128)(2,1)S(1)} collective-permute-done((bf16[288,128]{1,0:T(8,128)(2,1)S(1)}, bf16[288,128]{1,0:T(8,128)(2,1)S(1)}, u32[]{:S(2)}, u32[]{:S(2)}) %collective-permute-start.7) | collective-permute-done | bytes 73760 | tf_op jit(solution)/shard_map/ppermute | solution.py:32
  110.5 40.7 %reduce-scatter.2.cloned.1.call-done = bf16[24,4096]{1,0:T(8,128)(2,1)} async-done(((bf16[288,4096]{1,0:T(8,128)(2,1)}), bf16[24,4096]{1,0:T(8,128)(2,1)}) %reduce-scatter.2.cloned.1.call-update) | async-done | bytes 196624 | tf_op jit(solution)/shard_map/reduce_scatter | solution.py:271
  151.2 10.5 %collective-permute-start.8 = (bf16[24,4096]{1,0:T(8,128)(2,1)}, bf16[24,4096]{1,0:T(8,128)(2,1)S(1)}, u32[]{:S(2)}, u32[]{:S(2)}) collective-permute-start(bf16[24,4096]{1,0:T(8,128)(2,1)} %reduce-scatter.2.cloned.1.call-done), channel_id=1, source_target_pairs={{0,0},{12,24},{24,12},{36,36},{1,1},{13,25},{25,13},{37,37},{2,2},... | collective-permute-start | bytes 589832 | tf_op jit(solution)/shard_map/ppermute | solution.py:32
  161.8 3.5 %collective-permute-done.8 = bf16[24,4096]{1,0:T(8,128)(2,1)S(1)} collective-permute-done((bf16[24,4096]{1,0:T(8,128)(2,1)}, bf16[24,4096]{1,0:T(8,128)(2,1)S(1)}, u32[]{:S(2)}, u32[]{:S(2)}) %collective-permute-start.8) | collective-permute-done | bytes 196640 | tf_op jit(solution)/shard_map/ppermute | solution.py:32
  (21 shorter events, 4.0 us)
Async XLA Ops:
  7.2 144.1 %reduce-scatter.2.cloned.1.call-start = ((), (), s32[]{:S(2)}) async-start(), calls=%async_computation.1 | async-start | bytes 2555904 | tf_op jit(solution)/shard_map/reduce_scatter | solution.py:271
  9.5 17.0 %collective-permute-start = (f16[24,4224]{1,0:T(8,128)(2,1)S(1)}, f16[24,4224]{1,0:T(8,128)(2,1)S(1)}, u32[]{:S(2)}, u32[]{:S(2)}) collective-permute-start(f16[24,4224]{1,0:T(8,128)(2,1)S(1)} %pad_maximum_fusion.4), channel_id=1, source_target_pairs={{0,0},{12,24},{24,12},{36,36},{1,1},{13,25},{25,13},{37,37},{2,2},... | collective-permute-start | bytes 608264 | tf_op jit(solution)/shard_map/ppermute | solution.py:32
  16.4 6.5 %collective-permute-start.1 = (f32[304,128]{1,0:T(8,128)S(1)}, f32[304,128]{1,0:T(8,128)S(1)}, u32[]{:S(2)}, u32[]{:S(2)}) collective-permute-start(f32[304,128]{1,0:T(8,128)S(1)} %get-tuple-element.29), channel_id=1, source_target_pairs={{0,0},{12,24},{24,12},{36,36},{1,1},{13,25},{25,13},{37,37},{2,2},... | collective-permute-start | bytes 466952 | tf_op jit(solution)/shard_map/ppermute | solution.py:32
  18.4 8.1 %collective-permute-start.2 = (f32[304,128]{1,0:T(8,128)S(1)}, f32[304,128]{1,0:T(8,128)S(1)}, u32[]{:S(2)}, u32[]{:S(2)}) collective-permute-start(f32[304,128]{1,0:T(8,128)S(1)} %get-tuple-element.28), channel_id=1, source_target_pairs={{0,24},{12,0},{24,36},{36,12},{1,25},{13,1},{25,37},{37,13},{2,26}... | collective-permute-start | bytes 466952 | tf_op jit(solution)/shard_map/ppermute | solution.py:32
  26.5 0.7 copy-start.2
  27.2 46.5 %collective-permute-start.3 = (bf16[3,4096,128]{2,1,0:T(8,128)(2,1)}, bf16[3,4096,128]{2,1,0:T(8,128)(2,1)S(1)}, u32[]{:S(2)}, u32[]{:S(2)}) collective-permute-start(bf16[3,4096,128]{2,1,0:T(8,128)(2,1)} %bitcast.2), channel_id=1, source_target_pairs={{0,588},{12,0},{24,36},{36,216},{192,12},{204,192},{216,228},{228,... | collective-permute-start | bytes 9437192 | tf_op jit(solution)/shard_map/ppermute | solution.py:32
  72.7 0.9 copy-start.3
  72.7 2.0 %copy-start = (bf16[4096,3,128]{2,0,1:T(8,128)(2,1)S(1)}, bf16[4096,3,128]{2,0,1:T(8,128)(2,1)}, u32[]{:S(2)}) copy-start(bf16[4096,3,128]{2,0,1:T(8,128)(2,1)} %param.6) | copy-start | bytes 9437188
  79.6 13.2 %collective-permute-start.5 = (bf16[4,8,256]{2,1,0:T(8,128)(2,1)S(1)}, bf16[4,8,256]{2,1,0:T(8,128)(2,1)S(1)}, u32[]{:S(2)}, u32[]{:S(2)}) collective-permute-start(bf16[4,8,256]{2,1,0:T(8,128)(2,1)S(1)} %get-tuple-element.19), channel_id=1, source_target_pairs={{12,24},{24,0},{36,12},{48,36},{60,72},{72,48},{84,60},{96,84},{10... | collective-permute-start | bytes 49160 | tf_op jit(solution)/shard_map/ppermute | solution.py:32
  89.2 3.6 %collective-permute-start.4 = (bf16[3,8,256]{2,1,0:T(8,128)(2,1)S(1)}, bf16[3,8,256]{2,1,0:T(8,128)(2,1)S(1)}, u32[]{:S(2)}, u32[]{:S(2)}) collective-permute-start(bf16[3,8,256]{2,1,0:T(8,128)(2,1)S(1)} %get-tuple-element.18), channel_id=1, source_target_pairs={{0,24},{12,36},{24,12},{36,48},{48,72},{60,84},{72,60},{84,96},{96... | collective-permute-start | bytes 36872 | tf_op jit(solution)/shard_map/ppermute | solution.py:32
  99.0 1.4 copy-start.1
  100.5 6.2 %collective-permute-start.6 = (bf16[288,128]{1,0:T(8,128)(2,1)S(1)}, bf16[288,128]{1,0:T(8,128)(2,1)S(1)}, u32[]{:S(2)}, u32[]{:S(2)}) collective-permute-start(bf16[288,128]{1,0:T(8,128)(2,1)S(1)} %get-tuple-element.24), channel_id=1, source_target_pairs={{0,0},{12,24},{24,12},{36,36},{1,1},{13,25},{25,13},{37,37},{2,2},... | collective-permute-start | bytes 221192 | tf_op jit(solution)/shard_map/ppermute | solution.py:32
  104.7 5.1 %collective-permute-start.7 = (bf16[288,128]{1,0:T(8,128)(2,1)S(1)}, bf16[288,128]{1,0:T(8,128)(2,1)S(1)}, u32[]{:S(2)}, u32[]{:S(2)}) collective-permute-start(bf16[288,128]{1,0:T(8,128)(2,1)S(1)} %get-tuple-element.25), channel_id=1, source_target_pairs={{0,12},{12,36},{24,0},{36,24},{1,13},{13,37},{25,1},{37,25},{2,14}... | collective-permute-start | bytes 221192 | tf_op jit(solution)/shard_map/ppermute | solution.py:32
  151.2 14.1 %collective-permute-start.8 = (bf16[24,4096]{1,0:T(8,128)(2,1)}, bf16[24,4096]{1,0:T(8,128)(2,1)S(1)}, u32[]{:S(2)}, u32[]{:S(2)}) collective-permute-start(bf16[24,4096]{1,0:T(8,128)(2,1)} %reduce-scatter.2.cloned.1.call-done), channel_id=1, source_target_pairs={{0,0},{12,24},{24,12},{36,36},{1,1},{13,25},{25,13},{37,37},{2,2},... | collective-permute-start | bytes 589832 | tf_op jit(solution)/shard_map/ppermute | solution.py:32
Sparse Core Ops, SparseCore 0:
  100.6 50.6 reduce-scatter.1

commit v6 on v5

--- a/solution.py
+++ b/solution.py
@@ -56,49 +56,47 @@
     return pl.multiple_of(upper * lanes, lanes), pl.multiple_of((1 - upper) * lanes, lanes)
 
 
-def project_kernel(upper_ref, x_ref, packed_ref, mine_ref, theirs_ref, o_ref, head_ref, tail_ref, w_buf, sems):
+def side_by_side(mine_ref, theirs_ref, part, cut):
+    return jnp.concatenate([mine_ref[part, cut], theirs_ref[part, cut]], axis=1)
+
+
+def project_kernel(upper_ref, x_ref, packed_ref, mine_ref, theirs_ref, o_ref, head_ref, tail_ref):
     parts, depth, lanes = mine_ref.shape
+    count = x_ref.shape[0]
     own, other = slots(upper_ref, lanes)
-    copies = []
+    scale = jnp.exp2(x_ref[:, depth : depth + 1].astype(jnp.float32) - TOP)
+    block = min(depth, 1024)
     for j in range(parts):
-        moves = (
-            (mine_ref.at[j], w_buf.at[j, :, pl.ds(own, lanes)]),
-            (theirs_ref.at[j], w_buf.at[j, :, pl.ds(other, lanes)]),
-        )
-        copies.append(
-            [pltpu.make_async_copy(src, dst, sems.at[j, k]) for k, (src, dst) in enumerate(moves)]
-        )
-        for copy in copies[-1]:
-            copy.start()
-    rows = x_ref[:, :depth]
-    scale = jnp.exp2(x_ref[:, depth : depth + 1].astype(jnp.float32) - TOP)
-    count = rows.shape[0]
-    for j in range(parts):
-        for copy in copies[j]:
-            copy.wait()
-        total = jnp.dot(rows, w_buf[j], preferred_element_type=jnp.float32) * scale
-        o_ref[j] = total.astype(o_ref.dtype)
-        head_ref[j] = total[:HALO].astype(head_ref.dtype)
-        tail_ref[j] = total[count - HALO :].astype(tail_ref.dtype)
+        total = None
+        for begin in range(0, depth, block):
+            cut = slice(begin, begin + block)
+            piece = jnp.dot(
+                x_ref[:, cut],
+                side_by_side(mine_ref, theirs_ref, j, cut),
+                preferred_element_type=jnp.float32,
+            )
+            total = piece if total is None else total + piece
+        total = total * scale
+        for place, half in ((own, total[:, :lanes]), (other, total[:, lanes:])):
+            spot = pl.ds(place, lanes)
+            o_ref[j, :, spot] = half.astype(o_ref.dtype)
+            head_ref[j, :, spot] = half[:HALO].astype(head_ref.dtype)
+            tail_ref[j, :, spot] = half[count - HALO :].astype(tail_ref.dtype)
     head_ref[parts] = packed_ref[:HALO].astype(head_ref.dtype)
 
 
 def project(upper, rows, packed, mine, theirs):
-    parts, depth, lanes = mine.shape
+    parts, _, lanes = mine.shape
     count = rows.shape[0]
     return pl.pallas_call(
         project_kernel,
-        in_specs=[smem(), vmem(), vmem(), hbm(), hbm()],
+        in_specs=[smem()] + [vmem()] * 4,
         out_specs=[vmem()] * 3,
         out_shape=[
             jax.ShapeDtypeStruct((parts, count, 2 * lanes), jnp.bfloat16),
             jax.ShapeDtypeStruct((parts + 1, HALO, 2 * lanes), jnp.bfloat16),
             jax.ShapeDtypeStruct((parts, HALO, 2 * lanes), jnp.bfloat16),
         ],
-        scratch_shapes=[
-            pltpu.VMEM((parts, depth, 2 * lanes), mine.dtype),
-            pltpu.SemaphoreType.DMA((parts, 2)),
-        ],
         compiler_params=PARAMS,
         name="project",
     )(upper, rows, packed, mine, theirs)
@@ -120,7 +118,7 @@
 
 def mix_kernel(
     upper_ref, proj_ref, prev_ref, next_ref, packed_ref, mine_ref, theirs_ref,
-    gated_ref, o_ref, w_buf, back, o_buf, sems,
+    gated_ref, o_ref, back, o_buf, sems,
 ):
     parts, depth, lanes = mine_ref.shape
     count = proj_ref.shape[1]
@@ -128,25 +126,6 @@
     steps = sems.shape[0]
     block = depth // steps
     own, other = slots(upper_ref, lanes)
-    copies = []
-    for i in range(steps):
-        begin = i * block
-        copies.append(
-            (
-                pltpu.make_async_copy(
-                    mine_ref.at[:, pl.ds(begin, block), :],
-                    w_buf.at[:, pl.ds(begin, block), pl.ds(own, lanes)],
-                    sems.at[i, 0],
-                ),
-                pltpu.make_async_copy(
-                    theirs_ref.at[:, pl.ds(begin, block), :],
-                    w_buf.at[:, pl.ds(begin, block), pl.ds(other, lanes)],
-                    sems.at[i, 1],
-                ),
-            )
-        )
-        for copy in copies[-1]:
-            copy.start()
     for side in range(2):
         cut = slice(side * lanes, (side + 1) * lanes)
 
@@ -168,19 +147,25 @@
         back[0, :, cut] = adjoint(grad * inner, feat[0])[HALO:last].astype(back.dtype)
         back[1, :, cut] = adjoint(mixed * value, feat[1])[HALO:last].astype(back.dtype)
         back[2, :, cut] = adjoint(mixed * key, feat[2])[HALO:last].astype(back.dtype)
+    left = [
+        jnp.concatenate([back[part, :, pl.ds(own, lanes)], back[part, :, pl.ds(other, lanes)]], axis=1)
+        for part in range(parts)
+    ]
     contract = (((1,), (1,)), ((), ()))
     leaving = []
     for i in range(steps):
-        for copy in copies[i]:
-            copy.wait()
         cut = slice(i * block, (i + 1) * block)
-        total = lax.dot_general(back[0], w_buf[0, cut], contract, preferred_element_type=jnp.float32)
-        for part in range(1, parts):
-            total = total + lax.dot_general(
-                back[part], w_buf[part, cut], contract, preferred_element_type=jnp.float32
+        total = None
+        for part in range(parts):
+            piece = lax.dot_general(
+                left[part],
+                side_by_side(mine_ref, theirs_ref, part, cut),
+                contract,
+                preferred_element_type=jnp.float32,
             )
+            total = piece if total is None else total + piece
         o_buf[:, cut] = total.astype(o_buf.dtype)
-        leaving.append(pltpu.make_async_copy(o_buf.at[:, cut], o_ref.at[:, cut], sems.at[i, 2]))
+        leaving.append(pltpu.make_async_copy(o_buf.at[:, cut], o_ref.at[:, cut], sems.at[i]))
         leaving[-1].start()
     for copy in leaving:
         copy.wait()
@@ -192,17 +177,16 @@
     steps = 8
     return pl.pallas_call(
         mix_kernel,
-        in_specs=[smem()] + [vmem()] * 4 + [hbm()] * 2,
+        in_specs=[smem()] + [vmem()] * 6,
         out_specs=[vmem(), hbm()],
         out_shape=[
             jax.ShapeDtypeStruct((count, 2 * lanes), jnp.bfloat16),
-            jax.ShapeDtypeStruct((count, depth), jnp.bfloat16),
+            pltpu.HBM((count, depth), jnp.bfloat16),
         ],
         scratch_shapes=[
-            pltpu.VMEM((parts, depth, 2 * lanes), mine.dtype),
             pltpu.VMEM((parts, count, 2 * lanes), jnp.bfloat16),
             pltpu.VMEM((count, depth), jnp.bfloat16),
-            pltpu.SemaphoreType.DMA((steps, 3)),
+            pltpu.SemaphoreType.DMA((steps,)),
         ],
         compiler_params=PARAMS,
         name="mix",
@@ -246,18 +230,21 @@
             rows = lax.dynamic_slice_in_dim(grad_out, which * count, count, 0)
             return jnp.concatenate([rows.astype(jnp.float32), taps], axis=0)
 
-        near = swap_homes(message(upper))
-        far = exchange(message(1 - upper), ("c", "yl"), (2, 2), lambda c, yl: (1 - yl, c))
+        near, far = message(upper), message(1 - upper)
         planes = proj_weight.transpose(1, 0, 2)
         rehomed = swap_homes(encode(tokens))
-        rehomed, near, far, sent = lax.optimization_barrier((rehomed, near, far, planes))
+        rehomed, sent, near, far = lax.optimization_barrier((rehomed, planes, near, far))
+        near = swap_homes(near)
+        far = exchange(far, ("c", "yl"), (2, 2), lambda c, yl: (1 - yl, c))
 
         def beside(yh, c, yl):
             place = (yh * 2 + yl + (1 if c else ring - 1)) % ring
             return (place // 2, c, place % 2)
 
         theirs = exchange(sent, ("yh", "c", "yl"), (sizes[0], 2, 2), beside)
-        gathered = lax.all_gather(rehomed, "z", axis=0, tiled=True).astype(jnp.bfloat16)
+        gathered = lax.all_gather(rehomed, "z", axis=0, tiled=True)
+        gathered, near, far = lax.optimization_barrier((gathered, near, far))
+        gathered = gathered.astype(jnp.bfloat16)
         packed = jnp.where(
             core == 0,
             jnp.concatenate([near, far], axis=1),

time: 173 us -> 164 us (0.948)
  starting transfers between devices: 39.4 us -> 46.3 us
  waiting for transfers between devices: 54.5 us -> 48 us
  Pallas kernels: 11.1 us -> 6.54 us
  blocking collectives: 43.7 us -> 39.4 us
  local copies, waits for them, and re-layouts: 5.22 us -> 3.02 us
    ppermute x9, starting transfers between devices: 39.4 us -> 46.3 us  [exchange(): return lax.ppermute(value, axes, pairs)]
    ppermute x9, waiting for transfers between devices: 13.7 us -> 7.91 us  [exchange(): return lax.ppermute(value, axes, pairs)]
    pallas_call x2, Pallas kernels: 11.1 us -> 6.54 us  [the longest x1 4.49 us: mix(): pl.pallas_call(mix_kernel, in_specs=[smem()] + [vmem()] * 6, out_specs=[v...]
    all_gather x1, blocking collectives: 43.7 us -> 39.4 us  [local(): gathered = lax.all_gather(rehomed, 'z', axis=0, tiled=True)]
    unnamed x9 -> x3, local copies, waits for them, and re-layouts: 4.44 us -> 2.24 us
  transfers between devices with their start and end apart: 10 -> 10, of which waited for: 7 -> 6; matrix products, arithmetic and copies ran while one was open for 2% -> 2% of each run, Pallas kernels for 0% -> 0%
where the time goes in v6:
time: 164 us; the launch traced here: 163 us
  waiting for transfers between devices  48 us (29%)
  starting transfers between devices  46.3 us (28%)
  blocking collectives  39.4 us (24%)
  between operations  14.2 us (9%)
  Pallas kernels  6.54 us (4%)
  other arithmetic  5.51 us (3%)
  local copies, waits for them, and re-layouts  3.02 us (2%)
    ppermute x9, starting transfers between devices, exchange(): return lax.ppermute(value, axes, pairs)  46.3 us
    reduce_scatter x1, waiting for transfers between devices, local(): grad_tokens = lax.psum_scatter(spread, 'z', scatter_dimension=0, tiled=True)  40.1 us
    all_gather x1, blocking collectives, local(): gathered = lax.all_gather(rehomed, 'z', axis=0, tiled=True)  39.4 us
    ppermute x9, waiting for transfers between devices, exchange(): return lax.ppermute(value, axes, pairs)  7.91 us
    pallas_call x1, Pallas kernels, mix(): pl.pallas_call(mix_kernel, in_specs=[smem()] + [vmem()] * 6, out_specs=[v...  4.49 us
  transfers between devices with their start and end apart: 10, of which 6 were waited for; matrix products, arithmetic and copies ran while one was open for 2% of the time, Pallas kernels for 0%

profile of v6, /device:TPU:1, one launch (start us, length us, event | category | flops | bytes accessed | tf_op | source)
XLA Modules:
  0.0 163.0 jit_solution(17205712742931418910)
XLA Ops:
  7.2 1.1 fusion
  8.3 1.1 fusion.1
  9.5 4.6 %collective-permute-start = (f16[24,4224]{1,0:T(8,128)(2,1)S(1)}, f16[24,4224]{1,0:T(8,128)(2,1)S(1)}, u32[]{:S(2)}, u32[]{:S(2)}) collective-permute-start(f16[24,4224]{1,0:T(8,128)(2,1)S(1)} %pad_maximum_fusion.4), channel_id=1, source_target_pairs={{0,0},{12,24},{24,12},{36,36},{1,1},{13,25},{25,13},{37,37},{2,2},... | collective-permute-start | bytes 608264 | tf_op jit(solution)/shard_map/ppermute | solution.py:32
  14.1 0.7 reshape.31
  14.8 0.9 dynamic-slice_convert_fusion
  15.7 1.4 pad_maximum_fusion
  17.5 1.9 %collective-permute-start.3 = (bf16[3,4096,128]{2,1,0:T(8,128)(2,1)}, bf16[3,4096,128]{2,1,0:T(8,128)(2,1)S(1)}, u32[]{:S(2)}, u32[]{:S(2)}) collective-permute-start(bf16[3,4096,128]{2,1,0:T(8,128)(2,1)} %bitcast.2), channel_id=1, source_target_pairs={{0,588},{12,0},{24,36},{36,216},{192,12},{204,192},{216,228},{228,... | collective-permute-start | bytes 9437192 | tf_op jit(solution)/shard_map/ppermute | solution.py:32
  19.4 9.8 %collective-permute-start.1 = (f32[304,128]{1,0:T(8,128)}, f32[304,128]{1,0:T(8,128)S(1)}, u32[]{:S(2)}, u32[]{:S(2)}) collective-permute-start(f32[304,128]{1,0:T(8,128)} %get-tuple-element.17), channel_id=1, source_target_pairs={{0,0},{12,24},{24,12},{36,36},{1,1},{13,25},{25,13},{37,37},{2,2},... | collective-permute-start | bytes 466952 | tf_op jit(solution)/shard_map/ppermute | solution.py:32
  29.2 1.9 %collective-permute-start.2 = (f32[304,128]{1,0:T(8,128)S(1)}, f32[304,128]{1,0:T(8,128)S(1)}, u32[]{:S(2)}, u32[]{:S(2)}) collective-permute-start(f32[304,128]{1,0:T(8,128)S(1)} %get-tuple-element.18), channel_id=1, source_target_pairs={{0,24},{12,0},{24,36},{36,12},{1,25},{13,1},{25,37},{37,13},{2,26}... | collective-permute-start | bytes 466952 | tf_op jit(solution)/shard_map/ppermute | solution.py:32
  31.1 39.4 %all-gather.1 = f16[288,4224]{1,0:T(8,128)(2,1)S(1)} all-gather(f16[24,4224]{1,0:T(8,128)(2,1)S(1)} %collective-permute-done), channel_id=1, replica_groups=mesh['yh'=4,'x'=4,'c'=2,'yl'=2,'z'=12] {'z'}, dimensions={0}, use_global_device_ids=true | all-gather | bytes 2635776 | tf_op jit(solution)/shard_map/all_gather | solution.py:245
  70.9 1.6 copy-done
  72.4 2.1 %project.1 = (bf16[3,288,256]{2,1,0:T(8,128)(2,1)S(1)}, bf16[4,8,256]{2,1,0:T(8,128)(2,1)S(1)}, bf16[3,8,256]{2,1,0:T(8,128)(2,1)S(1)}) custom-call(s32[1]{0:T(128)} %bitcast.upper_ref, bf16[288,4224]{1,0:T(8,128)(2,1)S(1)} %convert_element_type.16.x_ref, f32[304,256]{1,0:T(8,128)S(1)} %maximum_select_fusion.packed_ref, bf16[3,4096,128]{2,1,0:T(8,128)(2,1)S(1)} %bitcast.3, ...), custom_call_target="tpu_custom_call" | custom-call | tf_op jit(solution)/shard_map/project/pallas_call | solution.py:91
  74.5 8.4 %collective-permute-start.5 = (bf16[4,8,256]{2,1,0:T(8,128)(2,1)S(1)}, bf16[4,8,256]{2,1,0:T(8,128)(2,1)S(1)}, u32[]{:S(2)}, u32[]{:S(2)}) collective-permute-start(bf16[4,8,256]{2,1,0:T(8,128)(2,1)S(1)} %get-tuple-element.25), channel_id=1, source_target_pairs={{12,24},{24,0},{36,12},{48,36},{60,72},{72,48},{84,60},{96,84},{10... | collective-permute-start | bytes 49160 | tf_op jit(solution)/shard_map/ppermute | solution.py:32
  82.9 3.0 %collective-permute-start.4 = (bf16[3,8,256]{2,1,0:T(8,128)(2,1)S(1)}, bf16[3,8,256]{2,1,0:T(8,128)(2,1)S(1)}, u32[]{:S(2)}, u32[]{:S(2)}) collective-permute-start(bf16[3,8,256]{2,1,0:T(8,128)(2,1)S(1)} %get-tuple-element.24), channel_id=1, source_target_pairs={{0,24},{12,36},{24,12},{36,48},{48,72},{60,84},{72,60},{84,96},{96... | collective-permute-start | bytes 36872 | tf_op jit(solution)/shard_map/ppermute | solution.py:32
  85.9 0.8 collective-permute-done.4.prev_ref
  86.7 4.5 %mix.1 = (bf16[288,256]{1,0:T(8,128)(2,1)S(1)}, bf16[288,4096]{1,0:T(8,128)(2,1)}) custom-call(s32[1]{0:T(128)} %bitcast.upper_ref, bf16[3,288,256]{2,1,0:T(8,128)(2,1)S(1)} %get-tuple-element.23.proj_ref, bf16[3,8,256]{2,1,0:T(8,128)(2,1)S(1)} %collective-permute-done.4.prev_ref, bf16[4,8,256]{2,1,0:T(8,128)(2,1)S(1)} %collective-permute-done.5.next_ref, ...), custom_call_target="tpu_custom_call" | custom-call | tf_op jit(solution)/shard_map/mix/pallas_call | solution.py:178
  91.3 4.2 %collective-permute-start.6 = (bf16[288,128]{1,0:T(8,128)(2,1)S(1)}, bf16[288,128]{1,0:T(8,128)(2,1)S(1)}, u32[]{:S(2)}, u32[]{:S(2)}) collective-permute-start(bf16[288,128]{1,0:T(8,128)(2,1)S(1)} %get-tuple-element.30), channel_id=1, source_target_pairs={{0,0},{12,24},{24,12},{36,36},{1,1},{13,25},{25,13},{37,37},{2,2},... | collective-permute-start | bytes 221192 | tf_op jit(solution)/shard_map/ppermute | solution.py:32
  95.5 1.9 %collective-permute-start.7 = (bf16[288,128]{1,0:T(8,128)(2,1)S(1)}, bf16[288,128]{1,0:T(8,128)(2,1)S(1)}, u32[]{:S(2)}, u32[]{:S(2)}) collective-permute-start(bf16[288,128]{1,0:T(8,128)(2,1)S(1)} %get-tuple-element.31), channel_id=1, source_target_pairs={{0,12},{12,36},{24,0},{36,24},{1,13},{13,37},{25,1},{37,25},{2,14}... | collective-permute-start | bytes 221192 | tf_op jit(solution)/shard_map/ppermute | solution.py:32
  97.5 3.1 %collective-permute-done.7 = bf16[288,128]{1,0:T(8,128)(2,1)S(1)} collective-permute-done((bf16[288,128]{1,0:T(8,128)(2,1)S(1)}, bf16[288,128]{1,0:T(8,128)(2,1)S(1)}, u32[]{:S(2)}, u32[]{:S(2)}) %collective-permute-start.7) | collective-permute-done | bytes 73760 | tf_op jit(solution)/shard_map/ppermute | solution.py:32
  100.6 0.7 maximum_select_fusion.1
  101.3 40.1 %reduce-scatter.2.cloned.1.call-done = bf16[24,4096]{1,0:T(8,128)(2,1)} async-done(((bf16[288,4096]{1,0:T(8,128)(2,1)}), bf16[24,4096]{1,0:T(8,128)(2,1)}) %reduce-scatter.2.cloned.1.call-update) | async-done | bytes 196624 | tf_op jit(solution)/shard_map/reduce_scatter | solution.py:258
  141.4 10.5 %collective-permute-start.8 = (bf16[24,4096]{1,0:T(8,128)(2,1)}, bf16[24,4096]{1,0:T(8,128)(2,1)S(1)}, u32[]{:S(2)}, u32[]{:S(2)}) collective-permute-start(bf16[24,4096]{1,0:T(8,128)(2,1)} %reduce-scatter.2.cloned.1.call-done), channel_id=1, source_target_pairs={{0,0},{12,24},{24,12},{36,36},{1,1},{13,25},{25,13},{37,37},{2,2},... | collective-permute-start | bytes 589832 | tf_op jit(solution)/shard_map/ppermute | solution.py:32
  151.9 3.5 %collective-permute-done.8 = bf16[24,4096]{1,0:T(8,128)(2,1)S(1)} collective-permute-done((bf16[24,4096]{1,0:T(8,128)(2,1)}, bf16[24,4096]{1,0:T(8,128)(2,1)S(1)}, u32[]{:S(2)}, u32[]{:S(2)}) %collective-permute-start.8) | collective-permute-done | bytes 196640 | tf_op jit(solution)/shard_map/ppermute | solution.py:32
  155.5 0.7 copy.8
  (15 shorter events, 1.0 us)
Async XLA Ops:
  7.2 134.2 %reduce-scatter.2.cloned.1.call-start = ((), (), s32[]{:S(2)}) async-start(), calls=%async_computation.1 | async-start | bytes 2555904 | tf_op jit(solution)/shard_map/reduce_scatter | solution.py:258
  9.5 8.0 %collective-permute-start = (f16[24,4224]{1,0:T(8,128)(2,1)S(1)}, f16[24,4224]{1,0:T(8,128)(2,1)S(1)}, u32[]{:S(2)}, u32[]{:S(2)}) collective-permute-start(f16[24,4224]{1,0:T(8,128)(2,1)S(1)} %pad_maximum_fusion.4), channel_id=1, source_target_pairs={{0,0},{12,24},{24,12},{36,36},{1,1},{13,25},{25,13},{37,37},{2,2},... | collective-permute-start | bytes 608264 | tf_op jit(solution)/shard_map/ppermute | solution.py:32
  17.5 53.4 %collective-permute-start.3 = (bf16[3,4096,128]{2,1,0:T(8,128)(2,1)}, bf16[3,4096,128]{2,1,0:T(8,128)(2,1)S(1)}, u32[]{:S(2)}, u32[]{:S(2)}) collective-permute-start(bf16[3,4096,128]{2,1,0:T(8,128)(2,1)} %bitcast.2), channel_id=1, source_target_pairs={{0,588},{12,0},{24,36},{36,216},{192,12},{204,192},{216,228},{228,... | collective-permute-start | bytes 9437192 | tf_op jit(solution)/shard_map/ppermute | solution.py:32
  19.4 51.1 %collective-permute-start.1 = (f32[304,128]{1,0:T(8,128)}, f32[304,128]{1,0:T(8,128)S(1)}, u32[]{:S(2)}, u32[]{:S(2)}) collective-permute-start(f32[304,128]{1,0:T(8,128)} %get-tuple-element.17), channel_id=1, source_target_pairs={{0,0},{12,24},{24,12},{36,36},{1,1},{13,25},{25,13},{37,37},{2,2},... | collective-permute-start | bytes 466952 | tf_op jit(solution)/shard_map/ppermute | solution.py:32
  29.2 41.4 %collective-permute-start.2 = (f32[304,128]{1,0:T(8,128)S(1)}, f32[304,128]{1,0:T(8,128)S(1)}, u32[]{:S(2)}, u32[]{:S(2)}) collective-permute-start(f32[304,128]{1,0:T(8,128)S(1)} %get-tuple-element.18), channel_id=1, source_target_pairs={{0,24},{12,0},{24,36},{36,12},{1,25},{13,1},{25,37},{37,13},{2,26}... | collective-permute-start | bytes 466952 | tf_op jit(solution)/shard_map/ppermute | solution.py:32
  70.5 1.9 %copy-start = (bf16[4096,3,128]{2,0,1:T(8,128)(2,1)S(1)}, bf16[4096,3,128]{2,0,1:T(8,128)(2,1)}, u32[]{:S(2)}) copy-start(bf16[4096,3,128]{2,0,1:T(8,128)(2,1)} %param.6) | copy-start | bytes 9437188
  74.5 12.3 %collective-permute-start.5 = (bf16[4,8,256]{2,1,0:T(8,128)(2,1)S(1)}, bf16[4,8,256]{2,1,0:T(8,128)(2,1)S(1)}, u32[]{:S(2)}, u32[]{:S(2)}) collective-permute-start(bf16[4,8,256]{2,1,0:T(8,128)(2,1)S(1)} %get-tuple-element.25), channel_id=1, source_target_pairs={{12,24},{24,0},{36,12},{48,36},{60,72},{72,48},{84,60},{96,84},{10... | collective-permute-start | bytes 49160 | tf_op jit(solution)/shard_map/ppermute | solution.py:32
  82.9 3.8 %collective-permute-start.4 = (bf16[3,8,256]{2,1,0:T(8,128)(2,1)S(1)}, bf16[3,8,256]{2,1,0:T(8,128)(2,1)S(1)}, u32[]{:S(2)}, u32[]{:S(2)}) collective-permute-start(bf16[3,8,256]{2,1,0:T(8,128)(2,1)S(1)} %get-tuple-element.24), channel_id=1, source_target_pairs={{0,24},{12,36},{24,12},{36,48},{48,72},{60,84},{72,60},{84,96},{96... | collective-permute-start | bytes 36872 | tf_op jit(solution)/shard_map/ppermute | solution.py:32
  91.3 6.2 %collective-permute-start.6 = (bf16[288,128]{1,0:T(8,128)(2,1)S(1)}, bf16[288,128]{1,0:T(8,128)(2,1)S(1)}, u32[]{:S(2)}, u32[]{:S(2)}) collective-permute-start(bf16[288,128]{1,0:T(8,128)(2,1)S(1)} %get-tuple-element.30), channel_id=1, source_target_pairs={{0,0},{12,24},{24,12},{36,36},{1,1},{13,25},{25,13},{37,37},{2,2},... | collective-permute-start | bytes 221192 | tf_op jit(solution)/shard_map/ppermute | solution.py:32
  95.5 5.1 %collective-permute-start.7 = (bf16[288,128]{1,0:T(8,128)(2,1)S(1)}, bf16[288,128]{1,0:T(8,128)(2,1)S(1)}, u32[]{:S(2)}, u32[]{:S(2)}) collective-permute-start(bf16[288,128]{1,0:T(8,128)(2,1)S(1)} %get-tuple-element.31), channel_id=1, source_target_pairs={{0,12},{12,36},{24,0},{36,24},{1,13},{13,37},{25,1},{37,25},{2,14}... | collective-permute-start | bytes 221192 | tf_op jit(solution)/shard_map/ppermute | solution.py:32
  141.4 14.1 %collective-permute-start.8 = (bf16[24,4096]{1,0:T(8,128)(2,1)}, bf16[24,4096]{1,0:T(8,128)(2,1)S(1)}, u32[]{:S(2)}, u32[]{:S(2)}) collective-permute-start(bf16[24,4096]{1,0:T(8,128)(2,1)} %reduce-scatter.2.cloned.1.call-done), channel_id=1, source_target_pairs={{0,0},{12,24},{24,12},{36,36},{1,1},{13,25},{25,13},{37,37},{2,2},... | collective-permute-start | bytes 589832 | tf_op jit(solution)/shard_map/ppermute | solution.py:32
Sparse Core Ops, SparseCore 0:
  91.4 49.9 reduce-scatter.1

commit v7 on v6

v7 whole, which is shorter than its diff:
```python
import jax
import jax.numpy as jnp
from jax import lax
from jax.experimental import pallas as pl
from jax.experimental.pallas import tpu as pltpu
from jax.sharding import Mesh
from jax.sharding import PartitionSpec as P

CTX = ("yh", "x", "c")
TP = ("yl", "z")
HALO = 8
TOP = 13.0


def exchange(value, axes, sizes, route):
    total = 1
    for size in sizes:
        total *= size
    pairs = []
    for source in range(total):
        coords, rest = [], source
        for size in reversed(sizes):
            coords.append(rest % size)
            rest //= size
        target = route(*reversed(coords))
        if target is None:
            continue
        flat = 0
        for place, size in zip(target, sizes):
            flat = flat * size + place
        pairs.append((source, flat))
    return lax.ppermute(value, axes, pairs)


def vmem():
    return pl.BlockSpec(memory_space=pltpu.MemorySpace.VMEM)


def smem():
    return pl.BlockSpec(memory_space=pltpu.MemorySpace.SMEM)


def hbm():
    return pl.BlockSpec(memory_space=pltpu.MemorySpace.HBM)


PARAMS = pltpu.CompilerParams(vmem_limit_bytes=24 * 1024 * 1024)


def slots(upper_ref, lanes):
    upper = upper_ref[0]
    return pl.multiple_of(upper * lanes, lanes), pl.multiple_of((1 - upper) * lanes, lanes)


def side_by_side(mine_ref, theirs_ref, part, cut):
    return jnp.concatenate([mine_ref[part, cut], theirs_ref[part, cut]], axis=1)


def message_kernel(upper_ref, grad_ref, feat_ref, inner_ref, o_ref):
    count = grad_ref.shape[0] // 2
    begin = pl.multiple_of((1 - upper_ref[0]) * count, 16)
    o_ref[:count] = grad_ref[pl.ds(begin, count)].astype(o_ref.dtype)
    for part in range(3):
        o_ref[count + 3 * part : count + 3 * part + 3] = feat_ref[part]
    o_ref[count + 9 :] = inner_ref[...]


def message(upper, grad, feat, inner):
    rows = grad.shape[0] // 2 + 9 + inner.shape[0]
    return pl.pallas_call(
        message_kernel,
        grid=(1,),
        in_specs=[smem()] + [pl.BlockSpec(v.shape, lambda i, n=v.ndim: (0,) * n) for v in (grad, feat, inner)],
        out_specs=pl.BlockSpec((rows, grad.shape[1]), lambda i: (0, 0)),
        out_shape=jax.ShapeDtypeStruct((rows, grad.shape[1]), jnp.float32),
        compiler_params=PARAMS,
        name="message",
    )(upper, grad, feat, inner)


def project_kernel(upper_ref, x_ref, grad_ref, came_ref, mine_ref, theirs_ref, o_ref, head_ref, tail_ref):
    parts, depth, lanes = mine_ref.shape
    count = x_ref.shape[0]
    own, other = slots(upper_ref, lanes)
    scale = jnp.exp2(x_ref[:, depth : depth + 1].astype(jnp.float32) - TOP)
    block = min(depth, 1024)
    for j in range(parts):
        total = None
        for begin in range(0, depth, block):
            cut = slice(begin, begin + block)
            piece = jnp.dot(
                x_ref[:, cut],
                side_by_side(mine_ref, theirs_ref, j, cut),
                preferred_element_type=jnp.float32,
            )
            total = piece if total is None else total + piece
        total = total * scale
        for place, half in ((own, total[:, :lanes]), (other, total[:, lanes:])):
            spot = pl.ds(place, lanes)
            o_ref[j, :, spot] = half.astype(o_ref.dtype)
            head_ref[j, :, spot] = half[:HALO].astype(head_ref.dtype)
            tail_ref[j, :, spot] = half[count - HALO :].astype(tail_ref.dtype)
    begin = pl.multiple_of(upper_ref[0] * count, 16)
    head_ref[parts, :, pl.ds(own, lanes)] = grad_ref[pl.ds(begin, count)][:HALO]
    head_ref[parts, :, pl.ds(other, lanes)] = came_ref[:HALO].astype(head_ref.dtype)


def project(upper, rows, grad, came, mine, theirs):
    parts, _, lanes = mine.shape
    count = rows.shape[0]
    return pl.pallas_call(
        project_kernel,
        in_specs=[smem()] + [vmem()] * 5,
        out_specs=[vmem()] * 3,
        out_shape=[
            jax.ShapeDtypeStruct((parts, count, 2 * lanes), jnp.bfloat16),
            jax.ShapeDtypeStruct((parts + 1, HALO, 2 * lanes), jnp.bfloat16),
            jax.ShapeDtypeStruct((parts, HALO, 2 * lanes), jnp.bfloat16),
        ],
        compiler_params=PARAMS,
        name="project",
    )(upper, rows, grad, came, mine, theirs)


def causal(series, taps):
    total = taps[0:1] * series
    for offset in range(1, taps.shape[0]):
        total = total + taps[offset : offset + 1] * pltpu.roll(series, offset, 0)
    return total


def adjoint(series, taps):
    total = taps[0:1] * series
    for offset in range(1, taps.shape[0]):
        total = total + taps[offset : offset + 1] * pltpu.roll(series, series.shape[0] - offset, 0)
    return total


def mix_kernel(
    upper_ref, proj_ref, prev_ref, next_ref, grad_ref, feat_ref, inner_ref, came_ref, mine_ref, theirs_ref,
    kept_ref, sent_ref, o_ref, back, o_buf, sems,
):
    parts, depth, lanes = mine_ref.shape
    count = proj_ref.shape[1]
    last = HALO + count
    steps = sems.shape[0]
    block = depth // steps
    own, other = slots(upper_ref, lanes)
    begin = pl.multiple_of(upper_ref[0] * count, 16)
    taps = came_ref[count:]
    sides = (
        (own, grad_ref[pl.ds(begin, count)], [feat_ref[part] for part in range(parts)], inner_ref[...], kept_ref),
        (other, came_ref[:count], [taps[3 * part : 3 * part + 3] for part in range(parts)], taps[9:], sent_ref),
    )
    for side, (place, here, feat, inner_taps, gated_ref) in enumerate(sides):
        spot = pl.ds(place, lanes)
        cut = slice(side * lanes, (side + 1) * lanes)

        def window(part):
            rows = [prev_ref[part, :, spot], proj_ref[part, :, spot], next_ref[part, :, spot]]
            return jnp.concatenate(rows, axis=0).astype(jnp.float32)

        query = causal(window(0), feat[0])
        key = causal(window(1), feat[1])
        value = causal(window(2), feat[2])
        inner = causal(key * value, inner_taps)
        gated_ref[...] = (query * inner)[HALO:last].astype(gated_ref.dtype)
        grad_next = next_ref[parts, :, spot].astype(jnp.float32)
        grad = jnp.concatenate([jnp.zeros_like(grad_next), here.astype(jnp.float32), grad_next], axis=0)
        mixed = adjoint(grad * query, inner_taps)
        back[0, :, cut] = adjoint(grad * inner, feat[0])[HALO:last].astype(back.dtype)
        back[1, :, cut] = adjoint(mixed * value, feat[1])[HALO:last].astype(back.dtype)
        back[2, :, cut] = adjoint(mixed * key, feat[2])[HALO:last].astype(back.dtype)
    contract = (((1,), (1,)), ((), ()))
    leaving = []
    for i in range(steps):
        cut = slice(i * block, (i + 1) * block)
        total = None
        for part in range(parts):
            piece = lax.dot_general(
                back[part],
                side_by_side(mine_ref, theirs_ref, part, cut),
                contract,
                preferred_element_type=jnp.float32,
            )
            total = piece if total is None else total + piece
        o_buf[:, cut] = total.astype(o_buf.dtype)
        leaving.append(pltpu.make_async_copy(o_buf.at[:, cut], o_ref.at[:, cut], sems.at[i]))
        leaving[-1].start()
    for copy in leaving:
        copy.wait()


def mix(upper, proj, prev, following, grad, feat, inner, came, mine, theirs):
    parts, depth, lanes = mine.shape
    count = proj.shape[1]
    steps = 8
    half = jax.ShapeDtypeStruct((count, lanes), jnp.bfloat16)
    return pl.pallas_call(
        mix_kernel,
        in_specs=[smem()] + [vmem()] * 9,
        out_specs=[vmem(), vmem(), hbm()],
        out_shape=[half, half, pltpu.HBM((count, depth), jnp.bfloat16)],
        scratch_shapes=[
            pltpu.VMEM((parts, count, 2 * lanes), jnp.bfloat16),
            pltpu.VMEM((count, depth), jnp.bfloat16),
            pltpu.SemaphoreType.DMA((steps,)),
        ],
        compiler_params=PARAMS,
        name="mix",
    )(upper, proj, prev, following, grad, feat, inner, came, mine, theirs)


def encode(tokens):
    wide = tokens.astype(jnp.float32)
    peak = jnp.max(jnp.abs(wide), axis=1, keepdims=True)
    power = jnp.clip(jnp.floor(jnp.log2(jnp.maximum(peak, 1e-37))), -110.0, 110.0)
    scaled = wide * jnp.exp2(TOP - power)
    return jnp.concatenate(
        [scaled, jnp.broadcast_to(power, (tokens.shape[0], 128))], axis=1
    ).astype(jnp.float16)


def build(sizes):
    ring = sizes[0] * 2

    strips = sizes[0] * sizes[1] * 4

    def along(value, step):
        def route(yh, x, c, yl):
            strip = ((yh * sizes[1] + x) * 2 + c) * 2 + yl + step
            if not 0 <= strip < strips:
                return None
            return (strip // 4 // sizes[1], strip // 4 % sizes[1], strip // 2 % 2, strip % 2)

        return exchange(value, ("yh", "x", "c", "yl"), (sizes[0], sizes[1], 2, 2), route)

    def across(value):
        return lax.ppermute(value, "yl", [(0, 1), (1, 0)])

    def local(tokens, proj_weight, feat_taps, inner_taps, grad_out):
        upper = lax.axis_index("yl")
        flag = upper.astype(jnp.int32).reshape(1)

        note = message(flag, grad_out, feat_taps, inner_taps)
        planes = proj_weight.transpose(1, 0, 2)
        rows, sent, note = lax.optimization_barrier((encode(tokens), planes, note))
        came = across(note)

        def beside(yh, c, yl):
            place = (yh * 2 + yl + (1 if c else ring - 1)) % ring
            return (place // 2, c, place % 2)

        theirs = exchange(sent, ("yh", "c", "yl"), (sizes[0], 2, 2), beside)
        gathered = lax.all_gather(rows, "z", axis=0, tiled=True)
        gathered, came = lax.optimization_barrier((gathered, came))
        gathered = gathered.astype(jnp.bfloat16)

        proj, head, tail = project(flag, gathered, grad_out, came, planes, theirs)
        prev = along(tail, 1)
        following = along(head, -1)
        kept, leaving, spread = mix(
            flag, proj, prev, following, grad_out, feat_taps, inner_taps, came, planes, theirs
        )
        grad_tokens = lax.psum_scatter(spread, "z", scatter_dimension=0, tiled=True)
        arrived = across(leaving)
        gated = jnp.where(
            upper == 0,
            jnp.concatenate([kept, arrived], axis=0),
            jnp.concatenate([arrived, kept], axis=0),
        )
        return (gated, grad_tokens)

    return local


def solution(mesh):
    sizes = (4, 4, 2, 2, 12)
    grid = Mesh(mesh.devices.reshape(sizes), CTX + TP)
    in_specs = (
        P(CTX + TP, None),
        P(None, None, TP),
        P(None, None, TP),
        P(None, TP),
        P(CTX, TP),
    )
    out_specs = (P(CTX, TP), P(CTX + TP, None))
    return jax.shard_map(build(sizes), mesh=grid, in_specs=in_specs, out_specs=out_specs, check_vma=False)
```

time: 164 us -> 151 us (0.921)
  the two profiles are of different devices: /device:TPU:1 before, /device:TPU:10 now
where the time goes in v7:
time: 151 us
  waiting for transfers between devices  58.3 us (39%)
  blocking collectives  49.8 us (33%)
  starting transfers between devices  15.6 us (10%)
  between operations  14.2 us (9%)
  Pallas kernels  6.04 us (4%)
  local copies, waits for them, and re-layouts  3.95 us (3%)
  other arithmetic  3.15 us (2%)
    reduce_scatter x1, waiting for transfers between devices, local(): grad_tokens = lax.psum_scatter(spread, 'z', scatter_dimension=0, tiled=True)  51.6 us
    all_gather x1, blocking collectives, local(): gathered = lax.all_gather(rows, 'z', axis=0, tiled=True)  49.8 us
    ppermute x3, starting transfers between devices, exchange(): return lax.ppermute(value, axes, pairs)  7.92 us
    ppermute x2, starting transfers between devices, across(): return lax.ppermute(value, 'yl', [(0, 1), (1, 0)])  7.65 us
    pallas_call x1, Pallas kernels, mix(): pl.pallas_call(mix_kernel, in_specs=[smem()] + [vmem()] * 9, out_specs=[v...  3.97 us
    ppermute x2, waiting for transfers between devices, across(): return lax.ppermute(value, 'yl', [(0, 1), (1, 0)])  3.97 us
    unnamed x14, local copies, waits for them, and re-layouts  3.88 us
  transfers between devices with their start and end apart: 6, of which 3 were waited for; matrix products, arithmetic and copies ran while one was open for 1% of the time, Pallas kernels for 0%

profile of v7, /device:TPU:10, one launch (start us, length us, event | category | flops | bytes accessed | tf_op | source)
XLA Modules:
  0.0 151.0 jit_solution(7659183353633416814)
XLA Ops:
  7.2 0.0 reduce-scatter.2.cloned.1.call-start
  7.2 1.1 fusion
  8.3 1.1 fusion.1
  9.3 0.1 broadcast_in_dim.2
  9.4 0.1 pad_maximum_fusion
  9.5 0.0 copy-start.1
  9.5 0.9 copy-done.1
  10.4 0.7 copy-done.3
  11.1 0.7 copy-done.5
  11.8 2.4 %collective-permute-start.1 = (bf16[3,4096,128]{2,1,0:T(8,128)(2,1)}, bf16[3,4096,128]{2,1,0:T(8,128)(2,1)S(1)}, u32[]{:S(2)}, u32[]{:S(2)}) collective-permute-start(bf16[3,4096,128]{2,1,0:T(8,128)(2,1)} %bitcast.2), channel_id=1, source_target_pairs={{0,588},{12,0},{24,36},{36,216},{192,12},{204,192},{216,228},{228,... | collective-permute-start | bytes 9437192 | tf_op jit(solution)/shard_map/ppermute | solution.py:32
  14.2 5.4 %collective-permute-start = (f32[304,128]{1,0:T(8,128)S(1)}, f32[304,128]{1,0:T(8,128)S(1)}, u32[]{:S(2)}, u32[]{:S(2)}) collective-permute-start(f32[304,128]{1,0:T(8,128)S(1)} %message.1), channel_id=1, source_target_pairs={{0,12},{12,0},{1,13},{13,1},{2,14},{14,2},{3,15},{15,3},{4,16},{16... | collective-permute-start | bytes 466952 | tf_op jit(solution)/shard_map/ppermute | solution.py:239
  19.5 49.8 %all-gather.1 = f16[288,4224]{1,0:T(8,128)(2,1)S(1)} all-gather(f16[24,4224]{1,0:T(8,128)(2,1)S(1)} %pad_maximum_fusion), channel_id=1, replica_groups=mesh['yh'=4,'x'=4,'c'=2,'yl'=2,'z'=12] {'z'}, dimensions={0}, use_global_device_ids=true | all-gather | bytes 2635776 | tf_op jit(solution)/shard_map/all_gather | solution.py:255
  69.3 0.3 convert_element_type.8.x_ref
  69.6 1.6 %copy-done = bf16[4096,3,128]{2,0,1:T(8,128)(2,1)S(1)} copy-done((bf16[4096,3,128]{2,0,1:T(8,128)(2,1)S(1)}, bf16[4096,3,128]{2,0,1:T(8,128)(2,1)}, u32[]{:S(2)}) %copy-start) | copy-done | bytes 3145752
  71.2 2.1 %project.1 = (bf16[3,288,256]{2,1,0:T(8,128)(2,1)S(1)}, bf16[4,8,256]{2,1,0:T(8,128)(2,1)S(1)}, bf16[3,8,256]{2,1,0:T(8,128)(2,1)S(1)}) custom-call(s32[1]{0:T(128)} %bitcast.upper_ref, bf16[288,4224]{1,0:T(8,128)(2,1)S(1)} %convert_element_type.8.x_ref, bf16[576,128]{1,0:T(8,128)(2,1)S(1)} %copy-done.2, f32[304,128]{1,0:T(8,128)S(1)} %collective-permute-done.came_ref, ...), custom_call_target="tpu_custom_call" | custom-call | tf_op jit(solution)/shard_map/project/pallas_call | solution.py:111
  73.3 2.8 %collective-permute-start.3 = (bf16[4,8,256]{2,1,0:T(8,128)(2,1)S(1)}, bf16[4,8,256]{2,1,0:T(8,128)(2,1)S(1)}, u32[]{:S(2)}, u32[]{:S(2)}) collective-permute-start(bf16[4,8,256]{2,1,0:T(8,128)(2,1)S(1)} %get-tuple-element.20), channel_id=1, source_target_pairs={{12,0},{24,12},{36,24},{48,36},{60,48},{72,60},{84,72},{96,84},{10... | collective-permute-start | bytes 49160 | tf_op jit(solution)/shard_map/ppermute | solution.py:32
  76.0 2.8 %collective-permute-start.2 = (bf16[3,8,256]{2,1,0:T(8,128)(2,1)S(1)}, bf16[3,8,256]{2,1,0:T(8,128)(2,1)S(1)}, u32[]{:S(2)}, u32[]{:S(2)}) collective-permute-start(bf16[3,8,256]{2,1,0:T(8,128)(2,1)S(1)} %get-tuple-element.19), channel_id=1, source_target_pairs={{0,12},{12,24},{24,36},{36,48},{48,60},{60,72},{72,84},{84,96},{96... | collective-permute-start | bytes 36872 | tf_op jit(solution)/shard_map/ppermute | solution.py:32
  78.8 2.8 %collective-permute-done.2.prev_ref = bf16[3,8,256]{2,1,0:T(8,128)(2,1)S(1)} collective-permute-done((bf16[3,8,256]{2,1,0:T(8,128)(2,1)S(1)}, bf16[3,8,256]{2,1,0:T(8,128)(2,1)S(1)}, u32[]{:S(2)}, u32[]{:S(2)}) %collective-permute-start.2) | collective-permute-done | bytes 12320 | tf_op jit(solution)/shard_map/ppermute | solution.py:32
  81.6 4.0 %mix.1 = (bf16[288,128]{1,0:T(8,128)(2,1)S(1)}, bf16[288,128]{1,0:T(8,128)(2,1)S(1)}, bf16[288,4096]{1,0:T(8,128)(2,1)}) custom-call(s32[1]{0:T(128)} %bitcast.upper_ref, bf16[3,288,256]{2,1,0:T(8,128)(2,1)S(1)} %get-tuple-element.18.proj_ref, bf16[3,8,256]{2,1,0:T(8,128)(2,1)S(1)} %collective-permute-done.2.prev_ref, ...), custom_call_target="tpu_custom_call" | custom-call | tf_op jit(solution)/shard_map/mix/pallas_call | solution.py:199
  85.6 0.0 reduce-scatter.2.cloned.1.call-update
  85.6 2.3 %collective-permute-start.4 = (bf16[288,128]{1,0:T(8,128)(2,1)S(1)}, bf16[288,128]{1,0:T(8,128)(2,1)S(1)}, u32[]{:S(2)}, u32[]{:S(2)}) collective-permute-start(bf16[288,128]{1,0:T(8,128)(2,1)S(1)} %get-tuple-element.22), channel_id=1, source_target_pairs={{0,12},{12,0},{1,13},{13,1},{2,14},{14,2},{3,15},{15,3},{4,16},{16... | collective-permute-start | bytes 221192 | tf_op jit(solution)/shard_map/ppermute | solution.py:239
  87.9 4.0 %collective-permute-done.4 = bf16[288,128]{1,0:T(8,128)(2,1)S(1)} collective-permute-done((bf16[288,128]{1,0:T(8,128)(2,1)S(1)}, bf16[288,128]{1,0:T(8,128)(2,1)S(1)}, u32[]{:S(2)}, u32[]{:S(2)}) %collective-permute-start.4) | collective-permute-done | bytes 73760 | tf_op jit(solution)/shard_map/ppermute | solution.py:239
  91.9 0.7 maximum_select_fusion
  92.6 51.6 %reduce-scatter.2.cloned.1.call-done = bf16[24,4096]{1,0:T(8,128)(2,1)} async-done(((bf16[288,4096]{1,0:T(8,128)(2,1)}), bf16[24,4096]{1,0:T(8,128)(2,1)}) %reduce-scatter.2.cloned.1.call-update) | async-done | bytes 196624 | tf_op jit(solution)/shard_map/reduce_scatter | solution.py:265
  (14 shorter events, 0.1 us)
Async XLA Ops:
  7.2 137.0 %reduce-scatter.2.cloned.1.call-start = ((), (), s32[]{:S(2)}) async-start(), calls=%async_computation.1 | async-start | bytes 2555904 | tf_op jit(solution)/shard_map/reduce_scatter | solution.py:265
  9.5 0.9 copy-start.1
  10.4 0.7 copy-start.3
  11.1 0.7 copy-start.5
  11.8 57.8 %collective-permute-start.1 = (bf16[3,4096,128]{2,1,0:T(8,128)(2,1)}, bf16[3,4096,128]{2,1,0:T(8,128)(2,1)S(1)}, u32[]{:S(2)}, u32[]{:S(2)}) collective-permute-start(bf16[3,4096,128]{2,1,0:T(8,128)(2,1)} %bitcast.2), channel_id=1, source_target_pairs={{0,588},{12,0},{24,36},{36,216},{192,12},{204,192},{216,228},{228,... | collective-permute-start | bytes 9437192 | tf_op jit(solution)/shard_map/ppermute | solution.py:32
  14.2 55.2 %collective-permute-start = (f32[304,128]{1,0:T(8,128)S(1)}, f32[304,128]{1,0:T(8,128)S(1)}, u32[]{:S(2)}, u32[]{:S(2)}) collective-permute-start(f32[304,128]{1,0:T(8,128)S(1)} %message.1), channel_id=1, source_target_pairs={{0,12},{12,0},{1,13},{13,1},{2,14},{14,2},{3,15},{15,3},{4,16},{16... | collective-permute-start | bytes 466952 | tf_op jit(solution)/shard_map/ppermute | solution.py:239
  69.3 1.9 %copy-start = (bf16[4096,3,128]{2,0,1:T(8,128)(2,1)S(1)}, bf16[4096,3,128]{2,0,1:T(8,128)(2,1)}, u32[]{:S(2)}) copy-start(bf16[4096,3,128]{2,0,1:T(8,128)(2,1)} %param.6) | copy-start | bytes 9437188
  69.3 1.9 %copy-start.2 = (bf16[576,128]{1,0:T(8,128)(2,1)S(1)}, bf16[576,128]{1,0:T(8,128)(2,1)}, u32[]{:S(2)}) copy-start(bf16[576,128]{1,0:T(8,128)(2,1)} %grad_ref.5) | copy-start | bytes 442372
  69.6 12.0 %copy-start.4 = (f32[3,3,128]{2,1,0:T(4,128)S(1)}, f32[3,3,128]{2,1,0:T(4,128)}, u32[]{:S(2)}) copy-start(f32[3,3,128]{2,1,0:T(4,128)} %feat_ref.3) | copy-start | bytes 13828
  69.6 12.0 %copy-start.6 = (f32[7,128]{1,0:T(8,128)S(1)}, f32[7,128]{1,0:T(8,128)}, u32[]{:S(2)}) copy-start(f32[7,128]{1,0:T(8,128)} %inner_ref.3) | copy-start | bytes 10756
  73.3 8.4 %collective-permute-start.3 = (bf16[4,8,256]{2,1,0:T(8,128)(2,1)S(1)}, bf16[4,8,256]{2,1,0:T(8,128)(2,1)S(1)}, u32[]{:S(2)}, u32[]{:S(2)}) collective-permute-start(bf16[4,8,256]{2,1,0:T(8,128)(2,1)S(1)} %get-tuple-element.20), channel_id=1, source_target_pairs={{12,0},{24,12},{36,24},{48,36},{60,48},{72,60},{84,72},{96,84},{10... | collective-permute-start | bytes 49160 | tf_op jit(solution)/shard_map/ppermute | solution.py:32
  76.0 5.6 %collective-permute-start.2 = (bf16[3,8,256]{2,1,0:T(8,128)(2,1)S(1)}, bf16[3,8,256]{2,1,0:T(8,128)(2,1)S(1)}, u32[]{:S(2)}, u32[]{:S(2)}) collective-permute-start(bf16[3,8,256]{2,1,0:T(8,128)(2,1)S(1)} %get-tuple-element.19), channel_id=1, source_target_pairs={{0,12},{12,24},{24,36},{36,48},{48,60},{60,72},{72,84},{84,96},{96... | collective-permute-start | bytes 36872 | tf_op jit(solution)/shard_map/ppermute | solution.py:32
  85.6 6.2 %collective-permute-start.4 = (bf16[288,128]{1,0:T(8,128)(2,1)S(1)}, bf16[288,128]{1,0:T(8,128)(2,1)S(1)}, u32[]{:S(2)}, u32[]{:S(2)}) collective-permute-start(bf16[288,128]{1,0:T(8,128)(2,1)S(1)} %get-tuple-element.22), channel_id=1, source_target_pairs={{0,12},{12,0},{1,13},{13,1},{2,14},{14,2},{3,15},{15,3},{4,16},{16... | collective-permute-start | bytes 221192 | tf_op jit(solution)/shard_map/ppermute | solution.py:239
Sparse Core Ops, SparseCore 0:
  85.8 58.3 reduce-scatter.1

commit v8 on v7

--- a/solution.py
+++ b/solution.py
@@ -10,6 +10,8 @@
 TP = ("yl", "z")
 HALO = 8
 TOP = 13.0
+SHARD = 24
+FOLD = 16
 
 
 def exchange(value, axes, sizes, route):
@@ -138,15 +140,17 @@
 
 def mix_kernel(
     upper_ref, proj_ref, prev_ref, next_ref, grad_ref, feat_ref, inner_ref, came_ref, mine_ref, theirs_ref,
-    kept_ref, sent_ref, o_ref, back, o_buf, sems,
+    kept_ref, sent_ref, o_ref, back, extra, o_buf, sems,
 ):
     parts, depth, lanes = mine_ref.shape
     count = proj_ref.shape[1]
     last = HALO + count
-    steps = sems.shape[0]
-    block = depth // steps
+    block = depth // 8
     own, other = slots(upper_ref, lanes)
     begin = pl.multiple_of(upper_ref[0] * count, 16)
+    shards = count // SHARD
+    body = SHARD - 1
+    main = shards * body
     taps = came_ref[count:]
     sides = (
         (own, grad_ref[pl.ds(begin, count)], [feat_ref[part] for part in range(parts)], inner_ref[...], kept_ref),
@@ -168,25 +172,38 @@
         grad_next = next_ref[parts, :, spot].astype(jnp.float32)
         grad = jnp.concatenate([jnp.zeros_like(grad_next), here.astype(jnp.float32), grad_next], axis=0)
         mixed = adjoint(grad * query, inner_taps)
-        back[0, :, cut] = adjoint(grad * inner, feat[0])[HALO:last].astype(back.dtype)
-        back[1, :, cut] = adjoint(mixed * value, feat[1])[HALO:last].astype(back.dtype)
-        back[2, :, cut] = adjoint(mixed * key, feat[2])[HALO:last].astype(back.dtype)
+        for part, series in enumerate((grad * inner, mixed * value, mixed * key)):
+            rows = adjoint(series, feat[part])[HALO:last]
+            for k in range(shards):
+                first = k * SHARD
+                back[part, k * body : (k + 1) * body, cut] = rows[first : first + body]
+                back[part, main + k : main + k + 1, cut] = rows[first + body : first + SHARD]
+    left = [back[part].astype(jnp.bfloat16) for part in range(parts)]
     contract = (((1,), (1,)), ((), ()))
+    extra[...] = jnp.zeros_like(extra)
     leaving = []
-    for i in range(steps):
+    wide = depth // FOLD
+    for i in range(depth // block):
         cut = slice(i * block, (i + 1) * block)
         total = None
         for part in range(parts):
             piece = lax.dot_general(
-                back[part],
+                left[part],
                 side_by_side(mine_ref, theirs_ref, part, cut),
                 contract,
                 preferred_element_type=jnp.float32,
             )
             total = piece if total is None else total + piece
-        o_buf[:, cut] = total.astype(o_buf.dtype)
+        o_buf[:, cut] = total[:main].astype(o_buf.dtype)
         leaving.append(pltpu.make_async_copy(o_buf.at[:, cut], o_ref.at[:, cut], sems.at[i]))
         leaving[-1].start()
+        for k in range(shards):
+            for fold in range(block // wide):
+                line = k * body + i * (block // wide) + fold
+                extra[line : line + 1] = total[main + k : main + k + 1, fold * wide : (fold + 1) * wide]
+    o_buf[:, depth:] = extra[...].astype(o_buf.dtype)
+    leaving.append(pltpu.make_async_copy(o_buf.at[:, depth:], o_ref.at[:, depth:], sems.at[8]))
+    leaving[-1].start()
     for copy in leaving:
         copy.wait()
 
@@ -194,17 +211,18 @@
 def mix(upper, proj, prev, following, grad, feat, inner, came, mine, theirs):
     parts, depth, lanes = mine.shape
     count = proj.shape[1]
-    steps = 8
     half = jax.ShapeDtypeStruct((count, lanes), jnp.bfloat16)
+    main = count // SHARD * (SHARD - 1)
     return pl.pallas_call(
         mix_kernel,
         in_specs=[smem()] + [vmem()] * 9,
         out_specs=[vmem(), vmem(), hbm()],
-        out_shape=[half, half, pltpu.HBM((count, depth), jnp.bfloat16)],
+        out_shape=[half, half, pltpu.HBM((main, depth + depth // FOLD), jnp.bfloat16)],
         scratch_shapes=[
-            pltpu.VMEM((parts, count, 2 * lanes), jnp.bfloat16),
-            pltpu.VMEM((count, depth), jnp.bfloat16),
-            pltpu.SemaphoreType.DMA((steps,)),
+            pltpu.VMEM((parts, count, 2 * lanes), jnp.float32),
+            pltpu.VMEM((main, depth // FOLD), jnp.float32),
+            pltpu.VMEM((main, depth + depth // FOLD), jnp.bfloat16),
+            pltpu.SemaphoreType.DMA((9,)),
         ],
         compiler_params=PARAMS,
         name="mix",
@@ -262,8 +280,13 @@
         kept, leaving, spread = mix(
             flag, proj, prev, following, grad_out, feat_taps, inner_taps, came, planes, theirs
         )
-        grad_tokens = lax.psum_scatter(spread, "z", scatter_dimension=0, tiled=True)
         arrived = across(leaving)
+        summed = lax.psum_scatter(spread, "z", scatter_dimension=0, tiled=True)
+        summed = lax.optimization_barrier(summed)
+        depth = tokens.shape[1]
+        grad_tokens = jnp.concatenate(
+            [summed[:, :depth], summed[:FOLD, depth:].reshape(1, depth)], axis=0
+        )
         gated = jnp.where(
             upper == 0,
             jnp.concatenate([kept, arrived], axis=0),

time: 151 us -> 131 us (0.87)
  the two profiles are of different devices: /device:TPU:10 before, /device:TPU:104 now
where the time goes in v8:
time: 131 us; the launch traced here: 130 us
  blocking collectives  82.1 us (63%)
  starting transfers between devices  19.8 us (15%)
  local copies, waits for them, and re-layouts  10.9 us (8%)
  Pallas kernels  6.91 us (5%)
  waiting for transfers between devices  5.28 us (4%)
  other arithmetic  3.86 us (3%)
  between operations  1.51 us (1%)
    all_gather x1, blocking collectives, local(): gathered = lax.all_gather(rows, 'z', axis=0, tiled=True)  47.5 us
    unnamed x1, blocking collectives  34.6 us
    unnamed x32, local copies, waits for them, and re-layouts  10.8 us
    ppermute x3, starting transfers between devices, exchange(): return lax.ppermute(value, axes, pairs)  10.1 us
    ppermute x2, starting transfers between devices, across(): return lax.ppermute(value, 'yl', [(0, 1), (1, 0)])  7.02 us
    pallas_call x1, Pallas kernels, mix(): pl.pallas_call(mix_kernel, in_specs=[smem()] + [vmem()] * 9, out_specs=[v...  4.78 us
    unnamed x1, waiting for transfers between devices  3.54 us
    unnamed x1, starting transfers between devices  2.69 us
  transfers between devices with their start and end apart: 6, of which 2 were waited for; matrix products, arithmetic and copies ran while one was open for 28% of the time, Pallas kernels for 0%

profile of v8, /device:TPU:104, one launch (start us, length us, event | category | flops | bytes accessed | tf_op | source)
XLA Modules:
  0.0 130.3 jit_solution(251684095665662803)
XLA Ops:
  0.6 1.1 fusion.1
  1.7 1.1 fusion.2
  2.9 0.9 copy-done.3
  3.8 0.7 copy-done.7
  5.2 3.3 %collective-permute-start.1 = (bf16[3,4096,128]{2,1,0:T(8,128)(2,1)}, bf16[3,4096,128]{2,1,0:T(8,128)(2,1)S(1)}, u32[]{:S(2)}, u32[]{:S(2)}) collective-permute-start(bf16[3,4096,128]{2,1,0:T(8,128)(2,1)} %bitcast.9), channel_id=1, source_target_pairs={{0,588},{12,0},{24,36},{36,216},{192,12},{204,192},{216,228},{228,... | collective-permute-start | bytes 9437192 | tf_op jit(solution)/shard_map/ppermute | solution.py:34
  8.5 2.4 %collective-permute-start = (f32[304,128]{1,0:T(8,128)S(1)}, f32[304,128]{1,0:T(8,128)S(1)}, u32[]{:S(2)}, u32[]{:S(2)}) collective-permute-start(f32[304,128]{1,0:T(8,128)S(1)} %message.1), channel_id=1, source_target_pairs={{0,12},{12,0},{1,13},{13,1},{2,14},{14,2},{3,15},{15,3},{4,16},{16... | collective-permute-start | bytes 466952 | tf_op jit(solution)/shard_map/ppermute | solution.py:257
  10.8 47.5 %all-gather.1 = f16[288,4224]{1,0:T(8,128)(2,1)S(1)} all-gather(f16[24,4224]{1,0:T(8,128)(2,1)S(1)} %pad_maximum_fusion), channel_id=1, replica_groups=mesh['yh'=4,'x'=4,'c'=2,'yl'=2,'z'=12] {'z'}, dimensions={0}, use_global_device_ids=true | all-gather | bytes 2635776 | tf_op jit(solution)/shard_map/all_gather | solution.py:273
  58.7 1.6 %copy-done = bf16[4096,3,128]{2,0,1:T(8,128)(2,1)S(1)} copy-done((bf16[4096,3,128]{2,0,1:T(8,128)(2,1)S(1)}, bf16[4096,3,128]{2,0,1:T(8,128)(2,1)}, u32[]{:S(2)}) %copy-start) | copy-done | bytes 3145752
  60.3 2.1 %project.1 = (bf16[3,288,256]{2,1,0:T(8,128)(2,1)S(1)}, bf16[4,8,256]{2,1,0:T(8,128)(2,1)S(1)}, bf16[3,8,256]{2,1,0:T(8,128)(2,1)S(1)}) custom-call(s32[1]{0:T(128)} %bitcast.upper_ref, bf16[288,4224]{1,0:T(8,128)(2,1)S(1)} %convert_element_type.8.x_ref, bf16[576,128]{1,0:T(8,128)(2,1)S(1)} %copy-done.4, f32[304,128]{1,0:T(8,128)S(1)} %collective-permute-done.came_ref, ...), custom_call_target="tpu_custom_call" | custom-call | tf_op jit(solution)/shard_map/project/pallas_call | solution.py:113
  62.4 0.8 copy-done.5
  63.2 4.9 %collective-permute-start.3 = (bf16[4,8,256]{2,1,0:T(8,128)(2,1)S(1)}, bf16[4,8,256]{2,1,0:T(8,128)(2,1)S(1)}, u32[]{:S(2)}, u32[]{:S(2)}) collective-permute-start(bf16[4,8,256]{2,1,0:T(8,128)(2,1)S(1)} %get-tuple-element.20), channel_id=1, source_target_pairs={{12,0},{24,12},{36,24},{48,36},{60,48},{72,60},{84,72},{96,84},{10... | collective-permute-start | bytes 49160 | tf_op jit(solution)/shard_map/ppermute | solution.py:34
  68.1 1.9 %collective-permute-start.2 = (bf16[3,8,256]{2,1,0:T(8,128)(2,1)S(1)}, bf16[3,8,256]{2,1,0:T(8,128)(2,1)S(1)}, u32[]{:S(2)}, u32[]{:S(2)}) collective-permute-start(bf16[3,8,256]{2,1,0:T(8,128)(2,1)S(1)} %get-tuple-element.19), channel_id=1, source_target_pairs={{0,12},{12,24},{24,36},{36,48},{48,60},{60,72},{72,84},{84,96},{96... | collective-permute-start | bytes 36872 | tf_op jit(solution)/shard_map/ppermute | solution.py:34
  70.0 1.3 dynamic-slice.4
  72.0 1.7 %collective-permute-done.2.prev_ref = bf16[3,8,256]{2,1,0:T(8,128)(2,1)S(1)} collective-permute-done((bf16[3,8,256]{2,1,0:T(8,128)(2,1)S(1)}, bf16[3,8,256]{2,1,0:T(8,128)(2,1)S(1)}, u32[]{:S(2)}, u32[]{:S(2)}) %collective-permute-start.2) | collective-permute-done | bytes 12320 | tf_op jit(solution)/shard_map/ppermute | solution.py:34
  74.3 1.9 %copy-done.2 = bf16[3,4096,128]{2,1,0:T(8,128)(2,1)S(1)} copy-done((bf16[3,4096,128]{2,1,0:T(8,128)(2,1)S(1)}, bf16[3,4096,128]{2,1,0:T(8,128)(2,1)}, u32[]{:S(2)}) %copy-start.2) | copy-done | bytes 3145752
  76.2 1.0 copy-done.6
  77.2 0.7 copy-done.12
  77.9 4.8 %mix.1 = (bf16[288,128]{1,0:T(8,128)(2,1)S(1)}, bf16[288,128]{1,0:T(8,128)(2,1)}, bf16[276,4352]{1,0:T(8,128)(2,1)}) custom-call(s32[1]{0:T(128)} %bitcast.upper_ref, bf16[3,288,256]{2,1,0:T(8,128)(2,1)S(1)} %copy-done.6, bf16[3,8,256]{2,1,0:T(8,128)(2,1)S(1)} %copy-done.12, bf16[4,8,256]{2,1,0:T(8,128)(2,1)S(1)} %collective-permute-done.3.next_ref, ...), custom_call_target="tpu_custom_call" | custom-call | tf_op jit(solution)/shard_map/mix/pallas_call | solution.py:216
  82.7 4.7 %collective-permute-start.4 = (bf16[288,128]{1,0:T(8,128)(2,1)}, bf16[288,128]{1,0:T(8,128)(2,1)S(1)}, u32[]{:S(2)}, u32[]{:S(2)}) collective-permute-start(bf16[288,128]{1,0:T(8,128)(2,1)} %get-tuple-element.22), channel_id=1, source_target_pairs={{0,12},{12,0},{1,13},{13,1},{2,14},{14,2},{3,15},{15,3},{4,16},{16... | collective-permute-start | bytes 221192 | tf_op jit(solution)/shard_map/ppermute | solution.py:257
  87.4 34.6 %fusion = bf16[24,4352]{1,0:T(8,128)(2,1)S(1)} fusion(bf16[276,4352]{1,0:T(8,128)(2,1)} %get-tuple-element.23), kind=kCustom, calls=%all-reduce-scatter | all-reduce-scatter fusion | flops 1253377 | bytes 2615296
  122.0 2.7 %collective-permute-start.5 = (bf16[11,4352]{1,0:T(8,128)(2,1)S(1)}, bf16[11,4352]{1,0:T(8,128)(2,1)S(1)}, u32[]{:S(2)}, u32[]{:S(2)}) collective-permute-start(bf16[11,4352]{1,0:T(8,128)(2,1)S(1)} %slice.10), channel_id=1, source_target_pairs={{0,1},{1,2},{2,3},{3,4},{4,5},{5,6},{6,7},{7,8},{8,9},{9,10},{10,1... | collective-permute-start | bytes 287240
  124.7 0.7 maximum_select_fusion
  125.4 3.5 %collective-permute-done.5 = bf16[11,4352]{1,0:T(8,128)(2,1)S(1)} collective-permute-done((bf16[11,4352]{1,0:T(8,128)(2,1)S(1)}, bf16[11,4352]{1,0:T(8,128)(2,1)S(1)}, u32[]{:S(2)}, u32[]{:S(2)}) %collective-permute-start.5) | collective-permute-done | bytes 95776
  129.6 0.7 pad_maximum_fusion.1
  (34 shorter events, 2.4 us)
Async XLA Ops:
  2.9 0.9 copy-start.3
  3.8 0.7 copy-start.7
  4.5 0.7 copy-start.9
  5.2 53.5 %collective-permute-start.1 = (bf16[3,4096,128]{2,1,0:T(8,128)(2,1)}, bf16[3,4096,128]{2,1,0:T(8,128)(2,1)S(1)}, u32[]{:S(2)}, u32[]{:S(2)}) collective-permute-start(bf16[3,4096,128]{2,1,0:T(8,128)(2,1)} %bitcast.9), channel_id=1, source_target_pairs={{0,588},{12,0},{24,36},{36,216},{192,12},{204,192},{216,228},{228,... | collective-permute-start | bytes 9437192 | tf_op jit(solution)/shard_map/ppermute | solution.py:34
  8.5 49.9 %collective-permute-start = (f32[304,128]{1,0:T(8,128)S(1)}, f32[304,128]{1,0:T(8,128)S(1)}, u32[]{:S(2)}, u32[]{:S(2)}) collective-permute-start(f32[304,128]{1,0:T(8,128)S(1)} %message.1), channel_id=1, source_target_pairs={{0,12},{12,0},{1,13},{13,1},{2,14},{14,2},{3,15},{15,3},{4,16},{16... | collective-permute-start | bytes 466952 | tf_op jit(solution)/shard_map/ppermute | solution.py:257
  58.4 1.9 %copy-start = (bf16[4096,3,128]{2,0,1:T(8,128)(2,1)S(1)}, bf16[4096,3,128]{2,0,1:T(8,128)(2,1)}, u32[]{:S(2)}) copy-start(bf16[4096,3,128]{2,0,1:T(8,128)(2,1)} %param.6) | copy-start | bytes 9437188
  58.4 1.9 %copy-start.4 = (bf16[576,128]{1,0:T(8,128)(2,1)S(1)}, bf16[576,128]{1,0:T(8,128)(2,1)}, u32[]{:S(2)}) copy-start(bf16[576,128]{1,0:T(8,128)(2,1)} %grad_ref.5) | copy-start | bytes 442372
  58.7 15.6 %copy-start.8 = (f32[3,3,128]{2,1,0:T(4,128)S(1)}, f32[3,3,128]{2,1,0:T(4,128)}, u32[]{:S(2)}) copy-start(f32[3,3,128]{2,1,0:T(4,128)} %feat_ref.3) | copy-start | bytes 13828
  58.7 15.6 %copy-start.10 = (f32[7,128]{1,0:T(8,128)S(1)}, f32[7,128]{1,0:T(8,128)}, u32[]{:S(2)}) copy-start(f32[7,128]{1,0:T(8,128)} %inner_ref.3) | copy-start | bytes 10756
  60.3 2.1 %copy-start.1 = (bf16[3,4096,128]{2,1,0:T(8,128)(2,1)}, bf16[3,4096,128]{2,1,0:T(8,128)(2,1)S(1)}, u32[]{:S(2)}) copy-start(bf16[3,4096,128]{2,1,0:T(8,128)(2,1)S(1)} %collective-permute-done.1.theirs_ref) | copy-start | bytes 9437188
  62.4 0.8 copy-start.5
  63.2 11.1 %collective-permute-start.3 = (bf16[4,8,256]{2,1,0:T(8,128)(2,1)S(1)}, bf16[4,8,256]{2,1,0:T(8,128)(2,1)S(1)}, u32[]{:S(2)}, u32[]{:S(2)}) collective-permute-start(bf16[4,8,256]{2,1,0:T(8,128)(2,1)S(1)} %get-tuple-element.20), channel_id=1, source_target_pairs={{12,0},{24,12},{36,24},{48,36},{60,48},{72,60},{84,72},{96,84},{10... | collective-permute-start | bytes 49160 | tf_op jit(solution)/shard_map/ppermute | solution.py:34
  68.1 5.6 %collective-permute-start.2 = (bf16[3,8,256]{2,1,0:T(8,128)(2,1)S(1)}, bf16[3,8,256]{2,1,0:T(8,128)(2,1)S(1)}, u32[]{:S(2)}, u32[]{:S(2)}) collective-permute-start(bf16[3,8,256]{2,1,0:T(8,128)(2,1)S(1)} %get-tuple-element.19), channel_id=1, source_target_pairs={{0,12},{12,24},{24,36},{36,48},{48,60},{60,72},{72,84},{84,96},{96... | collective-permute-start | bytes 36872 | tf_op jit(solution)/shard_map/ppermute | solution.py:34
  73.7 0.6 copy-start.11
  74.3 1.9 %copy-start.2 = (bf16[3,4096,128]{2,1,0:T(8,128)(2,1)S(1)}, bf16[3,4096,128]{2,1,0:T(8,128)(2,1)}, u32[]{:S(2)}) copy-start(bf16[3,4096,128]{2,1,0:T(8,128)(2,1)} %copy-done.1) | copy-start | bytes 9437188
  76.2 1.0 copy-start.6
  77.2 0.7 copy-start.12
  82.7 42.0 %collective-permute-start.4 = (bf16[288,128]{1,0:T(8,128)(2,1)}, bf16[288,128]{1,0:T(8,128)(2,1)S(1)}, u32[]{:S(2)}, u32[]{:S(2)}) collective-permute-start(bf16[288,128]{1,0:T(8,128)(2,1)} %get-tuple-element.22), channel_id=1, source_target_pairs={{0,12},{12,0},{1,13},{13,1},{2,14},{14,2},{3,15},{15,3},{4,16},{16... | collective-permute-start | bytes 221192 | tf_op jit(solution)/shard_map/ppermute | solution.py:257
  122.0 6.9 %collective-permute-start.5 = (bf16[11,4352]{1,0:T(8,128)(2,1)S(1)}, bf16[11,4352]{1,0:T(8,128)(2,1)S(1)}, u32[]{:S(2)}, u32[]{:S(2)}) collective-permute-start(bf16[11,4352]{1,0:T(8,128)(2,1)S(1)} %slice.10), channel_id=1, source_target_pairs={{0,1},{1,2},{2,3},{3,4},{4,5},{5,6},{6,7},{7,8},{8,9},{9,10},{10,1... | collective-permute-start | bytes 287240

commit v9 on v8

--- a/solution.py
+++ b/solution.py
@@ -229,6 +229,25 @@
     )(upper, proj, prev, following, grad, feat, inner, came, mine, theirs)
 
 
+def halves_kernel(upper_ref, kept_ref, arrived_ref, o_ref):
+    count = kept_ref.shape[0]
+    upper = upper_ref[0]
+    o_ref[pl.ds(pl.multiple_of(upper * count, 16), count)] = kept_ref[...]
+    o_ref[pl.ds(pl.multiple_of((1 - upper) * count, 16), count)] = arrived_ref[...]
+
+
+def gather_halves(upper, kept, arrived):
+    count, lanes = kept.shape
+    return pl.pallas_call(
+        halves_kernel,
+        in_specs=[smem(), vmem(), vmem()],
+        out_specs=vmem(),
+        out_shape=jax.ShapeDtypeStruct((2 * count, lanes), kept.dtype),
+        compiler_params=PARAMS,
+        name="halves",
+    )(upper, kept, arrived)
+
+
 def encode(tokens):
     wide = tokens.astype(jnp.float32)
     peak = jnp.max(jnp.abs(wide), axis=1, keepdims=True)
@@ -287,12 +306,8 @@
         grad_tokens = jnp.concatenate(
             [summed[:, :depth], summed[:FOLD, depth:].reshape(1, depth)], axis=0
         )
-        gated = jnp.where(
-            upper == 0,
-            jnp.concatenate([kept, arrived], axis=0),
-            jnp.concatenate([arrived, kept], axis=0),
-        )
-        return (gated, grad_tokens)
+        grad_tokens, kept, arrived = lax.optimization_barrier((grad_tokens, kept, arrived))
+        return (gather_halves(flag, kept, arrived), grad_tokens)
 
     return local
 

time: 131 us -> 126 us (0.962)
  the two profiles are of different devices: /device:TPU:104 before, /device:TPU:32 now
where the time goes in v9:
time: 126 us
  blocking collectives  85.4 us (68%)
  starting transfers between devices  16 us (13%)
  waiting for transfers between devices  7.32 us (6%)
  Pallas kernels  6.82 us (5%)
  local copies, waits for them, and re-layouts  5.91 us (5%)
  other arithmetic  3.16 us (3%)
  between operations  1.47 us (1%)
    all_gather x1, blocking collectives, local(): gathered = lax.all_gather(rows, 'z', axis=0, tiled=True)  51.8 us
    unnamed x1, blocking collectives  33.6 us
    ppermute x3, starting transfers between devices, exchange(): return lax.ppermute(value, axes, pairs)  8.2 us
    unnamed x20, local copies, waits for them, and re-layouts  5.82 us
    ppermute x2, starting transfers between devices, across(): return lax.ppermute(value, 'yl', [(0, 1), (1, 0)])  5.41 us
    ppermute x3, waiting for transfers between devices, exchange(): return lax.ppermute(value, axes, pairs)  4.41 us
    pallas_call x1, Pallas kernels, mix(): pl.pallas_call(mix_kernel, in_specs=[smem()] + [vmem()] * 9, out_specs=[v...  4.08 us
    ppermute x2, waiting for transfers between devices, across(): return lax.ppermute(value, 'yl', [(0, 1), (1, 0)])  2.91 us
  transfers between devices with their start and end apart: 6, of which 2 were waited for; matrix products, arithmetic and copies ran while one was open for 2% of the time, Pallas kernels for 0%

profile of v9, /device:TPU:32, one launch (start us, length us, event | category | flops | bytes accessed | tf_op | source)
XLA Modules:
  0.0 126.0 jit_solution(5836803655140693034)
XLA Ops:
  0.6 1.1 fusion.1
  1.7 1.1 fusion.2
  2.8 0.1 broadcast_in_dim.2
  2.9 0.9 copy-done.1
  3.8 0.7 copy-done.3
  4.5 0.7 copy-done.5
  5.2 2.4 %collective-permute-start.1 = (bf16[3,4096,128]{2,1,0:T(8,128)(2,1)}, bf16[3,4096,128]{2,1,0:T(8,128)(2,1)S(1)}, u32[]{:S(2)}, u32[]{:S(2)}) collective-permute-start(bf16[3,4096,128]{2,1,0:T(8,128)(2,1)} %bitcast.9), channel_id=1, source_target_pairs={{0,588},{12,0},{24,36},{36,216},{192,12},{204,192},{216,228},{228,... | collective-permute-start | bytes 9437192 | tf_op jit(solution)/shard_map/ppermute | solution.py:34
  7.6 3.5 %collective-permute-start = (f32[304,128]{1,0:T(8,128)S(1)}, f32[304,128]{1,0:T(8,128)S(1)}, u32[]{:S(2)}, u32[]{:S(2)}) collective-permute-start(f32[304,128]{1,0:T(8,128)S(1)} %message.1), channel_id=1, source_target_pairs={{0,12},{12,0},{1,13},{13,1},{2,14},{14,2},{3,15},{15,3},{4,16},{16... | collective-permute-start | bytes 466952 | tf_op jit(solution)/shard_map/ppermute | solution.py:276
  11.1 51.8 %all-gather.1 = f16[288,4224]{1,0:T(8,128)(2,1)S(1)} all-gather(f16[24,4224]{1,0:T(8,128)(2,1)S(1)} %pad_maximum_fusion), channel_id=1, replica_groups=mesh['yh'=4,'x'=4,'c'=2,'yl'=2,'z'=12] {'z'}, dimensions={0}, use_global_device_ids=true | all-gather | bytes 2635776 | tf_op jit(solution)/shard_map/all_gather | solution.py:292
  62.8 0.3 convert_element_type.8.x_ref
  63.2 1.6 %copy-done = bf16[4096,3,128]{2,0,1:T(8,128)(2,1)S(1)} copy-done((bf16[4096,3,128]{2,0,1:T(8,128)(2,1)S(1)}, bf16[4096,3,128]{2,0,1:T(8,128)(2,1)}, u32[]{:S(2)}) %copy-start) | copy-done | bytes 3145752
  64.7 2.1 %project.1 = (bf16[3,288,256]{2,1,0:T(8,128)(2,1)S(1)}, bf16[4,8,256]{2,1,0:T(8,128)(2,1)S(1)}, bf16[3,8,256]{2,1,0:T(8,128)(2,1)S(1)}) custom-call(s32[1]{0:T(128)} %bitcast.upper_ref, bf16[288,4224]{1,0:T(8,128)(2,1)S(1)} %convert_element_type.8.x_ref, bf16[576,128]{1,0:T(8,128)(2,1)S(1)} %copy-done.2, f32[304,128]{1,0:T(8,128)S(1)} %collective-permute-done.came_ref, ...), custom_call_target="tpu_custom_call" | custom-call | tf_op jit(solution)/shard_map/project/pallas_call | solution.py:113
  66.8 1.9 %collective-permute-start.3 = (bf16[4,8,256]{2,1,0:T(8,128)(2,1)S(1)}, bf16[4,8,256]{2,1,0:T(8,128)(2,1)S(1)}, u32[]{:S(2)}, u32[]{:S(2)}) collective-permute-start(bf16[4,8,256]{2,1,0:T(8,128)(2,1)S(1)} %get-tuple-element.23), channel_id=1, source_target_pairs={{12,0},{24,12},{36,24},{48,36},{60,48},{72,60},{84,72},{96,84},{10... | collective-permute-start | bytes 49160 | tf_op jit(solution)/shard_map/ppermute | solution.py:34
  68.7 3.9 %collective-permute-start.2 = (bf16[3,8,256]{2,1,0:T(8,128)(2,1)S(1)}, bf16[3,8,256]{2,1,0:T(8,128)(2,1)S(1)}, u32[]{:S(2)}, u32[]{:S(2)}) collective-permute-start(bf16[3,8,256]{2,1,0:T(8,128)(2,1)S(1)} %get-tuple-element.22), channel_id=1, source_target_pairs={{0,12},{12,24},{24,36},{36,48},{48,60},{60,72},{72,84},{84,96},{96... | collective-permute-start | bytes 36872 | tf_op jit(solution)/shard_map/ppermute | solution.py:34
  72.7 4.4 %collective-permute-done.2.prev_ref = bf16[3,8,256]{2,1,0:T(8,128)(2,1)S(1)} collective-permute-done((bf16[3,8,256]{2,1,0:T(8,128)(2,1)S(1)}, bf16[3,8,256]{2,1,0:T(8,128)(2,1)S(1)}, u32[]{:S(2)}, u32[]{:S(2)}) %collective-permute-start.2) | collective-permute-done | bytes 12320 | tf_op jit(solution)/shard_map/ppermute | solution.py:34
  77.1 4.1 %mix.1 = (bf16[288,128]{1,0:T(8,128)(2,1)S(1)}, bf16[288,128]{1,0:T(8,128)(2,1)S(1)}, bf16[276,4352]{1,0:T(8,128)(2,1)}) custom-call(s32[1]{0:T(128)} %bitcast.upper_ref, bf16[3,288,256]{2,1,0:T(8,128)(2,1)S(1)} %get-tuple-element.21.proj_ref, bf16[3,8,256]{2,1,0:T(8,128)(2,1)S(1)} %collective-permute-done.2.prev_ref, ...), custom_call_target="tpu_custom_call" | custom-call | tf_op jit(solution)/shard_map/mix/pallas_call | solution.py:216
  81.2 33.6 %fusion = bf16[24,4352]{1,0:T(8,128)(2,1)S(1)} fusion(bf16[276,4352]{1,0:T(8,128)(2,1)} %get-tuple-element.24), kind=kCustom, calls=%all-reduce-scatter | all-reduce-scatter fusion | flops 1253377 | bytes 2615296
  114.8 2.4 %collective-permute-start.5 = (bf16[11,4352]{1,0:T(8,128)(2,1)S(1)}, bf16[11,4352]{1,0:T(8,128)(2,1)S(1)}, u32[]{:S(2)}, u32[]{:S(2)}) collective-permute-start(bf16[11,4352]{1,0:T(8,128)(2,1)S(1)} %slice.10), channel_id=1, source_target_pairs={{0,1},{1,2},{2,3},{3,4},{4,5},{5,6},{6,7},{7,8},{8,9},{9,10},{10,1... | collective-permute-start | bytes 287240
  117.2 1.3 %dynamic-slice.4 = u32[1]{0:T(128)} dynamic-slice(u32[768]{0:T(1024)} %constant.26, u32[]{:S(6)} %partition-id.4), dynamic_slice_sizes={1} | dynamic-slice | bytes 12
  119.1 1.9 %collective-permute-start.4 = (bf16[288,128]{1,0:T(8,128)(2,1)S(1)}, bf16[288,128]{1,0:T(8,128)(2,1)S(1)}, u32[]{:S(2)}, u32[]{:S(2)}) collective-permute-start(bf16[288,128]{1,0:T(8,128)(2,1)S(1)} %get-tuple-element.26), channel_id=1, source_target_pairs={{0,12},{12,0},{1,13},{13,1},{2,14},{14,2},{3,15},{15,3},{4,16},{16... | collective-permute-start | bytes 221192 | tf_op jit(solution)/shard_map/ppermute | solution.py:276
  121.0 0.6 concatenate.9
  121.7 0.7 pad_maximum_fusion.1
  122.4 2.9 %collective-permute-done.4.arrived_ref = bf16[288,128]{1,0:T(8,128)(2,1)S(1)} collective-permute-done((bf16[288,128]{1,0:T(8,128)(2,1)S(1)}, bf16[288,128]{1,0:T(8,128)(2,1)S(1)}, u32[]{:S(2)}, u32[]{:S(2)}) %collective-permute-start.4) | collective-permute-done | bytes 73760 | tf_op jit(solution)/shard_map/ppermute | solution.py:276
  125.3 0.7 halves.1
  (22 shorter events, 0.2 us)
Async XLA Ops:
  2.9 0.9 copy-start.1
  3.8 0.7 copy-start.3
  4.5 0.7 copy-start.5
  5.2 57.9 %collective-permute-start.1 = (bf16[3,4096,128]{2,1,0:T(8,128)(2,1)}, bf16[3,4096,128]{2,1,0:T(8,128)(2,1)S(1)}, u32[]{:S(2)}, u32[]{:S(2)}) collective-permute-start(bf16[3,4096,128]{2,1,0:T(8,128)(2,1)} %bitcast.9), channel_id=1, source_target_pairs={{0,588},{12,0},{24,36},{36,216},{192,12},{204,192},{216,228},{228,... | collective-permute-start | bytes 9437192 | tf_op jit(solution)/shard_map/ppermute | solution.py:34
  7.6 55.3 %collective-permute-start = (f32[304,128]{1,0:T(8,128)S(1)}, f32[304,128]{1,0:T(8,128)S(1)}, u32[]{:S(2)}, u32[]{:S(2)}) collective-permute-start(f32[304,128]{1,0:T(8,128)S(1)} %message.1), channel_id=1, source_target_pairs={{0,12},{12,0},{1,13},{13,1},{2,14},{14,2},{3,15},{15,3},{4,16},{16... | collective-permute-start | bytes 466952 | tf_op jit(solution)/shard_map/ppermute | solution.py:276
  62.8 1.9 %copy-start = (bf16[4096,3,128]{2,0,1:T(8,128)(2,1)S(1)}, bf16[4096,3,128]{2,0,1:T(8,128)(2,1)}, u32[]{:S(2)}) copy-start(bf16[4096,3,128]{2,0,1:T(8,128)(2,1)} %param.6) | copy-start | bytes 9437188
  62.8 1.9 %copy-start.2 = (bf16[576,128]{1,0:T(8,128)(2,1)S(1)}, bf16[576,128]{1,0:T(8,128)(2,1)}, u32[]{:S(2)}) copy-start(bf16[576,128]{1,0:T(8,128)(2,1)} %grad_ref.5) | copy-start | bytes 442372
  63.1 13.9 %copy-start.4 = (f32[3,3,128]{2,1,0:T(4,128)S(1)}, f32[3,3,128]{2,1,0:T(4,128)}, u32[]{:S(2)}) copy-start(f32[3,3,128]{2,1,0:T(4,128)} %feat_ref.3) | copy-start | bytes 13828
  63.1 13.9 %copy-start.6 = (f32[7,128]{1,0:T(8,128)S(1)}, f32[7,128]{1,0:T(8,128)}, u32[]{:S(2)}) copy-start(f32[7,128]{1,0:T(8,128)} %inner_ref.3) | copy-start | bytes 10756
  66.8 10.3 %collective-permute-start.3 = (bf16[4,8,256]{2,1,0:T(8,128)(2,1)S(1)}, bf16[4,8,256]{2,1,0:T(8,128)(2,1)S(1)}, u32[]{:S(2)}, u32[]{:S(2)}) collective-permute-start(bf16[4,8,256]{2,1,0:T(8,128)(2,1)S(1)} %get-tuple-element.23), channel_id=1, source_target_pairs={{12,0},{24,12},{36,24},{48,36},{60,48},{72,60},{84,72},{96,84},{10... | collective-permute-start | bytes 49160 | tf_op jit(solution)/shard_map/ppermute | solution.py:34
  68.7 8.3 %collective-permute-start.2 = (bf16[3,8,256]{2,1,0:T(8,128)(2,1)S(1)}, bf16[3,8,256]{2,1,0:T(8,128)(2,1)S(1)}, u32[]{:S(2)}, u32[]{:S(2)}) collective-permute-start(bf16[3,8,256]{2,1,0:T(8,128)(2,1)S(1)} %get-tuple-element.22), channel_id=1, source_target_pairs={{0,12},{12,24},{24,36},{36,48},{48,60},{60,72},{72,84},{84,96},{96... | collective-permute-start | bytes 36872 | tf_op jit(solution)/shard_map/ppermute | solution.py:34
  114.8 6.2 %collective-permute-start.5 = (bf16[11,4352]{1,0:T(8,128)(2,1)S(1)}, bf16[11,4352]{1,0:T(8,128)(2,1)S(1)}, u32[]{:S(2)}, u32[]{:S(2)}) collective-permute-start(bf16[11,4352]{1,0:T(8,128)(2,1)S(1)} %slice.10), channel_id=1, source_target_pairs={{0,1},{1,2},{2,3},{3,4},{4,5},{5,6},{6,7},{7,8},{8,9},{9,10},{10,1... | collective-permute-start | bytes 287240
  119.1 6.2 %collective-permute-start.4 = (bf16[288,128]{1,0:T(8,128)(2,1)S(1)}, bf16[288,128]{1,0:T(8,128)(2,1)S(1)}, u32[]{:S(2)}, u32[]{:S(2)}) collective-permute-start(bf16[288,128]{1,0:T(8,128)(2,1)S(1)} %get-tuple-element.26), channel_id=1, source_target_pairs={{0,12},{12,0},{1,13},{13,1},{2,14},{14,2},{3,15},{15,3},{4,16},{16... | collective-permute-start | bytes 221192 | tf_op jit(solution)/shard_map/ppermute | solution.py:276

commit v10 on v9

--- a/solution.py
+++ b/solution.py
@@ -281,8 +281,7 @@
 
         note = message(flag, grad_out, feat_taps, inner_taps)
         planes = proj_weight.transpose(1, 0, 2)
-        rows, sent, note = lax.optimization_barrier((encode(tokens), planes, note))
-        came = across(note)
+        rows, sent, came = lax.optimization_barrier((encode(tokens), planes, across(note)))
 
         def beside(yh, c, yl):
             place = (yh * 2 + yl + (1 if c else ring - 1)) % ring
@@ -306,7 +305,6 @@
         grad_tokens = jnp.concatenate(
             [summed[:, :depth], summed[:FOLD, depth:].reshape(1, depth)], axis=0
         )
-        grad_tokens, kept, arrived = lax.optimization_barrier((grad_tokens, kept, arrived))
         return (gather_halves(flag, kept, arrived), grad_tokens)
 
     return local

time: 126 us -> 127 us (level)
  the two profiles are of different devices: /device:TPU:32 before, /device:TPU:48 now
where the time goes in v10:
time: 127 us
  blocking collectives  84.4 us (66%)
  starting transfers between devices  16.6 us (13%)
  waiting for transfers between devices  8.39 us (7%)
  Pallas kernels  6.82 us (5%)
  local copies, waits for them, and re-layouts  5.91 us (5%)
  other arithmetic  3.16 us (2%)
  between operations  1.46 us (1%)
    all_gather x1, blocking collectives, local(): gathered = lax.all_gather(rows, 'z', axis=0, tiled=True)  51.1 us
    unnamed x1, blocking collectives  33.4 us
    ppermute x3, starting transfers between devices, exchange(): return lax.ppermute(value, axes, pairs)  9.09 us
    unnamed x20, local copies, waits for them, and re-layouts  5.82 us
    ppermute x2, waiting for transfers between devices, across(): return lax.ppermute(value, 'yl', [(0, 1), (1, 0)])  5.19 us
    ppermute x2, starting transfers between devices, across(): return lax.ppermute(value, 'yl', [(0, 1), (1, 0)])  4.51 us
    pallas_call x1, Pallas kernels, mix(): pl.pallas_call(mix_kernel, in_specs=[smem()] + [vmem()] * 9, out_specs=[v...  4.08 us
    ppermute x3, waiting for transfers between devices, exchange(): return lax.ppermute(value, axes, pairs)  3.2 us
  transfers between devices with their start and end apart: 6, of which 3 were waited for; matrix products, arithmetic and copies ran while one was open for 3% of the time, Pallas kernels for 1%

profile of v10, /device:TPU:48, one launch (start us, length us, event | category | flops | bytes accessed | tf_op | source)
XLA Modules:
  0.0 126.8 jit_solution(13987572335768345127)
XLA Ops:
  0.6 0.9 copy-done.1
  1.6 0.7 copy-done.3
  2.2 0.7 copy-done.5
  2.9 2.6 %collective-permute-start = (f32[304,128]{1,0:T(8,128)S(1)}, f32[304,128]{1,0:T(8,128)S(1)}, u32[]{:S(2)}, u32[]{:S(2)}) collective-permute-start(f32[304,128]{1,0:T(8,128)S(1)} %message.1), channel_id=1, source_target_pairs={{0,12},{12,0},{1,13},{13,1},{2,14},{14,2},{3,15},{15,3},{4,16},{16... | collective-permute-start | bytes 466952 | tf_op jit(solution)/shard_map/ppermute | solution.py:276
  5.5 1.1 fusion.1
  6.6 1.1 fusion.2
  7.8 2.8 %collective-permute-done.came_ref = f32[304,128]{1,0:T(8,128)S(1)} collective-permute-done((f32[304,128]{1,0:T(8,128)S(1)}, f32[304,128]{1,0:T(8,128)S(1)}, u32[]{:S(2)}, u32[]{:S(2)}) %collective-permute-start) | collective-permute-done | bytes 155680 | tf_op jit(solution)/shard_map/ppermute | solution.py:276
  10.6 3.2 %collective-permute-start.1 = (bf16[3,4096,128]{2,1,0:T(8,128)(2,1)}, bf16[3,4096,128]{2,1,0:T(8,128)(2,1)S(1)}, u32[]{:S(2)}, u32[]{:S(2)}) collective-permute-start(bf16[3,4096,128]{2,1,0:T(8,128)(2,1)} %bitcast.9), channel_id=1, source_target_pairs={{0,588},{12,0},{24,36},{36,216},{192,12},{204,192},{216,228},{228,... | collective-permute-start | bytes 9437192 | tf_op jit(solution)/shard_map/ppermute | solution.py:34
  13.9 51.1 %all-gather.1 = f16[288,4224]{1,0:T(8,128)(2,1)S(1)} all-gather(f16[24,4224]{1,0:T(8,128)(2,1)S(1)} %pad_maximum_fusion), channel_id=1, replica_groups=mesh['yh'=4,'x'=4,'c'=2,'yl'=2,'z'=12] {'z'}, dimensions={0}, use_global_device_ids=true | all-gather | bytes 2635776 | tf_op jit(solution)/shard_map/all_gather | solution.py:291
  64.9 0.3 convert_element_type.8.x_ref
  65.2 1.6 %copy-done = bf16[4096,3,128]{2,0,1:T(8,128)(2,1)S(1)} copy-done((bf16[4096,3,128]{2,0,1:T(8,128)(2,1)S(1)}, bf16[4096,3,128]{2,0,1:T(8,128)(2,1)}, u32[]{:S(2)}) %copy-start) | copy-done | bytes 3145752
  66.8 2.1 %project.1 = (bf16[3,288,256]{2,1,0:T(8,128)(2,1)S(1)}, bf16[4,8,256]{2,1,0:T(8,128)(2,1)S(1)}, bf16[3,8,256]{2,1,0:T(8,128)(2,1)S(1)}) custom-call(s32[1]{0:T(128)} %bitcast.upper_ref, bf16[288,4224]{1,0:T(8,128)(2,1)S(1)} %convert_element_type.8.x_ref, bf16[576,128]{1,0:T(8,128)(2,1)S(1)} %copy-done.2, f32[304,128]{1,0:T(8,128)S(1)} %collective-permute-done.came_ref, ...), custom_call_target="tpu_custom_call" | custom-call | tf_op jit(solution)/shard_map/project/pallas_call | solution.py:113
  68.9 1.9 %collective-permute-start.3 = (bf16[4,8,256]{2,1,0:T(8,128)(2,1)S(1)}, bf16[4,8,256]{2,1,0:T(8,128)(2,1)S(1)}, u32[]{:S(2)}, u32[]{:S(2)}) collective-permute-start(bf16[4,8,256]{2,1,0:T(8,128)(2,1)S(1)} %get-tuple-element.20), channel_id=1, source_target_pairs={{12,0},{24,12},{36,24},{48,36},{60,48},{72,60},{84,72},{96,84},{10... | collective-permute-start | bytes 49160 | tf_op jit(solution)/shard_map/ppermute | solution.py:34
  70.8 3.9 %collective-permute-start.2 = (bf16[3,8,256]{2,1,0:T(8,128)(2,1)S(1)}, bf16[3,8,256]{2,1,0:T(8,128)(2,1)S(1)}, u32[]{:S(2)}, u32[]{:S(2)}) collective-permute-start(bf16[3,8,256]{2,1,0:T(8,128)(2,1)S(1)} %get-tuple-element.19), channel_id=1, source_target_pairs={{0,12},{12,24},{24,36},{36,48},{48,60},{60,72},{72,84},{84,96},{96... | collective-permute-start | bytes 36872 | tf_op jit(solution)/shard_map/ppermute | solution.py:34
  74.8 3.2 %collective-permute-done.2.prev_ref = bf16[3,8,256]{2,1,0:T(8,128)(2,1)S(1)} collective-permute-done((bf16[3,8,256]{2,1,0:T(8,128)(2,1)S(1)}, bf16[3,8,256]{2,1,0:T(8,128)(2,1)S(1)}, u32[]{:S(2)}, u32[]{:S(2)}) %collective-permute-start.2) | collective-permute-done | bytes 12320 | tf_op jit(solution)/shard_map/ppermute | solution.py:34
  78.0 4.1 %mix.1 = (bf16[288,128]{1,0:T(8,128)(2,1)S(1)}, bf16[288,128]{1,0:T(8,128)(2,1)S(1)}, bf16[276,4352]{1,0:T(8,128)(2,1)}) custom-call(s32[1]{0:T(128)} %bitcast.upper_ref, bf16[3,288,256]{2,1,0:T(8,128)(2,1)S(1)} %get-tuple-element.18.proj_ref, bf16[3,8,256]{2,1,0:T(8,128)(2,1)S(1)} %collective-permute-done.2.prev_ref, ...), custom_call_target="tpu_custom_call" | custom-call | tf_op jit(solution)/shard_map/mix/pallas_call | solution.py:216
  82.0 33.4 %fusion = bf16[24,4352]{1,0:T(8,128)(2,1)S(1)} fusion(bf16[276,4352]{1,0:T(8,128)(2,1)} %get-tuple-element.23), kind=kCustom, calls=%all-reduce-scatter | all-reduce-scatter fusion | flops 1253377 | bytes 2615296
  115.5 3.0 %collective-permute-start.5 = (bf16[11,4352]{1,0:T(8,128)(2,1)S(1)}, bf16[11,4352]{1,0:T(8,128)(2,1)S(1)}, u32[]{:S(2)}, u32[]{:S(2)}) collective-permute-start(bf16[11,4352]{1,0:T(8,128)(2,1)S(1)} %slice.10), channel_id=1, source_target_pairs={{0,1},{1,2},{2,3},{3,4},{4,5},{5,6},{6,7},{7,8},{8,9},{9,10},{10,1... | collective-permute-start | bytes 287240
  118.5 1.9 %collective-permute-start.4 = (bf16[288,128]{1,0:T(8,128)(2,1)S(1)}, bf16[288,128]{1,0:T(8,128)(2,1)S(1)}, u32[]{:S(2)}, u32[]{:S(2)}) collective-permute-start(bf16[288,128]{1,0:T(8,128)(2,1)S(1)} %get-tuple-element.22), channel_id=1, source_target_pairs={{0,12},{12,0},{1,13},{13,1},{2,14},{14,2},{3,15},{15,3},{4,16},{16... | collective-permute-start | bytes 221192 | tf_op jit(solution)/shard_map/ppermute | solution.py:276
  120.4 1.3 %dynamic-slice.4 = u32[1]{0:T(128)} dynamic-slice(u32[768]{0:T(1024)} %constant.26, u32[]{:S(6)} %partition-id.4), dynamic_slice_sizes={1} | dynamic-slice | bytes 12
  122.3 2.4 %collective-permute-done.4.arrived_ref = bf16[288,128]{1,0:T(8,128)(2,1)S(1)} collective-permute-done((bf16[288,128]{1,0:T(8,128)(2,1)S(1)}, bf16[288,128]{1,0:T(8,128)(2,1)S(1)}, u32[]{:S(2)}, u32[]{:S(2)}) %collective-permute-start.4) | collective-permute-done | bytes 73760 | tf_op jit(solution)/shard_map/ppermute | solution.py:276
  124.7 0.7 halves.1
  125.4 0.5 concatenate.9
  126.1 0.7 pad_maximum_fusion.1
  (22 shorter events, 0.3 us)
Async XLA Ops:
  0.6 0.9 copy-start.1
  1.5 0.7 copy-start.3
  2.2 0.7 copy-start.5
  2.9 7.7 %collective-permute-start = (f32[304,128]{1,0:T(8,128)S(1)}, f32[304,128]{1,0:T(8,128)S(1)}, u32[]{:S(2)}, u32[]{:S(2)}) collective-permute-start(f32[304,128]{1,0:T(8,128)S(1)} %message.1), channel_id=1, source_target_pairs={{0,12},{12,0},{1,13},{13,1},{2,14},{14,2},{3,15},{15,3},{4,16},{16... | collective-permute-start | bytes 466952 | tf_op jit(solution)/shard_map/ppermute | solution.py:276
  10.6 54.6 %collective-permute-start.1 = (bf16[3,4096,128]{2,1,0:T(8,128)(2,1)}, bf16[3,4096,128]{2,1,0:T(8,128)(2,1)S(1)}, u32[]{:S(2)}, u32[]{:S(2)}) collective-permute-start(bf16[3,4096,128]{2,1,0:T(8,128)(2,1)} %bitcast.9), channel_id=1, source_target_pairs={{0,588},{12,0},{24,36},{36,216},{192,12},{204,192},{216,228},{228,... | collective-permute-start | bytes 9437192 | tf_op jit(solution)/shard_map/ppermute | solution.py:34
  64.9 1.9 %copy-start = (bf16[4096,3,128]{2,0,1:T(8,128)(2,1)S(1)}, bf16[4096,3,128]{2,0,1:T(8,128)(2,1)}, u32[]{:S(2)}) copy-start(bf16[4096,3,128]{2,0,1:T(8,128)(2,1)} %param.6) | copy-start | bytes 9437188
  64.9 1.9 %copy-start.2 = (bf16[576,128]{1,0:T(8,128)(2,1)S(1)}, bf16[576,128]{1,0:T(8,128)(2,1)}, u32[]{:S(2)}) copy-start(bf16[576,128]{1,0:T(8,128)(2,1)} %grad_ref.5) | copy-start | bytes 442372
  65.2 12.7 %copy-start.4 = (f32[3,3,128]{2,1,0:T(4,128)S(1)}, f32[3,3,128]{2,1,0:T(4,128)}, u32[]{:S(2)}) copy-start(f32[3,3,128]{2,1,0:T(4,128)} %feat_ref.3) | copy-start | bytes 13828
  65.2 12.7 %copy-start.6 = (f32[7,128]{1,0:T(8,128)S(1)}, f32[7,128]{1,0:T(8,128)}, u32[]{:S(2)}) copy-start(f32[7,128]{1,0:T(8,128)} %inner_ref.3) | copy-start | bytes 10756
  68.9 9.1 %collective-permute-start.3 = (bf16[4,8,256]{2,1,0:T(8,128)(2,1)S(1)}, bf16[4,8,256]{2,1,0:T(8,128)(2,1)S(1)}, u32[]{:S(2)}, u32[]{:S(2)}) collective-permute-start(bf16[4,8,256]{2,1,0:T(8,128)(2,1)S(1)} %get-tuple-element.20), channel_id=1, source_target_pairs={{12,0},{24,12},{36,24},{48,36},{60,48},{72,60},{84,72},{96,84},{10... | collective-permute-start | bytes 49160 | tf_op jit(solution)/shard_map/ppermute | solution.py:34
  70.8 7.1 %collective-permute-start.2 = (bf16[3,8,256]{2,1,0:T(8,128)(2,1)S(1)}, bf16[3,8,256]{2,1,0:T(8,128)(2,1)S(1)}, u32[]{:S(2)}, u32[]{:S(2)}) collective-permute-start(bf16[3,8,256]{2,1,0:T(8,128)(2,1)S(1)} %get-tuple-element.19), channel_id=1, source_target_pairs={{0,12},{12,24},{24,36},{36,48},{48,60},{60,72},{72,84},{84,96},{96... | collective-permute-start | bytes 36872 | tf_op jit(solution)/shard_map/ppermute | solution.py:34
  115.5 9.9 %collective-permute-start.5 = (bf16[11,4352]{1,0:T(8,128)(2,1)S(1)}, bf16[11,4352]{1,0:T(8,128)(2,1)S(1)}, u32[]{:S(2)}, u32[]{:S(2)}) collective-permute-start(bf16[11,4352]{1,0:T(8,128)(2,1)S(1)} %slice.10), channel_id=1, source_target_pairs={{0,1},{1,2},{2,3},{3,4},{4,5},{5,6},{6,7},{7,8},{8,9},{9,10},{10,1... | collective-permute-start | bytes 287240
  118.5 6.2 %collective-permute-start.4 = (bf16[288,128]{1,0:T(8,128)(2,1)S(1)}, bf16[288,128]{1,0:T(8,128)(2,1)S(1)}, u32[]{:S(2)}, u32[]{:S(2)}) collective-permute-start(bf16[288,128]{1,0:T(8,128)(2,1)S(1)} %get-tuple-element.22), channel_id=1, source_target_pairs={{0,12},{12,0},{1,13},{13,1},{2,14},{14,2},{3,15},{15,3},{4,16},{16... | collective-permute-start | bytes 221192 | tf_op jit(solution)/shard_map/ppermute | solution.py:276

commit v11 on v10

--- a/solution.py
+++ b/solution.py
@@ -54,40 +54,67 @@
     return pl.multiple_of(upper * lanes, lanes), pl.multiple_of((1 - upper) * lanes, lanes)
 
 
+def bring(source, target, sems):
+    copies = [pltpu.make_async_copy(source.at[j], target.at[j], sems.at[j]) for j in range(source.shape[0])]
+    for copy in copies:
+        copy.start()
+    return copies
+
+
 def side_by_side(mine_ref, theirs_ref, part, cut):
     return jnp.concatenate([mine_ref[part, cut], theirs_ref[part, cut]], axis=1)
 
 
-def message_kernel(upper_ref, grad_ref, feat_ref, inner_ref, o_ref):
-    count = grad_ref.shape[0] // 2
+def message_kernel(upper_ref, grad_ref, feat_ref, inner_ref, o_ref, grad_buf, feat_buf, inner_buf, sems):
+    count = grad_buf.shape[0]
     begin = pl.multiple_of((1 - upper_ref[0]) * count, 16)
-    o_ref[:count] = grad_ref[pl.ds(begin, count)].astype(o_ref.dtype)
+    copies = [
+        pltpu.make_async_copy(grad_ref.at[pl.ds(begin, count)], grad_buf, sems.at[0]),
+        pltpu.make_async_copy(feat_ref, feat_buf, sems.at[1]),
+        pltpu.make_async_copy(inner_ref, inner_buf, sems.at[2]),
+    ]
+    for copy in copies:
+        copy.start()
+    for copy in copies:
+        copy.wait()
+    o_ref[:count] = grad_buf[...].astype(o_ref.dtype)
     for part in range(3):
-        o_ref[count + 3 * part : count + 3 * part + 3] = feat_ref[part]
-    o_ref[count + 9 :] = inner_ref[...]
+        o_ref[count + 3 * part : count + 3 * part + 3] = feat_buf[part]
+    o_ref[count + 9 :] = inner_buf[...]
 
 
 def message(upper, grad, feat, inner):
-    rows = grad.shape[0] // 2 + 9 + inner.shape[0]
+    half = (grad.shape[0] // 2, grad.shape[1])
     return pl.pallas_call(
         message_kernel,
-        grid=(1,),
-        in_specs=[smem()] + [pl.BlockSpec(v.shape, lambda i, n=v.ndim: (0,) * n) for v in (grad, feat, inner)],
-        out_specs=pl.BlockSpec((rows, grad.shape[1]), lambda i: (0, 0)),
-        out_shape=jax.ShapeDtypeStruct((rows, grad.shape[1]), jnp.float32),
+        in_specs=[smem()] + [hbm()] * 3,
+        out_specs=vmem(),
+        out_shape=jax.ShapeDtypeStruct((half[0] + 9 + inner.shape[0], half[1]), jnp.float32),
+        scratch_shapes=[
+            pltpu.VMEM(half, grad.dtype),
+            pltpu.VMEM(feat.shape, feat.dtype),
+            pltpu.VMEM(inner.shape, inner.dtype),
+            pltpu.SemaphoreType.DMA((3,)),
+        ],
         compiler_params=PARAMS,
         name="message",
-    )(upper, grad, feat, inner)
-
-
-def project_kernel(upper_ref, x_ref, grad_ref, came_ref, mine_ref, theirs_ref, o_ref, head_ref, tail_ref):
+    )(upper, *[in_hbm(value) for value in (grad, feat, inner)])
+
+
+def in_hbm(value):
+    return pltpu.with_memory_space_constraint(value, pltpu.MemorySpace.HBM)
+
+
+def project_kernel(upper_ref, x_ref, grad_ref, came_ref, mine_hbm, theirs_ref, o_ref, head_ref, tail_ref, mine_ref, sems):
     parts, depth, lanes = mine_ref.shape
     count = x_ref.shape[0]
     own, other = slots(upper_ref, lanes)
+    copies = bring(mine_hbm, mine_ref, sems)
     scale = jnp.exp2(x_ref[:, depth : depth + 1].astype(jnp.float32) - TOP)
     block = min(depth, 1024)
     for j in range(parts):
         total = None
+        copies[j].wait()
         for begin in range(0, depth, block):
             cut = slice(begin, begin + block)
             piece = jnp.dot(
@@ -112,16 +139,17 @@
     count = rows.shape[0]
     return pl.pallas_call(
         project_kernel,
-        in_specs=[smem()] + [vmem()] * 5,
+        in_specs=[smem()] + [vmem()] * 3 + [hbm(), vmem()],
         out_specs=[vmem()] * 3,
         out_shape=[
             jax.ShapeDtypeStruct((parts, count, 2 * lanes), jnp.bfloat16),
             jax.ShapeDtypeStruct((parts + 1, HALO, 2 * lanes), jnp.bfloat16),
             jax.ShapeDtypeStruct((parts, HALO, 2 * lanes), jnp.bfloat16),
         ],
+        scratch_shapes=[pltpu.VMEM(mine.shape, mine.dtype), pltpu.SemaphoreType.DMA((parts,))],
         compiler_params=PARAMS,
         name="project",
-    )(upper, rows, grad, came, mine, theirs)
+    )(upper, rows, grad, came, in_hbm(mine), theirs)
 
 
 def causal(series, taps):
@@ -139,13 +167,14 @@
 
 
 def mix_kernel(
-    upper_ref, proj_ref, prev_ref, next_ref, grad_ref, feat_ref, inner_ref, came_ref, mine_ref, theirs_ref,
-    kept_ref, sent_ref, o_ref, back, extra, o_buf, sems,
+    upper_ref, proj_ref, prev_ref, next_ref, grad_ref, feat_ref, inner_ref, came_ref, mine_hbm, theirs_ref,
+    kept_ref, sent_ref, o_ref, back, extra, o_buf, sems, mine_ref, mine_sems,
 ):
     parts, depth, lanes = mine_ref.shape
     count = proj_ref.shape[1]
     last = HALO + count
     block = depth // 8
+    copies = bring(mine_hbm, mine_ref, mine_sems)
     own, other = slots(upper_ref, lanes)
     begin = pl.multiple_of(upper_ref[0] * count, 16)
     shards = count // SHARD
@@ -178,6 +207,8 @@
                 first = k * SHARD
                 back[part, k * body : (k + 1) * body, cut] = rows[first : first + body]
                 back[part, main + k : main + k + 1, cut] = rows[first + body : first + SHARD]
+    for copy in copies:
+        copy.wait()
     left = [back[part].astype(jnp.bfloat16) for part in range(parts)]
     contract = (((1,), (1,)), ((), ()))
     extra[...] = jnp.zeros_like(extra)
@@ -215,7 +246,7 @@
     main = count // SHARD * (SHARD - 1)
     return pl.pallas_call(
         mix_kernel,
-        in_specs=[smem()] + [vmem()] * 9,
+        in_specs=[smem()] + [vmem()] * 7 + [hbm(), vmem()],
         out_specs=[vmem(), vmem(), hbm()],
         out_shape=[half, half, pltpu.HBM((main, depth + depth // FOLD), jnp.bfloat16)],
         scratch_shapes=[
@@ -223,10 +254,12 @@
             pltpu.VMEM((main, depth // FOLD), jnp.float32),
             pltpu.VMEM((main, depth + depth // FOLD), jnp.bfloat16),
             pltpu.SemaphoreType.DMA((9,)),
+            pltpu.VMEM(mine.shape, mine.dtype),
+            pltpu.SemaphoreType.DMA((parts,)),
         ],
         compiler_params=PARAMS,
         name="mix",
-    )(upper, proj, prev, following, grad, feat, inner, came, mine, theirs)
+    )(upper, proj, prev, following, grad, feat, inner, came, in_hbm(mine), theirs)
 
 
 def halves_kernel(upper_ref, kept_ref, arrived_ref, o_ref):

time: 127 us -> 128 us (level)
  Pallas kernels: 6.82 us -> 11.2 us
  local copies, waits for them, and re-layouts: 5.91 us -> 2.64 us
    pallas_call x3, Pallas kernels: 6.15 us -> 10.6 us  [the longest x1 4.81 us: mix(): pl.pallas_call(mix_kernel, in_specs=[smem()] + [vmem()] * 7 + [hbm(), vme...]
    unnamed x20 -> x12, local copies, waits for them, and re-layouts: 5.82 us -> 2.55 us
where the time goes in v11:
time: 128 us
  blocking collectives  84.4 us (66%)
  starting transfers between devices  16.6 us (13%)
  Pallas kernels  11.2 us (9%)
  waiting for transfers between devices  8.39 us (7%)
  other arithmetic  3.16 us (2%)
  local copies, waits for them, and re-layouts  2.64 us (2%)
  between operations  1.46 us (1%)
    all_gather x1, blocking collectives, local(): gathered = lax.all_gather(rows, 'z', axis=0, tiled=True)  51.1 us
    unnamed x1, blocking collectives  33.3 us
    ppermute x3, starting transfers between devices, exchange(): return lax.ppermute(value, axes, pairs)  9.09 us
    ppermute x2, waiting for transfers between devices, across(): return lax.ppermute(value, 'yl', [(0, 1), (1, 0)])  5.19 us
    pallas_call x1, Pallas kernels, mix(): pl.pallas_call(mix_kernel, in_specs=[smem()] + [vmem()] * 7 + [hbm(), vme...  4.81 us
    pallas_call x1, Pallas kernels, project(): pl.pallas_call(project_kernel, in_specs=[smem()] + [vmem()] * 3 + [hbm(),...  4.81 us
    ppermute x2, starting transfers between devices, across(): return lax.ppermute(value, 'yl', [(0, 1), (1, 0)])  4.51 us
    ppermute x3, waiting for transfers between devices, exchange(): return lax.ppermute(value, axes, pairs)  3.2 us
  transfers between devices with their start and end apart: 6, of which 3 were waited for; matrix products, arithmetic and copies ran while one was open for 3% of the time, Pallas kernels for 1%

profile of v11, /device:TPU:48, one launch (start us, length us, event | category | flops | bytes accessed | tf_op | source)
XLA Modules:
  0.0 127.9 jit_solution(13638394971849584291)
XLA Ops:
  0.6 0.9 message.1
  1.6 2.6 %collective-permute-start = (f32[304,128]{1,0:T(8,128)S(1)}, f32[304,128]{1,0:T(8,128)S(1)}, u32[]{:S(2)}, u32[]{:S(2)}) collective-permute-start(f32[304,128]{1,0:T(8,128)S(1)} %message.1), channel_id=1, source_target_pairs={{0,12},{12,0},{1,13},{13,1},{2,14},{14,2},{3,15},{15,3},{4,16},{16... | collective-permute-start | bytes 466952 | tf_op jit(solution)/shard_map/ppermute | solution.py:309
  4.2 1.1 fusion.1
  5.2 1.1 fusion.2
  6.3 0.1 broadcast_in_dim.2
  6.4 2.8 %collective-permute-done.came_ref = f32[304,128]{1,0:T(8,128)S(1)} collective-permute-done((f32[304,128]{1,0:T(8,128)S(1)}, f32[304,128]{1,0:T(8,128)S(1)}, u32[]{:S(2)}, u32[]{:S(2)}) %collective-permute-start) | collective-permute-done | bytes 155680 | tf_op jit(solution)/shard_map/ppermute | solution.py:309
  9.2 3.2 %collective-permute-start.1 = (bf16[3,4096,128]{2,1,0:T(8,128)(2,1)}, bf16[3,4096,128]{2,1,0:T(8,128)(2,1)S(1)}, u32[]{:S(2)}, u32[]{:S(2)}) collective-permute-start(bf16[3,4096,128]{2,1,0:T(8,128)(2,1)} %bitcast.9), channel_id=1, source_target_pairs={{0,588},{12,0},{24,36},{36,216},{192,12},{204,192},{216,228},{228,... | collective-permute-start | bytes 9437192 | tf_op jit(solution)/shard_map/ppermute | solution.py:34
  12.5 51.1 %all-gather.1 = f16[288,4224]{1,0:T(8,128)(2,1)S(1)} all-gather(f16[24,4224]{1,0:T(8,128)(2,1)S(1)} %pad_maximum_fusion), channel_id=1, replica_groups=mesh['yh'=4,'x'=4,'c'=2,'yl'=2,'z'=12] {'z'}, dimensions={0}, use_global_device_ids=true | all-gather | bytes 2635776 | tf_op jit(solution)/shard_map/all_gather | solution.py:324
  63.6 0.3 convert_element_type.8.x_ref
  63.9 0.6 copy-done
  64.5 4.8 %project.1 = (bf16[3,288,256]{2,1,0:T(8,128)(2,1)S(1)}, bf16[4,8,256]{2,1,0:T(8,128)(2,1)S(1)}, bf16[3,8,256]{2,1,0:T(8,128)(2,1)S(1)}) custom-call(s32[1]{0:T(128)} %bitcast.upper_ref, bf16[288,4224]{1,0:T(8,128)(2,1)S(1)} %convert_element_type.8.x_ref, bf16[576,128]{1,0:T(8,128)(2,1)S(1)} %copy-done, f32[304,128]{1,0:T(8,128)S(1)} %collective-permute-done.came_ref, ...), custom_call_target="tpu_custom_call" | custom-call | tf_op jit(solution)/shard_map/project/pallas_call | solution.py:140
  69.3 1.9 %collective-permute-start.3 = (bf16[4,8,256]{2,1,0:T(8,128)(2,1)S(1)}, bf16[4,8,256]{2,1,0:T(8,128)(2,1)S(1)}, u32[]{:S(2)}, u32[]{:S(2)}) collective-permute-start(bf16[4,8,256]{2,1,0:T(8,128)(2,1)S(1)} %get-tuple-element.20), channel_id=1, source_target_pairs={{12,0},{24,12},{36,24},{48,36},{60,48},{72,60},{84,72},{96,84},{10... | collective-permute-start | bytes 49160 | tf_op jit(solution)/shard_map/ppermute | solution.py:34
  71.2 3.9 %collective-permute-start.2 = (bf16[3,8,256]{2,1,0:T(8,128)(2,1)S(1)}, bf16[3,8,256]{2,1,0:T(8,128)(2,1)S(1)}, u32[]{:S(2)}, u32[]{:S(2)}) collective-permute-start(bf16[3,8,256]{2,1,0:T(8,128)(2,1)S(1)} %get-tuple-element.19), channel_id=1, source_target_pairs={{0,12},{12,24},{24,36},{36,48},{48,60},{60,72},{72,84},{84,96},{96... | collective-permute-start | bytes 36872 | tf_op jit(solution)/shard_map/ppermute | solution.py:34
  75.1 3.2 %collective-permute-done.2.prev_ref = bf16[3,8,256]{2,1,0:T(8,128)(2,1)S(1)} collective-permute-done((bf16[3,8,256]{2,1,0:T(8,128)(2,1)S(1)}, bf16[3,8,256]{2,1,0:T(8,128)(2,1)S(1)}, u32[]{:S(2)}, u32[]{:S(2)}) %collective-permute-start.2) | collective-permute-done | bytes 12320 | tf_op jit(solution)/shard_map/ppermute | solution.py:34
  78.4 4.8 %mix.1 = (bf16[288,128]{1,0:T(8,128)(2,1)S(1)}, bf16[288,128]{1,0:T(8,128)(2,1)S(1)}, bf16[276,4352]{1,0:T(8,128)(2,1)}) custom-call(s32[1]{0:T(128)} %bitcast.upper_ref, bf16[3,288,256]{2,1,0:T(8,128)(2,1)S(1)} %get-tuple-element.18.proj_ref, bf16[3,8,256]{2,1,0:T(8,128)(2,1)S(1)} %collective-permute-done.2.prev_ref, ...), custom_call_target="tpu_custom_call" | custom-call | tf_op jit(solution)/shard_map/mix/pallas_call | solution.py:247
  83.2 33.3 %fusion = bf16[24,4352]{1,0:T(8,128)(2,1)S(1)} fusion(bf16[276,4352]{1,0:T(8,128)(2,1)} %get-tuple-element.23), kind=kCustom, calls=%all-reduce-scatter | all-reduce-scatter fusion | flops 1253377 | bytes 2615296
  116.6 3.0 %collective-permute-start.5 = (bf16[11,4352]{1,0:T(8,128)(2,1)S(1)}, bf16[11,4352]{1,0:T(8,128)(2,1)S(1)}, u32[]{:S(2)}, u32[]{:S(2)}) collective-permute-start(bf16[11,4352]{1,0:T(8,128)(2,1)S(1)} %slice.10), channel_id=1, source_target_pairs={{0,1},{1,2},{2,3},{3,4},{4,5},{5,6},{6,7},{7,8},{8,9},{9,10},{10,1... | collective-permute-start | bytes 287240
  119.6 1.9 %collective-permute-start.4 = (bf16[288,128]{1,0:T(8,128)(2,1)S(1)}, bf16[288,128]{1,0:T(8,128)(2,1)S(1)}, u32[]{:S(2)}, u32[]{:S(2)}) collective-permute-start(bf16[288,128]{1,0:T(8,128)(2,1)S(1)} %get-tuple-element.22), channel_id=1, source_target_pairs={{0,12},{12,0},{1,13},{13,1},{2,14},{14,2},{3,15},{15,3},{4,16},{16... | collective-permute-start | bytes 221192 | tf_op jit(solution)/shard_map/ppermute | solution.py:309
  121.5 1.3 dynamic-slice.4
  123.5 2.4 %collective-permute-done.4.arrived_ref = bf16[288,128]{1,0:T(8,128)(2,1)S(1)} collective-permute-done((bf16[288,128]{1,0:T(8,128)(2,1)S(1)}, bf16[288,128]{1,0:T(8,128)(2,1)S(1)}, u32[]{:S(2)}, u32[]{:S(2)}) %collective-permute-start.4) | collective-permute-done | bytes 73760 | tf_op jit(solution)/shard_map/ppermute | solution.py:309
  125.9 0.7 halves.1
  126.5 0.5 concatenate.9
  127.1 0.1 constant_dynamic-slice_fusion
  127.2 0.7 pad_maximum_fusion.1
  (14 shorter events, 0.2 us)
Async XLA Ops:
  1.6 7.7 %collective-permute-start = (f32[304,128]{1,0:T(8,128)S(1)}, f32[304,128]{1,0:T(8,128)S(1)}, u32[]{:S(2)}, u32[]{:S(2)}) collective-permute-start(f32[304,128]{1,0:T(8,128)S(1)} %message.1), channel_id=1, source_target_pairs={{0,12},{12,0},{1,13},{13,1},{2,14},{14,2},{3,15},{15,3},{4,16},{16... | collective-permute-start | bytes 466952 | tf_op jit(solution)/shard_map/ppermute | solution.py:309
  9.2 54.6 %collective-permute-start.1 = (bf16[3,4096,128]{2,1,0:T(8,128)(2,1)}, bf16[3,4096,128]{2,1,0:T(8,128)(2,1)S(1)}, u32[]{:S(2)}, u32[]{:S(2)}) collective-permute-start(bf16[3,4096,128]{2,1,0:T(8,128)(2,1)} %bitcast.9), channel_id=1, source_target_pairs={{0,588},{12,0},{24,36},{36,216},{192,12},{204,192},{216,228},{228,... | collective-permute-start | bytes 9437192 | tf_op jit(solution)/shard_map/ppermute | solution.py:34
  63.6 0.9 copy-start
  63.8 14.5 %copy-start.1 = (f32[3,3,128]{2,1,0:T(4,128)S(1)}, f32[3,3,128]{2,1,0:T(4,128)}, u32[]{:S(2)}) copy-start(f32[3,3,128]{2,1,0:T(4,128)} %feat_ref.3) | copy-start | bytes 13828
  63.8 14.5 %copy-start.2 = (f32[7,128]{1,0:T(8,128)S(1)}, f32[7,128]{1,0:T(8,128)}, u32[]{:S(2)}) copy-start(f32[7,128]{1,0:T(8,128)} %inner_ref.3) | copy-start | bytes 10756
  69.3 9.1 %collective-permute-start.3 = (bf16[4,8,256]{2,1,0:T(8,128)(2,1)S(1)}, bf16[4,8,256]{2,1,0:T(8,128)(2,1)S(1)}, u32[]{:S(2)}, u32[]{:S(2)}) collective-permute-start(bf16[4,8,256]{2,1,0:T(8,128)(2,1)S(1)} %get-tuple-element.20), channel_id=1, source_target_pairs={{12,0},{24,12},{36,24},{48,36},{60,48},{72,60},{84,72},{96,84},{10... | collective-permute-start | bytes 49160 | tf_op jit(solution)/shard_map/ppermute | solution.py:34
  71.2 7.1 %collective-permute-start.2 = (bf16[3,8,256]{2,1,0:T(8,128)(2,1)S(1)}, bf16[3,8,256]{2,1,0:T(8,128)(2,1)S(1)}, u32[]{:S(2)}, u32[]{:S(2)}) collective-permute-start(bf16[3,8,256]{2,1,0:T(8,128)(2,1)S(1)} %get-tuple-element.19), channel_id=1, source_target_pairs={{0,12},{12,24},{24,36},{36,48},{48,60},{60,72},{72,84},{84,96},{96... | collective-permute-start | bytes 36872 | tf_op jit(solution)/shard_map/ppermute | solution.py:34
  116.6 10.0 %collective-permute-start.5 = (bf16[11,4352]{1,0:T(8,128)(2,1)S(1)}, bf16[11,4352]{1,0:T(8,128)(2,1)S(1)}, u32[]{:S(2)}, u32[]{:S(2)}) collective-permute-start(bf16[11,4352]{1,0:T(8,128)(2,1)S(1)} %slice.10), channel_id=1, source_target_pairs={{0,1},{1,2},{2,3},{3,4},{4,5},{5,6},{6,7},{7,8},{8,9},{9,10},{10,1... | collective-permute-start | bytes 287240
  119.6 6.2 %collective-permute-start.4 = (bf16[288,128]{1,0:T(8,128)(2,1)S(1)}, bf16[288,128]{1,0:T(8,128)(2,1)S(1)}, u32[]{:S(2)}, u32[]{:S(2)}) collective-permute-start(bf16[288,128]{1,0:T(8,128)(2,1)S(1)} %get-tuple-element.22), channel_id=1, source_target_pairs={{0,12},{12,0},{1,13},{13,1},{2,14},{14,2},{3,15},{15,3},{4,16},{16... | collective-permute-start | bytes 221192 | tf_op jit(solution)/shard_map/ppermute | solution.py:309

commit v12 on v11

--- a/solution.py
+++ b/solution.py
@@ -54,13 +54,6 @@
     return pl.multiple_of(upper * lanes, lanes), pl.multiple_of((1 - upper) * lanes, lanes)
 
 
-def bring(source, target, sems):
-    copies = [pltpu.make_async_copy(source.at[j], target.at[j], sems.at[j]) for j in range(source.shape[0])]
-    for copy in copies:
-        copy.start()
-    return copies
-
-
 def side_by_side(mine_ref, theirs_ref, part, cut):
     return jnp.concatenate([mine_ref[part, cut], theirs_ref[part, cut]], axis=1)
 
@@ -105,16 +98,14 @@
     return pltpu.with_memory_space_constraint(value, pltpu.MemorySpace.HBM)
 
 
-def project_kernel(upper_ref, x_ref, grad_ref, came_ref, mine_hbm, theirs_ref, o_ref, head_ref, tail_ref, mine_ref, sems):
+def project_kernel(upper_ref, x_ref, grad_ref, came_ref, mine_ref, theirs_ref, o_ref, head_ref, tail_ref):
     parts, depth, lanes = mine_ref.shape
     count = x_ref.shape[0]
     own, other = slots(upper_ref, lanes)
-    copies = bring(mine_hbm, mine_ref, sems)
     scale = jnp.exp2(x_ref[:, depth : depth + 1].astype(jnp.float32) - TOP)
     block = min(depth, 1024)
     for j in range(parts):
         total = None
-        copies[j].wait()
         for begin in range(0, depth, block):
             cut = slice(begin, begin + block)
             piece = jnp.dot(
@@ -139,17 +130,16 @@
     count = rows.shape[0]
     return pl.pallas_call(
         project_kernel,
-        in_specs=[smem()] + [vmem()] * 3 + [hbm(), vmem()],
+        in_specs=[smem()] + [vmem()] * 5,
         out_specs=[vmem()] * 3,
         out_shape=[
             jax.ShapeDtypeStruct((parts, count, 2 * lanes), jnp.bfloat16),
             jax.ShapeDtypeStruct((parts + 1, HALO, 2 * lanes), jnp.bfloat16),
             jax.ShapeDtypeStruct((parts, HALO, 2 * lanes), jnp.bfloat16),
         ],
-        scratch_shapes=[pltpu.VMEM(mine.shape, mine.dtype), pltpu.SemaphoreType.DMA((parts,))],
         compiler_params=PARAMS,
         name="project",
-    )(upper, rows, grad, came, in_hbm(mine), theirs)
+    )(upper, rows, grad, came, mine, theirs)
 
 
 def causal(series, taps):
@@ -167,14 +157,13 @@
 
 
 def mix_kernel(
-    upper_ref, proj_ref, prev_ref, next_ref, grad_ref, feat_ref, inner_ref, came_ref, mine_hbm, theirs_ref,
-    kept_ref, sent_ref, o_ref, back, extra, o_buf, sems, mine_ref, mine_sems,
+    upper_ref, proj_ref, prev_ref, next_ref, grad_ref, feat_ref, inner_ref, came_ref, mine_ref, theirs_ref,
+    kept_ref, sent_ref, o_ref, back, extra, o_buf, sems,
 ):
     parts, depth, lanes = mine_ref.shape
     count = proj_ref.shape[1]
     last = HALO + count
     block = depth // 8
-    copies = bring(mine_hbm, mine_ref, mine_sems)
     own, other = slots(upper_ref, lanes)
     begin = pl.multiple_of(upper_ref[0] * count, 16)
     shards = count // SHARD
@@ -207,8 +196,6 @@
                 first = k * SHARD
                 back[part, k * body : (k + 1) * body, cut] = rows[first : first + body]
                 back[part, main + k : main + k + 1, cut] = rows[first + body : first + SHARD]
-    for copy in copies:
-        copy.wait()
     left = [back[part].astype(jnp.bfloat16) for part in range(parts)]
     contract = (((1,), (1,)), ((), ()))
     extra[...] = jnp.zeros_like(extra)
@@ -246,7 +233,7 @@
     main = count // SHARD * (SHARD - 1)
     return pl.pallas_call(
         mix_kernel,
-        in_specs=[smem()] + [vmem()] * 7 + [hbm(), vmem()],
+        in_specs=[smem()] + [vmem()] * 9,
         out_specs=[vmem(), vmem(), hbm()],
         out_shape=[half, half, pltpu.HBM((main, depth + depth // FOLD), jnp.bfloat16)],
         scratch_shapes=[
@@ -254,12 +241,10 @@
             pltpu.VMEM((main, depth // FOLD), jnp.float32),
             pltpu.VMEM((main, depth + depth // FOLD), jnp.bfloat16),
             pltpu.SemaphoreType.DMA((9,)),
-            pltpu.VMEM(mine.shape, mine.dtype),
-            pltpu.SemaphoreType.DMA((parts,)),
         ],
         compiler_params=PARAMS,
         name="mix",
-    )(upper, proj, prev, following, grad, feat, inner, came, in_hbm(mine), theirs)
+    )(upper, proj, prev, following, grad, feat, inner, came, mine, theirs)
 
 
 def halves_kernel(upper_ref, kept_ref, arrived_ref, o_ref):

time: 128 us -> 126 us (0.984)
  Pallas kernels: 11.2 us -> 7.79 us
    pallas_call x2, Pallas kernels: 9.62 us -> 6.19 us  [the longest x1 4.13 us: mix(): pl.pallas_call(mix_kernel, in_specs=[smem()] + [vmem()] * 9, out_specs=[v...]
    unnamed x12 -> x14, local copies, waits for them, and re-layouts: 2.55 us -> 3.53 us
where the time goes in v12:
time: 126 us; the launch traced here: 125 us
  blocking collectives  84.4 us (67%)
  starting transfers between devices  16.6 us (13%)
  waiting for transfers between devices  8.39 us (7%)
  Pallas kernels  7.79 us (6%)
  local copies, waits for them, and re-layouts  3.62 us (3%)
  other arithmetic  3.16 us (3%)
  between operations  1.46 us (1%)
    all_gather x1, blocking collectives, local(): gathered = lax.all_gather(rows, 'z', axis=0, tiled=True)  51.1 us
    unnamed x1, blocking collectives  33.4 us
    ppermute x3, starting transfers between devices, exchange(): return lax.ppermute(value, axes, pairs)  9.09 us
    ppermute x2, waiting for transfers between devices, across(): return lax.ppermute(value, 'yl', [(0, 1), (1, 0)])  5.19 us
    ppermute x2, starting transfers between devices, across(): return lax.ppermute(value, 'yl', [(0, 1), (1, 0)])  4.51 us
    pallas_call x1, Pallas kernels, mix(): pl.pallas_call(mix_kernel, in_specs=[smem()] + [vmem()] * 9, out_specs=[v...  4.13 us
    unnamed x14, local copies, waits for them, and re-layouts  3.53 us
    ppermute x3, waiting for transfers between devices, exchange(): return lax.ppermute(value, axes, pairs)  3.2 us
  transfers between devices with their start and end apart: 6, of which 3 were waited for; matrix products, arithmetic and copies ran while one was open for 3% of the time, Pallas kernels for 1%

profile of v12, /device:TPU:48, one launch (start us, length us, event | category | flops | bytes accessed | tf_op | source)
XLA Modules:
  0.0 125.5 jit_solution(11283887704842551238)
XLA Ops:
  0.6 0.9 message.1
  1.6 2.6 %collective-permute-start = (f32[304,128]{1,0:T(8,128)S(1)}, f32[304,128]{1,0:T(8,128)S(1)}, u32[]{:S(2)}, u32[]{:S(2)}) collective-permute-start(f32[304,128]{1,0:T(8,128)S(1)} %message.1), channel_id=1, source_target_pairs={{0,12},{12,0},{1,13},{13,1},{2,14},{14,2},{3,15},{15,3},{4,16},{16... | collective-permute-start | bytes 466952 | tf_op jit(solution)/shard_map/ppermute | solution.py:294
  4.2 1.1 fusion.1
  5.2 1.1 fusion.2
  6.3 0.1 broadcast_in_dim.2
  6.4 2.8 %collective-permute-done.came_ref = f32[304,128]{1,0:T(8,128)S(1)} collective-permute-done((f32[304,128]{1,0:T(8,128)S(1)}, f32[304,128]{1,0:T(8,128)S(1)}, u32[]{:S(2)}, u32[]{:S(2)}) %collective-permute-start) | collective-permute-done | bytes 155680 | tf_op jit(solution)/shard_map/ppermute | solution.py:294
  9.2 3.2 %collective-permute-start.1 = (bf16[3,4096,128]{2,1,0:T(8,128)(2,1)}, bf16[3,4096,128]{2,1,0:T(8,128)(2,1)S(1)}, u32[]{:S(2)}, u32[]{:S(2)}) collective-permute-start(bf16[3,4096,128]{2,1,0:T(8,128)(2,1)} %bitcast.9), channel_id=1, source_target_pairs={{0,588},{12,0},{24,36},{36,216},{192,12},{204,192},{216,228},{228,... | collective-permute-start | bytes 9437192 | tf_op jit(solution)/shard_map/ppermute | solution.py:34
  12.5 51.1 %all-gather.1 = f16[288,4224]{1,0:T(8,128)(2,1)S(1)} all-gather(f16[24,4224]{1,0:T(8,128)(2,1)S(1)} %pad_maximum_fusion), channel_id=1, replica_groups=mesh['yh'=4,'x'=4,'c'=2,'yl'=2,'z'=12] {'z'}, dimensions={0}, use_global_device_ids=true | all-gather | bytes 2635776 | tf_op jit(solution)/shard_map/all_gather | solution.py:309
  63.6 0.3 convert_element_type.8.x_ref
  63.9 1.6 %copy-done = bf16[4096,3,128]{2,0,1:T(8,128)(2,1)S(1)} copy-done((bf16[4096,3,128]{2,0,1:T(8,128)(2,1)S(1)}, bf16[4096,3,128]{2,0,1:T(8,128)(2,1)}, u32[]{:S(2)}) %copy-start) | copy-done | bytes 3145752
  65.5 2.1 %project.1 = (bf16[3,288,256]{2,1,0:T(8,128)(2,1)S(1)}, bf16[4,8,256]{2,1,0:T(8,128)(2,1)S(1)}, bf16[3,8,256]{2,1,0:T(8,128)(2,1)S(1)}) custom-call(s32[1]{0:T(128)} %bitcast.upper_ref, bf16[288,4224]{1,0:T(8,128)(2,1)S(1)} %convert_element_type.8.x_ref, bf16[576,128]{1,0:T(8,128)(2,1)S(1)} %copy-done.1, f32[304,128]{1,0:T(8,128)S(1)} %collective-permute-done.came_ref, ...), custom_call_target="tpu_custom_call" | custom-call | tf_op jit(solution)/shard_map/project/pallas_call | solution.py:131
  67.5 1.9 %collective-permute-start.3 = (bf16[4,8,256]{2,1,0:T(8,128)(2,1)S(1)}, bf16[4,8,256]{2,1,0:T(8,128)(2,1)S(1)}, u32[]{:S(2)}, u32[]{:S(2)}) collective-permute-start(bf16[4,8,256]{2,1,0:T(8,128)(2,1)S(1)} %get-tuple-element.20), channel_id=1, source_target_pairs={{12,0},{24,12},{36,24},{48,36},{60,48},{72,60},{84,72},{96,84},{10... | collective-permute-start | bytes 49160 | tf_op jit(solution)/shard_map/ppermute | solution.py:34
  69.5 3.9 %collective-permute-start.2 = (bf16[3,8,256]{2,1,0:T(8,128)(2,1)S(1)}, bf16[3,8,256]{2,1,0:T(8,128)(2,1)S(1)}, u32[]{:S(2)}, u32[]{:S(2)}) collective-permute-start(bf16[3,8,256]{2,1,0:T(8,128)(2,1)S(1)} %get-tuple-element.19), channel_id=1, source_target_pairs={{0,12},{12,24},{24,36},{36,48},{48,60},{60,72},{72,84},{84,96},{96... | collective-permute-start | bytes 36872 | tf_op jit(solution)/shard_map/ppermute | solution.py:34
  73.4 3.2 %collective-permute-done.2.prev_ref = bf16[3,8,256]{2,1,0:T(8,128)(2,1)S(1)} collective-permute-done((bf16[3,8,256]{2,1,0:T(8,128)(2,1)S(1)}, bf16[3,8,256]{2,1,0:T(8,128)(2,1)S(1)}, u32[]{:S(2)}, u32[]{:S(2)}) %collective-permute-start.2) | collective-permute-done | bytes 12320 | tf_op jit(solution)/shard_map/ppermute | solution.py:34
  76.6 4.1 %mix.1 = (bf16[288,128]{1,0:T(8,128)(2,1)S(1)}, bf16[288,128]{1,0:T(8,128)(2,1)S(1)}, bf16[276,4352]{1,0:T(8,128)(2,1)}) custom-call(s32[1]{0:T(128)} %bitcast.upper_ref, bf16[3,288,256]{2,1,0:T(8,128)(2,1)S(1)} %get-tuple-element.18.proj_ref, bf16[3,8,256]{2,1,0:T(8,128)(2,1)S(1)} %collective-permute-done.2.prev_ref, ...), custom_call_target="tpu_custom_call" | custom-call | tf_op jit(solution)/shard_map/mix/pallas_call | solution.py:234
  80.7 33.4 %fusion = bf16[24,4352]{1,0:T(8,128)(2,1)S(1)} fusion(bf16[276,4352]{1,0:T(8,128)(2,1)} %get-tuple-element.23), kind=kCustom, calls=%all-reduce-scatter | all-reduce-scatter fusion | flops 1253377 | bytes 2615296
  114.1 3.0 %collective-permute-start.5 = (bf16[11,4352]{1,0:T(8,128)(2,1)S(1)}, bf16[11,4352]{1,0:T(8,128)(2,1)S(1)}, u32[]{:S(2)}, u32[]{:S(2)}) collective-permute-start(bf16[11,4352]{1,0:T(8,128)(2,1)S(1)} %slice.10), channel_id=1, source_target_pairs={{0,1},{1,2},{2,3},{3,4},{4,5},{5,6},{6,7},{7,8},{8,9},{9,10},{10,1... | collective-permute-start | bytes 287240
  117.2 1.9 %collective-permute-start.4 = (bf16[288,128]{1,0:T(8,128)(2,1)S(1)}, bf16[288,128]{1,0:T(8,128)(2,1)S(1)}, u32[]{:S(2)}, u32[]{:S(2)}) collective-permute-start(bf16[288,128]{1,0:T(8,128)(2,1)S(1)} %get-tuple-element.22), channel_id=1, source_target_pairs={{0,12},{12,0},{1,13},{13,1},{2,14},{14,2},{3,15},{15,3},{4,16},{16... | collective-permute-start | bytes 221192 | tf_op jit(solution)/shard_map/ppermute | solution.py:294
  119.1 1.3 %dynamic-slice.4 = u32[1]{0:T(128)} dynamic-slice(u32[768]{0:T(1024)} %constant.26, u32[]{:S(6)} %partition-id.4), dynamic_slice_sizes={1} | dynamic-slice | bytes 12
  121.0 2.4 %collective-permute-done.4.arrived_ref = bf16[288,128]{1,0:T(8,128)(2,1)S(1)} collective-permute-done((bf16[288,128]{1,0:T(8,128)(2,1)S(1)}, bf16[288,128]{1,0:T(8,128)(2,1)S(1)}, u32[]{:S(2)}, u32[]{:S(2)}) %collective-permute-start.4) | collective-permute-done | bytes 73760 | tf_op jit(solution)/shard_map/ppermute | solution.py:294
  123.4 0.7 halves.1
  124.1 0.5 concatenate.9
  124.6 0.1 constant_dynamic-slice_fusion
  124.8 0.7 pad_maximum_fusion.1
  (16 shorter events, 0.2 us)
Async XLA Ops:
  1.6 7.7 %collective-permute-start = (f32[304,128]{1,0:T(8,128)S(1)}, f32[304,128]{1,0:T(8,128)S(1)}, u32[]{:S(2)}, u32[]{:S(2)}) collective-permute-start(f32[304,128]{1,0:T(8,128)S(1)} %message.1), channel_id=1, source_target_pairs={{0,12},{12,0},{1,13},{13,1},{2,14},{14,2},{3,15},{15,3},{4,16},{16... | collective-permute-start | bytes 466952 | tf_op jit(solution)/shard_map/ppermute | solution.py:294
  9.2 54.6 %collective-permute-start.1 = (bf16[3,4096,128]{2,1,0:T(8,128)(2,1)}, bf16[3,4096,128]{2,1,0:T(8,128)(2,1)S(1)}, u32[]{:S(2)}, u32[]{:S(2)}) collective-permute-start(bf16[3,4096,128]{2,1,0:T(8,128)(2,1)} %bitcast.9), channel_id=1, source_target_pairs={{0,588},{12,0},{24,36},{36,216},{192,12},{204,192},{216,228},{228,... | collective-permute-start | bytes 9437192 | tf_op jit(solution)/shard_map/ppermute | solution.py:34
  63.6 1.9 %copy-start = (bf16[4096,3,128]{2,0,1:T(8,128)(2,1)S(1)}, bf16[4096,3,128]{2,0,1:T(8,128)(2,1)}, u32[]{:S(2)}) copy-start(bf16[4096,3,128]{2,0,1:T(8,128)(2,1)} %param.6) | copy-start | bytes 9437188
  63.6 1.9 %copy-start.1 = (bf16[576,128]{1,0:T(8,128)(2,1)S(1)}, bf16[576,128]{1,0:T(8,128)(2,1)}, u32[]{:S(2)}) copy-start(bf16[576,128]{1,0:T(8,128)(2,1)} %grad_ref.5) | copy-start | bytes 442372
  63.8 12.7 %copy-start.2 = (f32[3,3,128]{2,1,0:T(4,128)S(1)}, f32[3,3,128]{2,1,0:T(4,128)}, u32[]{:S(2)}) copy-start(f32[3,3,128]{2,1,0:T(4,128)} %feat_ref.3) | copy-start | bytes 13828
  63.9 12.7 %copy-start.3 = (f32[7,128]{1,0:T(8,128)S(1)}, f32[7,128]{1,0:T(8,128)}, u32[]{:S(2)}) copy-start(f32[7,128]{1,0:T(8,128)} %inner_ref.3) | copy-start | bytes 10756
  67.5 9.1 %collective-permute-start.3 = (bf16[4,8,256]{2,1,0:T(8,128)(2,1)S(1)}, bf16[4,8,256]{2,1,0:T(8,128)(2,1)S(1)}, u32[]{:S(2)}, u32[]{:S(2)}) collective-permute-start(bf16[4,8,256]{2,1,0:T(8,128)(2,1)S(1)} %get-tuple-element.20), channel_id=1, source_target_pairs={{12,0},{24,12},{36,24},{48,36},{60,48},{72,60},{84,72},{96,84},{10... | collective-permute-start | bytes 49160 | tf_op jit(solution)/shard_map/ppermute | solution.py:34
  69.5 7.1 %collective-permute-start.2 = (bf16[3,8,256]{2,1,0:T(8,128)(2,1)S(1)}, bf16[3,8,256]{2,1,0:T(8,128)(2,1)S(1)}, u32[]{:S(2)}, u32[]{:S(2)}) collective-permute-start(bf16[3,8,256]{2,1,0:T(8,128)(2,1)S(1)} %get-tuple-element.19), channel_id=1, source_target_pairs={{0,12},{12,24},{24,36},{36,48},{48,60},{60,72},{72,84},{84,96},{96... | collective-permute-start | bytes 36872 | tf_op jit(solution)/shard_map/ppermute | solution.py:34
  114.1 9.9 %collective-permute-start.5 = (bf16[11,4352]{1,0:T(8,128)(2,1)S(1)}, bf16[11,4352]{1,0:T(8,128)(2,1)S(1)}, u32[]{:S(2)}, u32[]{:S(2)}) collective-permute-start(bf16[11,4352]{1,0:T(8,128)(2,1)S(1)} %slice.10), channel_id=1, source_target_pairs={{0,1},{1,2},{2,3},{3,4},{4,5},{5,6},{6,7},{7,8},{8,9},{9,10},{10,1... | collective-permute-start | bytes 287240
  117.2 6.2 %collective-permute-start.4 = (bf16[288,128]{1,0:T(8,128)(2,1)S(1)}, bf16[288,128]{1,0:T(8,128)(2,1)S(1)}, u32[]{:S(2)}, u32[]{:S(2)}) collective-permute-start(bf16[288,128]{1,0:T(8,128)(2,1)S(1)} %get-tuple-element.22), channel_id=1, source_target_pairs={{0,12},{12,0},{1,13},{13,1},{2,14},{14,2},{3,15},{15,3},{4,16},{16... | collective-permute-start | bytes 221192 | tf_op jit(solution)/shard_map/ppermute | solution.py:294
